TPU v7x, 32 devices: a whole 2x2x4 slice. The times are simulated.
32 devices in a mesh: rep: 8 (over y, x, core), seq: 4 (over z).
Axes of the slice: x: 2, y: 2, z: 4, core: 2. Of those that a mesh axis runs over, the one named last changes fastest.
Arguments:
- tokens: bfloat16 [16384, 896], P(('rep', 'seq')), may hold values from -6 to 6
- cotangent: bfloat16 [16384, 896], P(('rep', 'seq')), may hold values from -6 to 6
- seq_ids: int32 [16384], P(('rep', 'seq')), may hold values from 0 to 4, as said below
- block_ids: int32 [16384], P(('rep', 'seq')), may hold values from 0 to 3, as said below
- positions: int32 [16384], P(('rep', 'seq')), may hold values from 0 to 1023, as said below
- first_gain: bfloat16 [896], P('seq'), may hold values from 0.5 to 1.5
- query_weight: bfloat16 [896, 896], P('seq'), may hold values from -0.1875 to 0.1875
- query_bias: bfloat16 [896], P('seq'), may hold values from -1.796875 to 1.796875
- key_weight: bfloat16 [896, 128], P('seq'), may hold values from -0.1875 to 0.1875
- key_bias: bfloat16 [128], P('seq'), may hold values from -1.796875 to 1.796875
- value_weight: bfloat16 [896, 128], P('seq'), may hold values from -0.1875 to 0.1875
- value_bias: bfloat16 [128], P('seq'), may hold values from -0.119628906 to 0.119628906
- out_weight: bfloat16 [896, 896], P('seq'), may hold values from -2 to 2
- second_gain: bfloat16 [896], P('seq'), may hold values from 0.5 to 1.5
- gate_weight: bfloat16 [896, 4864], P('seq'), may hold values from -0.1875 to 0.1875
- up_weight: bfloat16 [896, 4864], P('seq'), may hold values from -0.1875 to 0.1875
- down_weight: bfloat16 [4864, 896], P('seq'), may hold values from -0.078125 to 0.078125
Outputs:
- output: bfloat16 [16384, 896], P(('rep', 'seq'))
- tokens_grad: bfloat16 [16384, 896], P(('rep', 'seq'))
- first_gain_grad: float32 [896], P('seq')
- query_weight_grad: float32 [896, 896], P('seq')
- query_bias_grad: float32 [896], P('seq')
- key_weight_grad: float32 [896, 128], P('seq')
- key_bias_grad: float32 [128], P('seq')
- value_weight_grad: float32 [896, 128], P('seq')
- value_bias_grad: float32 [128], P('seq')
- out_weight_grad: float32 [896, 896], P('seq')
- second_gain_grad: float32 [896], P('seq')
- gate_weight_grad: float32 [896, 4864], P('seq')
- up_weight_grad: float32 [896, 4864], P('seq')
- down_weight_grad: float32 [4864, 896], P('seq')
Inputs may be any that keep to these rules, and one draw needn't show every extreme that they name: `seq_ids`: each group of 2048 consecutive tokens holds whole sequences made of whole blocks of 256 tokens, numbered 0, 1, 2, ... in order within the group; a sequence has 1 to 4 blocks, and each group has one of exactly 4 blocks, which begins at the last block of some run of 2 blocks (block index k * 2 - 1 within the group); the largest number, 4, is reached in some group. `block_ids`: the index of the token's block of 256 tokens within its sequence. The token's index within its sequence, so that positions // 256 equals block_ids.
All inputs are finite; a program needn't handle non-finite values.
Results may differ from a plain program's by a relative error of at most 0.024.
Values may be sent and summed in bfloat16 or wider, within the bound.
No kernel may reach another device: no remote copies, remote signals or barrier semaphores. Data moves between devices by JAX's collectives and lax.ppermute only.
A program may use at most 256 MiB of HBM per device.

v0:
```python
from functools import partial

import jax
import jax.numpy as jnp
from jax import lax
from jax.sharding import PartitionSpec as P

H = 14
KVH = 2
HD = 64


EPS = 1e-06
ROPE_BASE = 1000000.0
NEG_FILL = -1e30


def rope_tables(positions, head_size):
    half_size = head_size // 2
    freqs = ROPE_BASE ** (-(jnp.arange(half_size, dtype=jnp.float32) * 2.0 / head_size))
    angles = positions.astype(jnp.float32)[:, None] * freqs[None, :]
    angles = jnp.concatenate([angles, angles], axis=-1)
    return (jnp.cos(angles), jnp.sin(angles))


def rotate(values, cosine, sine_table):
    half_size = values.shape[-1] // 2
    turned = jnp.concatenate([-values[..., half_size:], values[..., :half_size]], axis=-1)
    return values * cosine[:, None, :] + turned * sine_table[:, None, :]


def matmul(left, right):
    return jnp.dot(left, right, preferred_element_type=jnp.float32)


def times_trans(left, right):
    return lax.dot_general(
        left, right, (((1,), (1,)), ((), ())), preferred_element_type=jnp.float32
    )


def over_rows(left, right):
    return lax.dot_general(
        left, right, (((0,), (0,)), ((), ())), preferred_element_type=jnp.float32
    )


def rms_unit(values):
    factor_rows = lax.rsqrt(jnp.mean(values * values, axis=-1, keepdims=True) + EPS)
    return (values * factor_rows, factor_rows)


def norm_back(grad_unit, unit_rows, factor_rows):
    return factor_rows * (
        grad_unit - unit_rows * jnp.mean(grad_unit * unit_rows, axis=-1, keepdims=True)
    )


def attend_forward(query_head, key_head, value_head, allowed, factor):
    scores = times_trans(query_head, key_head) * factor
    masked = jnp.where(allowed, scores, NEG_FILL)
    top_score = jnp.max(masked, axis=-1, keepdims=True)
    expon = jnp.exp(masked - top_score)
    totals = jnp.sum(expon, axis=-1, keepdims=True)
    probs = expon / totals
    return (matmul(probs.astype(jnp.bfloat16), value_head), (top_score + jnp.log(totals))[:, 0])


def attend_backward(triple, key_head, value_head, allowed, factor):
    query_head, grad_head, log_total = triple
    scores = times_trans(query_head, key_head) * factor
    probs = jnp.where(allowed, jnp.exp(scores - log_total[:, None]), 0.0)
    d_probs = times_trans(grad_head, value_head)
    delta = jnp.sum(probs * d_probs, axis=-1, keepdims=True)
    d_scores = (probs * (d_probs - delta)).astype(jnp.bfloat16)
    d_query = matmul(d_scores, key_head) * factor
    d_key = over_rows(d_scores, query_head) * factor
    d_value = over_rows(probs.astype(jnp.bfloat16), grad_head)
    return (d_query, d_key, d_value)


def on_device(
    tokens,
    cotangent,
    seq_ids,
    block_ids,
    positions,
    first_gain,
    query_weight,
    query_bias,
    key_weight,
    key_bias,
    value_weight,
    value_bias,
    out_weight,
    second_gain,
    gate_weight,
    up_weight,
    down_weight,
):
    row_count = tokens.shape[0]
    group_heads = H // KVH
    factor = HD ** (-0.5)
    gathered_attn = (
        lax.all_gather(first_gain, "seq", axis=0, tiled=True),
        lax.all_gather(query_weight, "seq", axis=0, tiled=True),
        lax.all_gather(query_bias, "seq", axis=0, tiled=True),
        lax.all_gather(key_weight, "seq", axis=0, tiled=True),
        lax.all_gather(key_bias, "seq", axis=0, tiled=True),
        lax.all_gather(value_weight, "seq", axis=0, tiled=True),
        lax.all_gather(value_bias, "seq", axis=0, tiled=True),
        lax.all_gather(out_weight, "seq", axis=0, tiled=True),
    )
    (
        gain_one_full,
        query_full,
        query_bias_full,
        key_full,
        key_bias_full,
        value_full,
        value_bias_full,
        out_full,
    ) = gathered_attn
    tokens_wide = tokens.astype(jnp.float32)
    cosine, sine_table = rope_tables(positions, HD)
    unit_one, scale_one = rms_unit(tokens_wide)
    normed_one = (unit_one * gain_one_full.astype(jnp.float32)).astype(jnp.bfloat16)
    query_pre = matmul(normed_one, query_full) + query_bias_full.astype(jnp.float32)
    key_pre = matmul(normed_one, key_full) + key_bias_full.astype(jnp.float32)
    value_rows = (matmul(normed_one, value_full) + value_bias_full.astype(jnp.float32)).astype(
        jnp.bfloat16
    )
    queries = rotate(query_pre.reshape(row_count, H, HD), cosine, sine_table).astype(jnp.bfloat16)
    key_rows = rotate(key_pre.reshape(row_count, KVH, HD), cosine, sine_table).astype(jnp.bfloat16)
    key_rows = key_rows.reshape(row_count, KVH * HD)
    all_keys, all_values, key_seqs, key_blocks = (
        lax.all_gather(key_rows, "seq", axis=0, tiled=True),
        lax.all_gather(value_rows, "seq", axis=0, tiled=True),
        lax.all_gather(seq_ids.astype(jnp.bfloat16), "seq", axis=0, tiled=True),
        lax.all_gather(block_ids.astype(jnp.bfloat16), "seq", axis=0, tiled=True),
    )
    allowed = (seq_ids.astype(jnp.float32)[:, None] == key_seqs.astype(jnp.float32)[None, :]) & (
        key_blocks.astype(jnp.float32)[None, :] <= block_ids.astype(jnp.float32)[:, None]
    )
    total_keys = all_keys.shape[0]
    query_heads = jnp.transpose(queries, (1, 0, 2))
    key_heads = jnp.transpose(all_keys.reshape(total_keys, KVH, HD), (1, 0, 2))
    value_heads = jnp.transpose(all_values.reshape(total_keys, KVH, HD), (1, 0, 2))
    head_outs = []
    head_totals = []
    for kv_index in range(KVH):
        step_fn = partial(
            attend_forward,
            key_head=key_heads[kv_index],
            value_head=value_heads[kv_index],
            allowed=allowed,
            factor=factor,
        )
        outs_part, totals_part = lax.map(
            step_fn, query_heads[kv_index * group_heads : (kv_index + 1) * group_heads]
        )
        head_outs.append(outs_part)
        head_totals.append(totals_part)
    attended_heads = jnp.concatenate(head_outs, axis=0)
    log_totals = jnp.concatenate(head_totals, axis=0)
    attended = (
        jnp.transpose(attended_heads, (1, 0, 2)).reshape(row_count, H * HD).astype(jnp.bfloat16)
    )
    mixed = tokens_wide + matmul(attended, out_full)
    gain_two_full, gate_full, up_full, down_full = (
        lax.all_gather(second_gain, "seq", axis=0, tiled=True),
        lax.all_gather(gate_weight, "seq", axis=0, tiled=True),
        lax.all_gather(up_weight, "seq", axis=0, tiled=True),
        lax.all_gather(down_weight, "seq", axis=0, tiled=True),
    )
    unit_two, scale_two = rms_unit(mixed)
    normed_two = (unit_two * gain_two_full.astype(jnp.float32)).astype(jnp.bfloat16)
    gate_pre = matmul(normed_two, gate_full)
    up_pre = matmul(normed_two, up_full)
    sigmoid_gate = jax.nn.sigmoid(gate_pre)
    silu_gate = gate_pre * sigmoid_gate
    hidden = (silu_gate * up_pre).astype(jnp.bfloat16)
    output = (mixed + matmul(hidden, down_full)).astype(jnp.bfloat16)
    gain_two_back, gate_back, up_back, down_back = (
        lax.all_gather(second_gain, "seq", axis=0, tiled=True),
        lax.all_gather(gate_weight, "seq", axis=0, tiled=True),
        lax.all_gather(up_weight, "seq", axis=0, tiled=True),
        lax.all_gather(down_weight, "seq", axis=0, tiled=True),
    )
    grad_down = over_rows(hidden, cotangent)
    d_hidden = times_trans(cotangent, down_back)
    d_gate = (d_hidden * up_pre * sigmoid_gate * (1.0 + gate_pre * (1.0 - sigmoid_gate))).astype(
        jnp.bfloat16
    )
    d_up = (d_hidden * silu_gate).astype(jnp.bfloat16)
    grad_gate = over_rows(normed_two, d_gate)
    grad_up = over_rows(normed_two, d_up)
    d_normed_two = times_trans(d_gate, gate_back) + times_trans(d_up, up_back)
    grad_gain_two = jnp.sum(d_normed_two * unit_two, axis=0)
    d_mixed = cotangent.astype(jnp.float32) + norm_back(
        d_normed_two * gain_two_back.astype(jnp.float32), unit_two, scale_two
    )
    own_gain_two, own_gate, own_up, own_down = (
        lax.psum_scatter(
            grad_gain_two.astype(jnp.bfloat16), "seq", scatter_dimension=0, tiled=True
        ).astype(jnp.float32),
        lax.psum_scatter(
            grad_gate.astype(jnp.bfloat16), "seq", scatter_dimension=0, tiled=True
        ).astype(jnp.float32),
        lax.psum_scatter(
            grad_up.astype(jnp.bfloat16), "seq", scatter_dimension=0, tiled=True
        ).astype(jnp.float32),
        lax.psum_scatter(
            grad_down.astype(jnp.bfloat16), "seq", scatter_dimension=0, tiled=True
        ).astype(jnp.float32),
    )
    sum_gain_two, sum_gate, sum_up, sum_down = (
        lax.psum(own_gain_two.astype(jnp.bfloat16), "rep").astype(jnp.float32),
        lax.psum(own_gate.astype(jnp.bfloat16), "rep").astype(jnp.float32),
        lax.psum(own_up.astype(jnp.bfloat16), "rep").astype(jnp.float32),
        lax.psum(own_down.astype(jnp.bfloat16), "rep").astype(jnp.float32),
    )
    (
        gain_one_back,
        query_back,
        query_bias_back,
        key_back,
        key_bias_back,
        value_back,
        value_bias_back,
        out_back,
    ) = (
        lax.all_gather(first_gain, "seq", axis=0, tiled=True),
        lax.all_gather(query_weight, "seq", axis=0, tiled=True),
        lax.all_gather(query_bias, "seq", axis=0, tiled=True),
        lax.all_gather(key_weight, "seq", axis=0, tiled=True),
        lax.all_gather(key_bias, "seq", axis=0, tiled=True),
        lax.all_gather(value_weight, "seq", axis=0, tiled=True),
        lax.all_gather(value_bias, "seq", axis=0, tiled=True),
        lax.all_gather(out_weight, "seq", axis=0, tiled=True),
    )
    d_branch = d_mixed.astype(jnp.bfloat16)
    grad_out = over_rows(attended, d_branch)
    d_attended = times_trans(d_branch, out_back).astype(jnp.bfloat16)
    d_att_heads = jnp.transpose(d_attended.reshape(row_count, H, HD), (1, 0, 2))
    query_grads = []
    key_terms = []
    value_terms = []
    for kv_index in range(KVH):
        lower = kv_index * group_heads
        upper = lower + group_heads
        step_fn = partial(
            attend_backward,
            key_head=key_heads[kv_index],
            value_head=value_heads[kv_index],
            allowed=allowed,
            factor=factor,
        )
        d_query_part, d_key_part, d_value_part = lax.map(
            step_fn, (query_heads[lower:upper], d_att_heads[lower:upper], log_totals[lower:upper])
        )
        query_grads.append(d_query_part)
        key_terms.append(jnp.sum(d_key_part, axis=0))
        value_terms.append(jnp.sum(d_value_part, axis=0))
    d_key_term = jnp.stack(key_terms, axis=1).reshape(total_keys, KVH * HD)
    d_value_term = jnp.stack(value_terms, axis=1).reshape(total_keys, KVH * HD)
    d_key_own, d_value_own = (
        lax.psum_scatter(d_key_term, "seq", scatter_dimension=0, tiled=True),
        lax.psum_scatter(d_value_term, "seq", scatter_dimension=0, tiled=True),
    )
    d_key_pre = rotate(d_key_own.reshape(row_count, KVH, HD), cosine, -sine_table)
    d_key_pre = d_key_pre.reshape(row_count, KVH * HD).astype(jnp.bfloat16)
    d_value_pre = d_value_own.astype(jnp.bfloat16)
    d_query_rot = jnp.transpose(jnp.concatenate(query_grads, axis=0), (1, 0, 2))
    d_query_pre = (
        rotate(d_query_rot, cosine, -sine_table).reshape(row_count, H * HD).astype(jnp.bfloat16)
    )
    grad_query = over_rows(normed_one, d_query_pre)
    grad_key = over_rows(normed_one, d_key_pre)
    grad_value = over_rows(normed_one, d_value_pre)
    grad_query_bias = jnp.sum(d_query_pre.astype(jnp.float32), axis=0)
    grad_key_bias = jnp.sum(d_key_pre.astype(jnp.float32), axis=0)
    grad_value_bias = jnp.sum(d_value_pre.astype(jnp.float32), axis=0)
    d_normed_one = (
        times_trans(d_query_pre, query_back)
        + times_trans(d_key_pre, key_back)
        + times_trans(d_value_pre, value_back)
    )
    grad_gain_one = jnp.sum(d_normed_one * unit_one, axis=0)
    tokens_grad = (
        d_mixed + norm_back(d_normed_one * gain_one_back.astype(jnp.float32), unit_one, scale_one)
    ).astype(jnp.bfloat16)
    (
        own_gain_one,
        own_query,
        own_query_bias,
        own_key,
        own_key_bias,
        own_value,
        own_value_bias,
        own_out,
    ) = (
        lax.psum_scatter(
            grad_gain_one.astype(jnp.bfloat16), "seq", scatter_dimension=0, tiled=True
        ).astype(jnp.float32),
        lax.psum_scatter(
            grad_query.astype(jnp.bfloat16), "seq", scatter_dimension=0, tiled=True
        ).astype(jnp.float32),
        lax.psum_scatter(
            grad_query_bias.astype(jnp.bfloat16), "seq", scatter_dimension=0, tiled=True
        ).astype(jnp.float32),
        lax.psum_scatter(
            grad_key.astype(jnp.bfloat16), "seq", scatter_dimension=0, tiled=True
        ).astype(jnp.float32),
        lax.psum_scatter(
            grad_key_bias.astype(jnp.bfloat16), "seq", scatter_dimension=0, tiled=True
        ).astype(jnp.float32),
        lax.psum_scatter(
            grad_value.astype(jnp.bfloat16), "seq", scatter_dimension=0, tiled=True
        ).astype(jnp.float32),
        lax.psum_scatter(
            grad_value_bias.astype(jnp.bfloat16), "seq", scatter_dimension=0, tiled=True
        ).astype(jnp.float32),
        lax.psum_scatter(
            grad_out.astype(jnp.bfloat16), "seq", scatter_dimension=0, tiled=True
        ).astype(jnp.float32),
    )
    (
        sum_gain_one,
        sum_query,
        sum_query_bias,
        sum_key,
        sum_key_bias,
        sum_value,
        sum_value_bias,
        sum_out,
    ) = (
        lax.psum(own_gain_one.astype(jnp.bfloat16), "rep").astype(jnp.float32),
        lax.psum(own_query.astype(jnp.bfloat16), "rep").astype(jnp.float32),
        lax.psum(own_query_bias.astype(jnp.bfloat16), "rep").astype(jnp.float32),
        lax.psum(own_key.astype(jnp.bfloat16), "rep").astype(jnp.float32),
        lax.psum(own_key_bias.astype(jnp.bfloat16), "rep").astype(jnp.float32),
        lax.psum(own_value.astype(jnp.bfloat16), "rep").astype(jnp.float32),
        lax.psum(own_value_bias.astype(jnp.bfloat16), "rep").astype(jnp.float32),
        lax.psum(own_out.astype(jnp.bfloat16), "rep").astype(jnp.float32),
    )
    return (
        output,
        tokens_grad,
        sum_gain_one,
        sum_query,
        sum_query_bias,
        sum_key,
        sum_key_bias,
        sum_value,
        sum_value_bias,
        sum_out,
        sum_gain_two,
        sum_gate,
        sum_up,
        sum_down,
    )


def solution(mesh):
    return jax.shard_map(
        on_device,
        mesh=mesh,
        in_specs=(
            P(("rep", "seq"), None),
            P(("rep", "seq"), None),
            P(("rep", "seq")),
            P(("rep", "seq")),
            P(("rep", "seq")),
            P("seq"),
            P("seq", None),
            P("seq"),
            P("seq", None),
            P("seq"),
            P("seq", None),
            P("seq"),
            P("seq", None),
            P("seq"),
            P("seq", None),
            P("seq", None),
            P("seq", None),
        ),
        out_specs=(
            P(("rep", "seq"), None),
            P(("rep", "seq"), None),
            P("seq"),
            P("seq", None),
            P("seq"),
            P("seq", None),
            P("seq"),
            P("seq", None),
            P("seq"),
            P("seq", None),
            P("seq"),
            P("seq", None),
            P("seq", None),
            P("seq", None),
        ),
        check_vma=False,
    )
```

profile of v0, /device:TPU:0, one launch (start us, length us, event | category | flops | bytes accessed | tf_op | source)
XLA Modules:
  0.0 1590.1 jit_solution(1129512579268830386)
XLA Ops:
  14.0 14.2 all-reduce.13
  29.5 15.5 all_gather.60
  45.7 18.3 %all_gather.62 = bf16[2048,128]{0,1:T(8,128)(2,1)S(1)} all-gather(bf16[512,128]{0,1:T(8,128)(2,1)S(1)} %fusion.82), channel_id=1, replica_groups=mesh['rep'=8,'seq'=4] {'seq'}, dimensions={0}, use_global_device_ids=true | all-gather | bytes 655360 | tf_op jit(solution)/shard_map/all_gather | solution.py:137
  66.7 15.9 %all_gather.65 = bf16[896,128]{1,0:T(8,128)(2,1)S(1)} all-gather(bf16[224,128]{1,0:T(8,128)(2,1)S(1)} %copy-done.39), channel_id=1, replica_groups=mesh['rep'=8,'seq'=4] {'seq'}, dimensions={0}, use_global_device_ids=true | all-gather | bytes 286720 | tf_op jit(solution)/shard_map/all_gather | solution.py:110
  83.8 20.8 %all_gather.67 = bf16[2048,128]{1,0:T(8,128)(2,1)S(1)} all-gather(bf16[512,128]{1,0:T(8,128)(2,1)S(1)} %fusion.77), channel_id=1, replica_groups=mesh['rep'=8,'seq'=4] {'seq'}, dimensions={0}, use_global_device_ids=true | all-gather | bytes 655360 | tf_op jit(solution)/shard_map/all_gather | solution.py:138
  105.8 11.9 all-gather
  117.8 16.3 %all-gather.1 = bf16[4,1,512]{2,1,0:T(2,128)(2,1)S(1)} all-gather(bf16[1,1,512]{2,1,0:T(2,128)(2,1)S(1)} %reshape.243), channel_id=1, replica_groups=mesh['rep'=8,'seq'=4] {'seq'}, dimensions={0}, use_global_device_ids=true | all-gather | bytes 5120 | tf_op jit(solution)/shard_map/all_gather | solution.py:140
  148.0 56.6 %while.56 = (s32[]{:T(128)}, bf16[7,512,64]{1,2,0:T(8,128)(2,1)S(1)}, f32[7,512]{1,0:T(8,128)S(1)}, bf16[7,512,64]{2,1,0:T(8,128)(2,1)}, bf16[2048,64]{1,0:T(8,1...) while((s32[]{:T(128)}, ...), condition=%wide.region_4.5_spmd.clone, body=%wide.region_1.4_spmd.clone.sunk | while | flops 279969280 | bytes 30450328 | solution.py:159
  207.0 61.8 %while.57 = (s32[]{:T(128)}, bf16[7,512,64]{1,2,0:T(8,128)(2,1)}, f32[7,512]{1,0:T(8,128)S(1)}, bf16[7,512,64]{2,1,0:T(8,128)(2,1)}, bf16[2048,64]{1,0:T(8,128)(...) while((s32[]{:T(128)}, bf16[7,512,64]{1,2,0:T(8,128)(2,1)}, ...), condition=%wide.region_8.9_spmd.clone, body=%wide.region_5.8_spmd.clone.sunk | while | flops 279969280 | bytes 34120400 | solution.py:159
  288.3 130.9 %all-gather.14.cloned.1.call-done = bf16[896,4864]{1,0:T(8,128)(2,1)} async-done(((bf16[224,4864]{1,0:T(8,128)(2,1)}), bf16[896,4864]{1,0:T(8,128)(2,1)}) %all-gather.14.cloned.1.call-update) | async-done | bytes 8716304 | tf_op jit(solution)/shard_map/all_gather | solution.py:173
  430.9 142.9 %all-gather.16.cloned.1.call-done = bf16[4864,896]{1,0:T(8,128)(2,1)} async-done(((bf16[1216,896]{1,0:T(8,128)(2,1)}), bf16[4864,896]{1,0:T(8,128)(2,1)}) %all-gather.16.cloned.1.call-update) | async-done | bytes 8716304 | tf_op jit(solution)/shard_map/all_gather | solution.py:174
  573.8 18.9 %multiply_convert_fusion.2 = (bf16[512,4864]{1,0:T(8,128)(2,1)}, bf16[512,4864]{1,0:T(8,128)(2,1)}, bf16[512,4864]{1,0:T(8,128)(2,1)}) fusion(f32[512,4864]{1,0:T(8,128)} %fusion.108, f32[512,4864]{1,0:T(8,128)} %fusion.109, bf16[512,896]{1,0:T(8,128)(2,1)S(1)} %copy-done.28, bf16[4864,896]{1,0:T(8,128)(2,1)} %all-gather.16.cloned.1.call-done), kind=kOutput, calls=%fused_computation.78 | convolution fusion | flops 4500094976 | bytes 44498944 | tf_op jit(solution)/shard_map/dot_general | solution.py:37
  592.7 12.0 fusion.110
  624.1 71.0 %while.58 = (s32[]{:T(128)}, f32[7,512,64]{1,2,0:T(8,128)S(1)}, f32[7,2048,64]{1,2,0:T(8,128)}, f32[7,2048,64]{1,2,0:T(8,128)}, bf16[7,512,64]{2,1,0:T(8,128)(2,...) while((s32[]{:T(128)}, f32[7,512,64]{1,2,0:T(8,128)S(1)}, ...), condition=%wide.region_13.14_spmd.clone, body=%wide.region_11.13_spmd.clone.sunk | while | flops 683834880 | bytes 34112652 | solution.py:259
  699.8 59.1 %while.59 = (s32[]{:T(128)}, f32[7,512,64]{1,2,0:T(8,128)S(1)}, f32[7,2048,64]{1,2,0:T(8,128)}, f32[7,2048,64]{1,2,0:T(8,128)}, bf16[7,512,64]{2,1,0:T(8,128)(2,...) while((s32[]{:T(128)}, f32[7,512,64]{1,2,0:T(8,128)S(1)}, ...), condition=%wide.region_16.17_spmd.clone, body=%wide.region_14.16_spmd.clone.sunk | while | flops 683834880 | bytes 34374288 | solution.py:259
  771.9 18.3 %reduce-scatter.10.cloned.1.call-done = f32[512,128]{0,1:T(8,128)} async-done(((f32[2048,128]{0,1:T(8,128)}), f32[512,128]{0,1:T(8,128)}) %reduce-scatter.10.cloned.1.call-update) | async-done | bytes 262160 | tf_op jit(solution)/shard_map/reduce_scatter | solution.py:268
  796.9 22.0 %reduce-scatter.12.cloned.1.call-done = f32[512,128]{0,1:T(8,128)} async-done(((f32[2048,128]{0,1:T(8,128)}), f32[512,128]{0,1:T(8,128)}) %reduce-scatter.12.cloned.1.call-update) | async-done | bytes 262160 | tf_op jit(solution)/shard_map/reduce_scatter | solution.py:269
  884.1 14.3 reduce-scatter.14.cloned.1.call-done
  898.4 37.7 %reduce-scatter.20.cloned.1.call-done = bf16[224,896]{1,0:T(8,128)(2,1)} async-done(((bf16[896,896]{1,0:T(8,128)(2,1)}), bf16[224,896]{1,0:T(8,128)(2,1)}) %reduce-scatter.20.cloned.1.call-update) | async-done | bytes 401424 | tf_op jit(solution)/shard_map/reduce_scatter | solution.py:324
  936.1 150.9 %reduce-scatter.22.cloned.1.call-done = bf16[224,4864]{1,0:T(8,128)(2,1)} async-done(((bf16[896,4864]{1,0:T(8,128)(2,1)}), bf16[224,4864]{1,0:T(8,128)(2,1)}) %reduce-scatter.22.cloned.1.call-update) | async-done | bytes 2179088 | tf_op jit(solution)/shard_map/reduce_scatter | solution.py:207
  1087.0 152.9 %reduce-scatter.24.cloned.1.call-done = bf16[224,4864]{1,0:T(8,128)(2,1)} async-done(((bf16[896,4864]{1,0:T(8,128)(2,1)}), bf16[224,4864]{1,0:T(8,128)(2,1)}) %reduce-scatter.24.cloned.1.call-update) | async-done | bytes 2179088 | tf_op jit(solution)/shard_map/reduce_scatter | solution.py:210
  1240.0 152.8 %reduce-scatter.26.cloned.1.call-done = bf16[1216,896]{1,0:T(8,128)(2,1)} async-done(((bf16[4864,896]{1,0:T(8,128)(2,1)}), bf16[1216,896]{1,0:T(8,128)(2,1)}) %reduce-scatter.26.cloned.1.call-update) | async-done | bytes 2179088 | tf_op jit(solution)/shard_map/reduce_scatter | solution.py:213
  1406.4 46.2 %all-reduce.17.cloned.1.call-done = (bf16[224]{0:T(256)(128)(2,1)}, bf16[224]{0:T(256)(128)(2,1)}, bf16[224,128]{1,0:T(8,128)(2,1)}, bf16[32]{0:T(256)(128)(2,1)...) async-done(((bf16[224]{0:T(256)(128)(2,1)}, bf16[224]{0:T(256)(128)(2,1)}, bf16[224,128]{1,0:T(8,128)(2,1)}, bf16[32]{0:T(256)(128)(2,1)}, ...) | async-done | bytes 116176 | tf_op jit(solution)/shard_map/psum | solution.py:338
  1461.4 110.9 %all-reduce.19.cloned.1.call-done = (bf16[224,896]{1,0:T(8,128)(2,1)}, bf16[224,896]{1,0:T(8,128)(2,1)}, bf16[224,4864]{1,0:T(8,128)(2,1)}, bf16[224,4864]{1,0:T(8,128)(2,1)}, bf16[1216,896]{1,0:T(8,128)(2,1)}) async-done(((bf16[224,896]{1,0:T(8,128)(2,1)}, bf16[224,896]{1,0:T(8,128)(2,1)}, bf16[224,4864]{1,0:T(8,128)(2,1)}, bf16[224,4864]{1,0:T(8,128)(2,1)}, bf16[1216,896]{1,0:T(8,128)(2,1)}), ...) | async-done | bytes 7340048 | tf_op jit(solution)/shard_map/psum | solution.py:339
  (477 shorter events, 447.3 us)
Async XLA Ops:
  7.2 128.3 %all-gather.8.cloned.1.call-start = ((), (), s32[]{:S(2)}) async-start(), calls=%async_computation.9 | async-start | bytes 2007040 | tf_op jit(solution)/shard_map/all_gather | solution.py:106
  7.9 263.1 %all-gather.10.cloned.1.call-start = ((), (), s32[]{:S(2)}) async-start(), calls=%async_computation.10 | async-start | bytes 2007040 | tf_op jit(solution)/shard_map/all_gather | solution.py:112
  8.7 267.2 %all-gather.12.cloned.1.call-start = ((), (), s32[]{:S(2)}) async-start(), calls=%async_computation.11 | async-start | bytes 10895360 | tf_op jit(solution)/shard_map/all_gather | solution.py:172
  9.5 409.7 %all-gather.14.cloned.1.call-start = ((), (), s32[]{:S(2)}) async-start(), calls=%async_computation.12 | async-start | bytes 10895360 | tf_op jit(solution)/shard_map/all_gather | solution.py:173
  10.1 563.7 %all-gather.16.cloned.1.call-start = ((), (), s32[]{:S(2)}) async-start(), calls=%async_computation.13 | async-start | bytes 10895360 | tf_op jit(solution)/shard_map/all_gather | solution.py:174
  10.7 779.6 %reduce-scatter.10.cloned.1.call-start = ((), (), s32[]{:S(2)}) async-start(), calls=%async_computation.14 | async-start | bytes 1310720 | tf_op jit(solution)/shard_map/reduce_scatter | solution.py:268
  10.8 128.6 %copy-start.12 = (bf16[7,512,64]{1,2,0:T(8,128)(2,1)}, bf16[7,512,64]{1,2,0:T(8,128)(2,1)S(1)}, u32[]{:S(2)}) copy-start(bf16[7,512,64]{1,2,0:T(8,128)(2,1)S(1)} %fusion.104) | copy-start | bytes 1376260
  28.2 107.3 %copy-start.40 = (f32[896]{0:T(1024)}, f32[896]{0:T(1024)S(1)}, u32[]{:S(2)}) copy-start(f32[896]{0:T(1024)S(1)} %convert_element_type.213) | copy-start | bytes 10756
  28.5 107.0 %copy-start.42 = (f32[512]{0:T(512)}, f32[512]{0:T(512)S(1)}, u32[]{:S(2)}) copy-start(f32[512]{0:T(512)S(1)} %add_rsqrt_fusion.1) | copy-start | bytes 6148
  65.4 40.4 %copy-start.47 = (s32[512]{0:T(512)S(1)}, s32[512]{0:T(512)}, u32[]{:S(2)}) copy-start(s32[512]{0:T(512)} %param.27) | copy-start | bytes 6148
  65.4 52.4 %copy-start.48 = (s32[512]{0:T(512)S(1)}, s32[512]{0:T(512)}, u32[]{:S(2)}) copy-start(s32[512]{0:T(512)} %param.28) | copy-start | bytes 6148
  288.3 285.5 %copy-start.28 = (bf16[512,896]{1,0:T(8,128)(2,1)S(1)}, bf16[512,896]{1,0:T(8,128)(2,1)}, u32[]{:S(2)}) copy-start(bf16[512,896]{1,0:T(8,128)(2,1)} %param.26) | copy-start | bytes 2752516
  764.6 54.3 %reduce-scatter.12.cloned.1.call-start = ((), (), s32[]{:S(2)}) async-start(), calls=%async_computation.15 | async-start | bytes 1310720 | tf_op jit(solution)/shard_map/reduce_scatter | solution.py:269
  770.4 22.0 %copy-start.41 = (f32[896]{0:T(1024)S(1)}, f32[896]{0:T(1024)}, u32[]{:S(2)}) copy-start(f32[896]{0:T(1024)} %copy-done.40) | copy-start | bytes 10756
  770.4 22.0 %copy-start.43 = (f32[512]{0:T(512)S(1)}, f32[512]{0:T(512)}, u32[]{:S(2)}) copy-start(f32[512]{0:T(512)} %copy-done.42) | copy-start | bytes 6148
  770.4 113.3 %reduce-scatter.16.cloned.1.call-start = ((), (), s32[]{:S(2)}) async-start(), calls=%async_computation.17 | async-start | bytes 286720 | tf_op jit(solution)/shard_map/reduce_scatter | solution.py:312
  793.7 90.1 %reduce-scatter.18.cloned.1.call-start = ((), (), s32[]{:S(2)}) async-start(), calls=%async_computation.18 | async-start | bytes 286720 | tf_op jit(solution)/shard_map/reduce_scatter | solution.py:318
  821.1 77.3 %reduce-scatter.14.cloned.1.call-start = ((), (), s32[]{:S(2)}) async-start(), calls=%async_computation.16 | async-start | bytes 2007040 | tf_op jit(solution)/shard_map/reduce_scatter | solution.py:306
  826.4 109.7 %reduce-scatter.20.cloned.1.call-start = ((), (), s32[]{:S(2)}) async-start(), calls=%async_computation.19 | async-start | bytes 2007040 | tf_op jit(solution)/shard_map/reduce_scatter | solution.py:324
  830.0 257.1 %reduce-scatter.22.cloned.1.call-start = ((), (), s32[]{:S(2)}) async-start(), calls=%async_computation.20 | async-start | bytes 10895360 | tf_op jit(solution)/shard_map/reduce_scatter | solution.py:207
  840.9 399.1 %reduce-scatter.24.cloned.1.call-start = ((), (), s32[]{:S(2)}) async-start(), calls=%async_computation.21 | async-start | bytes 10895360 | tf_op jit(solution)/shard_map/reduce_scatter | solution.py:210
  852.6 540.1 %reduce-scatter.26.cloned.1.call-start = ((), (), s32[]{:S(2)}) async-start(), calls=%async_computation.22 | async-start | bytes 10895360 | tf_op jit(solution)/shard_map/reduce_scatter | solution.py:213
  863.7 588.9 %all-reduce.17.cloned.1.call-start = ((), (), s32[]{:S(2)}) async-start(), calls=%async_computation.23 | async-start | bytes 234496 | tf_op jit(solution)/shard_map/psum | solution.py:338
  883.8 688.5 %all-reduce.19.cloned.1.call-start = ((), (), s32[]{:S(2)}) async-start(), calls=%async_computation.24 | async-start | bytes 14680064 | tf_op jit(solution)/shard_map/psum | solution.py:339
  (72 other events, 372.5 us)
Sparse Core Ops, SparseCore 0:
  9.6 50.8 all-gather.7
  62.1 46.8 all-gather.9
  110.5 154.0 all-gather.11
  266.0 153.1 all-gather.13
  420.6 153.1 all-gather.15
  764.7 25.4 reduce-scatter.9
  793.1 25.7 reduce-scatter.11
  821.7 18.3 reduce-scatter.15
  842.9 17.9 reduce-scatter.17
  863.7 34.6 reduce-scatter.13
  901.3 34.7 reduce-scatter.19
  938.3 148.6 reduce-scatter.21
  1089.4 150.5 reduce-scatter.23
  1242.2 150.5 reduce-scatter.25
  1397.6 54.8 all-reduce.16
  1456.3 115.9 all-reduce.18
where the time goes:
time: 1600 us; the launch traced here: 1590 us
  waiting for transfers between devices  983 us (61%)
  matrix products  327 us (20%)
  blocking collectives  123 us (8%)
  local copies, waits for them, and re-layouts  73.3 us (5%)
  other arithmetic  63.4 us (4%)
  between operations  17.9 us (1%)
    reduce_scatter x1, waiting for transfers between devices, on_device(): lax.psum_scatter(grad_up.astype(jnp.bfloat16), 'seq', scatter_dimension=0...  153 us
    reduce_scatter x1, waiting for transfers between devices, on_device(): lax.psum_scatter(grad_down.astype(jnp.bfloat16), 'seq', scatter_dimension...  153 us
    reduce_scatter x1, waiting for transfers between devices, on_device(): lax.psum_scatter(grad_gate.astype(jnp.bfloat16), 'seq', scatter_dimension...  151 us
    all_gather x1, waiting for transfers between devices, on_device(): lax.all_gather(down_weight, 'seq', axis=0, tiled=True)  143 us
    dot_general x49, matrix products, times_trans(): lax.dot_general(left, right, (((1,), (1,)), ((), ())), preferred_element_...  133 us
    all_gather x1, waiting for transfers between devices, on_device(): lax.all_gather(up_weight, 'seq', axis=0, tiled=True)  131 us
    psum x1, waiting for transfers between devices, on_device(): lax.psum(own_query.astype(jnp.bfloat16), 'rep').astype(jnp.float32)  111 us
    dot_general x35, matrix products, matmul(): return jnp.dot(left, right, preferred_element_type=jnp.float32)  97.4 us
  transfers between devices with their start and end apart: 16, of which 11 were waited for; matrix products, arithmetic and copies ran while one was open for 14% of the time, Pallas kernels for 0%

commit v1 on v0

v1 whole, which is shorter than its diff:
```python
import jax
import jax.numpy as jnp
from jax import lax
from jax.experimental import pallas as pl
from jax.experimental.pallas import tpu as pltpu
from jax.sharding import PartitionSpec as P

H = 14
KVH = 2
HD = 64
BLK = 256
SEQ_BLOCKS = 4
LANES = 128

EPS = 1e-06
ROPE_BASE = 1000000.0

F32 = jnp.float32
BF16 = jnp.bfloat16


class Net:
    def __init__(self):
        self.reps = lax.axis_size("rep")
        self.seqs = lax.axis_size("seq")
        self.rep = lax.axis_index("rep").astype(jnp.int32)
        self.seq = lax.axis_index("seq").astype(jnp.int32)
        self.place = jnp.stack([self.rep, self.seq])
        self.pairs = self.reps // 2
        self.half = self.rep % 2
        self.pair = self.rep // 2
        bits = []
        bit = 1
        while bit < self.pairs:
            bits.append(bit)
            bit *= 2
        self.orders = (tuple(bits), tuple(bits[::-1]))
        self.same_half = [[2 * k + c for k in range(self.pairs)] for c in range(2)]

    def flip(self, value, bit):
        return lax.ppermute(value, "rep", [(i, i ^ bit) for i in range(self.reps)])

    def flip_seq(self, value, bit):
        return lax.ppermute(value, "seq", [(i, i ^ bit) for i in range(self.seqs)])

    def slide(self, value, step):
        pairs = [(i, i + step) for i in range(self.seqs) if 0 <= i + step < self.seqs]
        return lax.ppermute(value, "seq", pairs)

    def gather_seq(self, value):
        return lax.all_gather(value, "seq", axis=0, tiled=True)

    def spread(self, piece, order):
        held = {0: piece}
        for bit in order:
            held.update({m ^ bit: self.flip(v, 2 * bit) for m, v in list(held.items())})
        return [held[m] for m in range(self.pairs)]

    def grow(self, held, bit):
        held.update({m ^ bit: self.flip(v, 2 * bit) for m, v in list(held.items())})


class Fold:
    def __init__(self, net, parts, order):
        self.net = net
        self.keep, self.send = parts
        self.bits = list(order)

    def step(self):
        got = self.net.flip(self.send, 2 * self.bits.pop(0))
        half = self.keep.shape[0] // 2
        if half == 0:
            self.keep = (self.keep.astype(F32) + got.astype(F32)).astype(BF16)
            return
        self.send = (self.keep[half:].astype(F32) + got[half:].astype(F32)).astype(BF16)
        self.keep = (self.keep[:half].astype(F32) + got[:half].astype(F32)).astype(BF16)

    def state(self):
        return (self.keep, self.send) if self.bits else (self.keep,)

    def rest(self):
        while self.bits:
            self.step()
        return self.keep[0]


def after(value, *others):
    return lax.optimization_barrier((value, others))[0]


def cut_width(columns, parts):
    return pl.cdiv(columns // LANES, parts) * LANES


def cut_offset(index, columns, parts):
    width = cut_width(columns, parts)
    return jnp.minimum(index * width, columns - width)


def piece_of_rank(rank, order):
    count = len(order)
    piece = 0
    for at, bit in enumerate(order):
        piece = piece | (((rank >> (count - 1 - at)) & 1) * bit)
    return piece


def assemble(net, regions, columns, index, rows, steps, place_of, own=None):
    flat = [p for region in regions for p in region[3]]
    skip = 0 if own is None else 1

    def body(place, *refs):
        out = refs[-1]

        def fill():
            at = 0
            for start, span, parts, pieces in regions:
                for m, piece in enumerate(pieces):
                    offset = start + cut_offset(index(place) ^ m, span, parts)
                    col = pl.multiple_of(offset, LANES)
                    out[:, pl.ds(col, piece.shape[1])] = refs[at][...]
                    at += 1

        if own is None:
            fill()
        else:

            @pl.when(pl.program_id(0) == 0)
            def _():
                out[...] = refs[-2][...]

            @pl.when(pl.program_id(0) > 0)
            def _():
                fill()

    in_specs = [
        pl.BlockSpec((rows, p.shape[1]), lambda i, p: (jnp.maximum(i - skip, 0), 0)) for p in flat
    ]
    if own is not None:
        in_specs.append(pl.BlockSpec((rows, columns), lambda i, p: (0, 0)))
        flat = flat + [own]
    return pl.pallas_call(
        body,
        name="assemble",
        out_shape=jax.ShapeDtypeStruct((rows * steps, columns), flat[0].dtype),
        grid_spec=pltpu.PrefetchScalarGridSpec(
            num_scalar_prefetch=1,
            grid=(steps,),
            in_specs=in_specs,
            out_specs=pl.BlockSpec((rows, columns), lambda i, p: (place_of(i, p), 0)),
        ),
        cost_estimate=pl.CostEstimate(
            flops=0, transcendentals=0, bytes_accessed=4 * rows * steps * columns
        ),
    )(net.place, *flat)


def widen(stack, columns, moves, first, rows):
    count, _, width = stack.shape
    block = rows // 4
    skip = first // block

    def body(stack_ref, out_ref):
        for k, source, span, target in moves:
            out_ref[:, target : target + span] = stack_ref[k, :, source : source + span].astype(
                F32
            )

    return pl.pallas_call(
        body,
        name="widen",
        out_shape=jax.ShapeDtypeStruct((rows, columns), F32),
        grid=(4,),
        in_specs=[pl.BlockSpec((count, block, width), lambda i: (0, i + skip, 0))],
        out_specs=pl.BlockSpec((block, columns), lambda i: (i, 0)),
        cost_estimate=pl.CostEstimate(
            flops=0, transcendentals=0, bytes_accessed=6 * rows * columns
        ),
    )(stack)


def weight_grad(net, left_t, right, cuts, split_left):
    total, tokens = left_t.shape
    columns = right.shape[1]
    widths = [cut_width(span, net.pairs) for _, span, _ in cuts]
    half = net.pairs // 2
    shapes = [(w, columns) if split_left else (total, w) for w in widths]

    def body(place, left_ref, right_ref, *outs):
        step = pl.program_id(0)
        slabs = []
        for (start, span, order), width in zip(cuts, widths):
            piece = (place[0] // 2) ^ piece_of_rank(step, order)
            at = pl.multiple_of(start + cut_offset(piece, span, net.pairs), LANES)
            if split_left:
                slabs.append(left_ref[pl.ds(at, width), :])
            else:
                slabs.append(right_ref[:, pl.ds(at, width)])
        axis = 0 if split_left else 1
        slab = slabs[0] if len(slabs) == 1 else jnp.concatenate(slabs, axis=axis)
        pair = (slab, right_ref[...]) if split_left else (left_ref[...], slab)
        val = jnp.dot(*pair, preferred_element_type=F32).astype(BF16)

        def put(which):
            at = 0
            for k, width in enumerate(widths):
                span = slice(at, at + width)
                outs[2 * k + which][0] = val[span, :] if split_left else val[:, span]
                at += width

        @pl.when(step < half)
        def _():
            put(0)

        @pl.when(step >= half)
        def _():
            put(1)

    out_shape, out_specs = [], []
    for shape in shapes:
        out_shape += [jax.ShapeDtypeStruct((half,) + shape, BF16)] * 2
        out_specs += [
            pl.BlockSpec((1,) + shape, lambda i, p: (jnp.minimum(i, half - 1), 0, 0)),
            pl.BlockSpec((1,) + shape, lambda i, p: (jnp.maximum(i - half, 0), 0, 0)),
        ]
    outs = pl.pallas_call(
        body,
        name="weight_grad",
        out_shape=out_shape,
        grid_spec=pltpu.PrefetchScalarGridSpec(
            num_scalar_prefetch=1,
            grid=(net.pairs,),
            in_specs=[
                pl.BlockSpec((total, tokens), lambda i, p: (0, 0)),
                pl.BlockSpec((tokens, columns), lambda i, p: (0, 0)),
            ],
            out_specs=out_specs,
        ),
        cost_estimate=pl.CostEstimate(
            flops=2 * total * tokens * columns,
            transcendentals=0,
            bytes_accessed=2 * (total * tokens + tokens * columns + total * columns),
        ),
    )(net.place, left_t, right)
    return [tuple(outs[2 * k : 2 * k + 2]) for k in range(len(cuts))]


def attend_forward(queries_t, keys, values_t, runs):
    heads, size, rows = queries_t.shape
    total = keys.shape[1]
    blocks = rows // BLK
    lead = total // BLK - blocks

    def body(runs_ref, q_ref, k_ref, v_ref, o_ref):
        block = pl.program_id(0)
        run = runs_ref[block]
        for n in range(1, SEQ_BLOCKS + 1):

            @pl.when(run == n - 1)
            def _():
                low = pl.multiple_of((block + (lead + 1 - n)) * BLK, BLK)

                def head(h, carry):
                    g = h // (heads // KVH)
                    scores = jnp.dot(
                        k_ref[g, pl.ds(low, n * BLK), :], q_ref[h], preferred_element_type=F32
                    )
                    top = jnp.max(scores, axis=0, keepdims=True)
                    expon = jnp.exp(scores - top)
                    norm = jnp.sum(expon, axis=0, keepdims=True)
                    out = jnp.dot(
                        v_ref[g, :, pl.ds(low, n * BLK)],
                        expon.astype(BF16),
                        preferred_element_type=F32,
                    )
                    o_ref[h] = (out / norm).astype(BF16)
                    return carry

                lax.fori_loop(0, heads, head, 0, unroll=2)

    return pl.pallas_call(
        body,
        name="attend_forward",
        out_shape=jax.ShapeDtypeStruct((heads, size, rows), BF16),
        grid_spec=pltpu.PrefetchScalarGridSpec(
            num_scalar_prefetch=1,
            grid=(blocks,),
            in_specs=[
                pl.BlockSpec((heads, size, BLK), lambda i, r: (0, 0, i)),
                pl.BlockSpec((KVH, total, size), lambda i, r: (0, 0, 0)),
                pl.BlockSpec((KVH, size, total), lambda i, r: (0, 0, 0)),
            ],
            out_specs=pl.BlockSpec((heads, size, BLK), lambda i, r: (0, 0, i)),
        ),
        cost_estimate=pl.CostEstimate(
            flops=32 * heads * rows * total * size,
            transcendentals=heads * rows * total,
            bytes_accessed=8 * heads * rows * size,
        ),
    )(runs, queries_t, keys, values_t)


def attend_backward(queries_t, grads_t, keys, keys_t, values, runs):
    heads, size, rows = queries_t.shape
    total = keys.shape[1]
    blocks = rows // BLK
    lead = total // BLK - blocks

    def body(runs_ref, q_ref, g_ref, k_ref, kt_ref, v_ref, dq_ref, dk_ref, dv_ref, dk_acc, dv_acc):
        block = pl.program_id(0)
        run = runs_ref[block]

        @pl.when(block == 0)
        def _():
            dk_acc[...] = jnp.zeros_like(dk_acc)
            dv_acc[...] = jnp.zeros_like(dv_acc)

        for n in range(1, SEQ_BLOCKS + 1):

            @pl.when(run == n - 1)
            def _():
                low = pl.multiple_of((block + (lead + 1 - n)) * BLK, BLK)
                span = pl.ds(low, n * BLK)

                def head(h, carry):
                    g = h // (heads // KVH)
                    query_t = q_ref[h]
                    grad_t = g_ref[h]
                    scores = jnp.dot(k_ref[g, span, :], query_t, preferred_element_type=F32)
                    d_probs = jnp.dot(v_ref[g, span, :], grad_t, preferred_element_type=F32)
                    top = jnp.max(scores, axis=0, keepdims=True)
                    expon = jnp.exp(scores - top)
                    probs = expon * (1.0 / jnp.sum(expon, axis=0, keepdims=True))
                    delta = jnp.sum(probs * d_probs, axis=0, keepdims=True)
                    d_scores = (probs * (d_probs - delta)).astype(BF16)
                    dq_ref[h] = jnp.dot(kt_ref[g, :, span], d_scores, preferred_element_type=F32)
                    dk_acc[g, span, :] += jnp.dot(
                        d_scores, query_t.T, preferred_element_type=F32
                    )
                    dv_acc[g, span, :] += jnp.dot(
                        probs.astype(BF16), grad_t.T, preferred_element_type=F32
                    )
                    return carry

                lax.fori_loop(0, heads, head, 0)

        @pl.when(block == blocks - 1)
        def _():
            for g in range(KVH):
                dk_ref[g] = dk_acc[g].T
                dv_ref[g] = dv_acc[g].T

    return pl.pallas_call(
        body,
        name="attend_backward",
        out_shape=(
            jax.ShapeDtypeStruct((heads, size, rows), F32),
            jax.ShapeDtypeStruct((KVH, size, total), F32),
            jax.ShapeDtypeStruct((KVH, size, total), F32),
        ),
        grid_spec=pltpu.PrefetchScalarGridSpec(
            num_scalar_prefetch=1,
            grid=(blocks,),
            in_specs=[
                pl.BlockSpec((heads, size, BLK), lambda i, r: (0, 0, i)),
                pl.BlockSpec((heads, size, BLK), lambda i, r: (0, 0, i)),
                pl.BlockSpec((KVH, total, size), lambda i, r: (0, 0, 0)),
                pl.BlockSpec((KVH, size, total), lambda i, r: (0, 0, 0)),
                pl.BlockSpec((KVH, total, size), lambda i, r: (0, 0, 0)),
            ],
            out_specs=(
                pl.BlockSpec((heads, size, BLK), lambda i, r: (0, 0, i)),
                pl.BlockSpec((KVH, size, total), lambda i, r: (0, 0, 0)),
                pl.BlockSpec((KVH, size, total), lambda i, r: (0, 0, 0)),
            ),
            scratch_shapes=[
                pltpu.VMEM((KVH, total, size), F32),
                pltpu.VMEM((KVH, total, size), F32),
            ],
        ),
        cost_estimate=pl.CostEstimate(
            flops=64 * heads * rows * total * size,
            transcendentals=heads * rows * total,
            bytes_accessed=8 * heads * rows * size,
        ),
    )(runs, queries_t, grads_t, keys, keys_t, values)


def contract(left, right, left_dim, right_dim):
    return lax.dot_general(
        left, right, (((left_dim,), (right_dim,)), ((), ())), preferred_element_type=F32
    )


def rotate(values, cosine, sine):
    half = HD // 2
    upper, lower = values[:, :half], values[:, half:]
    return jnp.concatenate(
        [upper * cosine - lower * sine, lower * cosine + upper * sine], axis=1
    )


def rms_unit(values, axis):
    scale = lax.rsqrt(jnp.mean(values * values, axis=axis, keepdims=True) + EPS)
    return (values * scale, scale)


def norm_back(grad, unit, scale, axis):
    return scale * (grad - unit * jnp.mean(grad * unit, axis=axis, keepdims=True))


def on_device(
    tokens,
    cotangent,
    seq_ids,
    block_ids,
    positions,
    first_gain,
    query_weight,
    query_bias,
    key_weight,
    key_bias,
    value_weight,
    value_bias,
    out_weight,
    second_gain,
    gate_weight,
    up_weight,
    down_weight,
):
    net = Net()
    seqs = net.seqs
    order_a, order_b = net.orders
    rows, width = tokens.shape
    kv_width = KVH * HD
    query_width = H * HD
    runs = block_ids[::BLK]
    own_half = net.seq // (seqs // 2) == net.half
    even = net.seq % 2 == 0

    attn_shard = jnp.concatenate([query_weight, key_weight, value_weight, out_weight], axis=1)
    attn_columns = attn_shard.shape[1]
    vectors = jnp.concatenate([first_gain, query_bias, key_bias, value_bias, second_gain])
    sizes = [
        first_gain.shape[0],
        query_bias.shape[0],
        key_bias.shape[0],
        value_bias.shape[0],
        second_gain.shape[0],
    ]
    ends = [sum(sizes[: i + 1]) for i in range(len(sizes))]
    shard = attn_shard.shape[0]
    attn_width = cut_width(attn_columns, net.reps)
    attn_piece = lax.dynamic_slice_in_dim(
        attn_shard, cut_offset(net.rep, attn_columns, net.reps), attn_width, 1
    )
    extra = pl.cdiv(vectors.shape[0], attn_width * 8) * 8
    vector_rows = jnp.pad(vectors, (0, extra * attn_width - vectors.shape[0])).reshape(
        extra, attn_width
    )
    attn_seq = net.gather_seq(jnp.concatenate([attn_piece, vector_rows], axis=0)).reshape(
        seqs, shard + extra, attn_width
    )
    vector_all = attn_seq[:, shard:].reshape(seqs, -1).astype(F32)
    attn_seq = attn_seq[:, :shard].reshape(seqs * shard, attn_width)
    gain_one, query_bias_f, key_bias_f, value_bias_f, gain_two = [
        vector_all[:, e - s : e].reshape(-1) for s, e in zip(sizes, ends)
    ]
    top, low = attn_seq[: seqs * shard // 2], attn_seq[seqs * shard // 2 :]
    pieces = [net.spread(top, order_a), net.spread(low, order_b)]
    pieces = [
        [v for m in range(net.pairs) for v in (group[m], net.flip(group[m], 1))]
        for group in pieces
    ]
    part = seqs * shard // 2
    attn_full = jnp.concatenate(
        [
            assemble(
                net,
                [(0, attn_columns, net.reps, group)],
                attn_columns,
                lambda place: place[0],
                part // 2,
                2,
                lambda i, p: i,
            )
            for group in pieces
        ],
        axis=0,
    )
    proj_full = attn_full[:, : query_width + 2 * kv_width]
    out_full = attn_full[:, query_width + 2 * kv_width :]

    units = gate_weight.shape[1] // 2
    unit_width = cut_width(units, net.pairs)

    def gather_units(weight):
        start = net.half * units + cut_offset(net.pair, units, net.pairs)
        return lax.dynamic_slice_in_dim(weight, start, unit_width, 1)

    both_seq = net.gather_seq(
        jnp.concatenate([gather_units(gate_weight), gather_units(up_weight)], axis=0)
    ).reshape(seqs, 2, shard, unit_width)
    both_seq = jnp.concatenate([both_seq, both_seq], axis=0)
    both_seq = lax.dynamic_slice_in_dim(both_seq, net.seq + 1, seqs - 1, 0)
    gate_seq = both_seq[:, 0].reshape((seqs - 1) * shard, unit_width)
    up_seq = both_seq[:, 1].reshape((seqs - 1) * shard, unit_width)
    tiles = width // LANES
    split = pl.cdiv(tiles, 2) * LANES
    colours = [(0, split, order_a), (split, width - split, order_b)]
    down_piece = jnp.concatenate(
        [
            lax.dynamic_slice_in_dim(
                down_weight,
                start + cut_offset(net.pair, span, net.pairs),
                cut_width(span, net.pairs),
                1,
            )
            for start, span, _ in colours
        ],
        axis=1,
    )
    down_piece = after(down_piece, gate_seq, up_seq)
    held = jnp.where(own_half, down_piece, net.flip_seq(down_piece, seqs // 2))
    other = net.flip_seq(held, 1)
    down_seq = jnp.concatenate(
        [jnp.where(even, held, other), jnp.where(even, other, held)], axis=0
    )

    cotangent_both = jnp.concatenate([cotangent, net.flip(cotangent, 1)], axis=0)

    tokens_wide = tokens.astype(F32)
    unit_one, scale_one = rms_unit(tokens_wide, 1)
    normed_one = (unit_one * gain_one).astype(BF16)
    freqs = ROPE_BASE ** (-(jnp.arange(HD // 2, dtype=F32) * 2.0 / HD))
    angles = freqs[:, None] * positions.astype(F32)[None, :]
    cosine, sine = jnp.cos(angles), jnp.sin(angles)
    bias = jnp.concatenate([query_bias_f, key_bias_f, value_bias_f])
    proj_t = contract(proj_full, normed_one, 0, 1) + bias[:, None]
    factor = HD ** (-0.5)
    queries_t = rotate(proj_t[:query_width].reshape(H, HD, rows), cosine, sine)
    queries_t = (queries_t.astype(BF16).astype(F32) * factor).astype(BF16)
    keys_own = rotate(
        proj_t[query_width : query_width + kv_width].reshape(KVH, HD, rows), cosine, sine
    ).astype(BF16)
    values_own = proj_t[query_width + kv_width :].astype(BF16)
    kv_own = jnp.concatenate([keys_own.reshape(kv_width, rows), values_own], axis=0)
    gate_parts, up_parts = {0: gate_seq}, {0: up_seq}
    bits_a, bits_b = list(order_a), list(order_b)
    net.grow(gate_parts, bits_a[0])
    net.grow(up_parts, bits_b[0])
    halo = []
    need = (SEQ_BLOCKS - 1) * BLK
    step = 1
    while need > 0:
        take = min(need, rows)
        halo.insert(0, net.slide(kv_own[:, rows - take :], step))
        need -= take
        step += 1
    kv_t = jnp.concatenate(halo + [kv_own], axis=1).reshape(2 * KVH, HD, -1)
    kv_t = after(kv_t, gate_parts, up_parts)
    for bit_a, bit_b in zip(bits_a[1:], bits_b[1:]):
        net.grow(gate_parts, bit_a)
        net.grow(up_parts, bit_b)
    gate_pieces = [gate_parts[m] for m in range(net.pairs)]
    up_pieces = [up_parts[m] for m in range(net.pairs)]
    kv = jnp.transpose(kv_t, (0, 2, 1))
    attended_t = attend_forward(queries_t, kv[:KVH], kv_t[KVH:], runs)
    attended_t = attended_t.reshape(query_width, rows)
    mixed = tokens_wide + contract(attended_t, out_full, 0, 0)

    unit_two, scale_two = rms_unit(mixed, 1)
    normed_two = (unit_two * gain_two).astype(BF16)
    normed_both = jnp.concatenate([normed_two, net.flip(normed_two, 1)], axis=0)
    pair_index = lambda place: place[0] // 2
    down_seq = after(down_seq, gate_pieces, up_pieces)
    down_pieces, at = [], 0
    for start, span, order in colours:
        piece_width = cut_width(span, net.pairs)
        piece = down_seq[:, at : at + piece_width]
        down_pieces.append((start, span, net.pairs, net.spread(piece, order)))
        at += piece_width
    next_shard = lambda i, p: (p[1] + i) % seqs

    def assemble_units(pieces, weight):
        own = lax.dynamic_slice_in_dim(weight, net.half * units, units, 1)
        region = (0, units, net.pairs, pieces)
        return assemble(net, [region], units, pair_index, shard, seqs, next_shard, own)

    gate_half = assemble_units(gate_pieces, gate_weight)
    up_half = assemble_units(up_pieces, up_weight)
    gate_pre = contract(normed_both, gate_half, 1, 0)
    up_pre = contract(normed_both, up_half, 1, 0)
    sigmoid_gate = jax.nn.sigmoid(gate_pre)
    silu_gate = gate_pre * sigmoid_gate
    hidden = (silu_gate * up_pre).astype(BF16)
    grad_down = weight_grad(net, cotangent_both.T, hidden, colours, True)
    fold_down = [Fold(net, g, order) for g, (_, _, order) in zip(grad_down, colours)]
    down_half = assemble(
        net, down_pieces, width, pair_index, units // 4, 4, lambda i, p: i
    )
    output_both = contract(hidden, down_half, 1, 0)
    output = (mixed + output_both[:rows] + net.flip(output_both[rows:], 1)).astype(BF16)
    d_hidden = contract(after(cotangent_both, grad_down), down_half, 1, 1)
    d_gate = (d_hidden * up_pre * sigmoid_gate * (1.0 + gate_pre * (1.0 - sigmoid_gate))).astype(
        BF16
    )
    d_up = (d_hidden * silu_gate).astype(BF16)
    normed_both_t = normed_both.T
    for fold in fold_down:
        fold.step()
    grad_gate = weight_grad(net, normed_both_t, d_gate, [(0, units, order_a)], False)
    grad_up = weight_grad(net, normed_both_t, d_up, [(0, units, order_b)], False)
    fold_units = [Fold(net, grad_gate[0], order_a), Fold(net, grad_up[0], order_b)]
    d_gate, d_up = after((d_gate, d_up), grad_gate, grad_up, *[f.state() for f in fold_down])
    d_normed_both = contract(d_gate, gate_half, 1, 1) + contract(d_up, up_half, 1, 1)
    d_normed_two = d_normed_both[:rows] + net.flip(d_normed_both[rows:], 1)
    grad_gain_two = jnp.sum(d_normed_two * unit_two, axis=0)
    d_mixed = cotangent.astype(F32) + norm_back(d_normed_two * gain_two, unit_two, scale_two, 1)

    for fold in fold_down:
        fold.rest()
    d_mixed = after(d_mixed, *[f.keep for f in fold_down])
    for fold in fold_units:
        fold.step()
    piece = jnp.concatenate([f.keep[0] for f in fold_down], axis=0).T
    span = piece.shape[0] // 2
    first, second = piece[:span], piece[span:]
    mine = jnp.where(even, first, second)
    mine = mine.astype(F32) + net.flip_seq(jnp.where(even, second, first), 1).astype(F32)
    mine = (mine + net.flip_seq(mine.astype(BF16), seqs // 2).astype(F32)).astype(BF16)
    mine = jnp.where(own_half, mine, net.flip(mine, 1))

    d_branch = d_mixed.astype(BF16)
    d_attended_t = contract(out_full, d_branch, 1, 1).astype(BF16)
    d_query_t, d_key_t, d_value_t = attend_backward(
        queries_t, d_attended_t.reshape(H, HD, rows), kv[:KVH], kv_t[:KVH], kv[KVH:], runs
    )
    d_key_t, d_value_t = after((d_key_t, d_value_t), *[f.state() for f in fold_units])
    d_kv = jnp.concatenate(
        [d_key_t.reshape(kv_width, -1), d_value_t.reshape(kv_width, -1)], axis=0
    )
    lead = (SEQ_BLOCKS - 1) * BLK
    d_kv_own = d_kv[:, lead:]
    need = lead
    step = 1
    while need > 0:
        take = min(need, rows)
        back = net.slide(d_kv[:, need - take : need].astype(BF16), -step).astype(F32)
        d_kv_own = d_kv_own + jnp.pad(back, ((0, 0), (rows - take, 0)))
        need -= take
        step += 1
    d_query_pre_t = rotate(d_query_t * factor, cosine, -sine).reshape(query_width, rows)
    d_key_pre_t = rotate(d_kv_own[:kv_width].reshape(KVH, HD, rows), cosine, -sine)
    d_proj_t = jnp.concatenate(
        [d_query_pre_t, d_key_pre_t.reshape(kv_width, rows), d_kv_own[kv_width:]], axis=0
    ).astype(BF16)
    d_proj = d_proj_t.T
    grad_bias = jnp.sum(d_proj_t.astype(F32), axis=1)
    d_normed_one = contract(d_proj, proj_full, 1, 1)
    grad_gain_one = jnp.sum(d_normed_one * unit_one, axis=0)
    tokens_grad = (d_mixed + norm_back(d_normed_one * gain_one, unit_one, scale_one, 1)).astype(
        BF16
    )

    both = jnp.concatenate(
        [f.rest().reshape(seqs, shard, unit_width) for f in fold_units], axis=1
    ).reshape(-1, unit_width)
    both = lax.psum_scatter(both, "seq", scatter_dimension=0, tiled=True)
    both = lax.all_gather(both, "rep", axis=0)
    moves = [
        (2 * k + h, 0, unit_width, h * units + min(k * unit_width, units - unit_width))
        for k in range(net.pairs)
        for h in range(2)
    ]
    sum_gate = widen(both, 2 * units, moves, 0, shard)
    sum_up = widen(both, 2 * units, moves, shard, shard)
    mine = lax.all_gather(mine, "rep", axis=0, axis_index_groups=net.same_half)
    moves, at = [], 0
    for start, span, _ in colours:
        w = cut_width(span, net.pairs)
        moves += [(k, at, w, start + min(k * w, span - w)) for k in range(net.pairs)]
        at += w
    sum_down = widen(mine, width, moves, 0, mine.shape[1])

    grad_qkv = contract(normed_one, d_proj, 0, 0)
    grad_out = contract(attended_t, d_branch, 1, 0)
    grad_attn = jnp.concatenate([grad_qkv, grad_out], axis=1).astype(BF16)
    grad_attn = grad_attn.reshape(seqs, shard, attn_columns)
    pieces_of = lambda v: v.reshape(seqs, -1)
    small = jnp.concatenate(
        [
            pieces_of(grad_gain_one),
            pieces_of(grad_bias[:query_width]),
            pieces_of(grad_bias[query_width : query_width + kv_width]),
            pieces_of(grad_bias[query_width + kv_width :]),
            pieces_of(grad_gain_two),
        ],
        axis=1,
    ).astype(BF16)
    pad = 32
    small = jnp.pad(small, ((0, 0), (0, attn_columns - small.shape[1])))[:, None]
    small = jnp.pad(small, ((0, 0), (0, pad - 1), (0, 0)))
    grad_attn = jnp.concatenate([grad_attn, small], axis=1).reshape(-1, attn_columns)
    if attn_columns % (net.reps * LANES) == 0:
        stack = jnp.transpose(
            grad_attn.reshape(-1, net.reps, attn_width), (1, 0, 2)
        )
    else:
        stack = jnp.stack(
            [
                grad_attn[:, o : o + attn_width]
                for o in (
                    min(k * attn_width, attn_columns - attn_width) for k in range(net.reps)
                )
            ]
        )
    stack = lax.psum_scatter(stack, "rep", scatter_dimension=0, tiled=True)[0]
    stack = lax.psum_scatter(stack, "seq", scatter_dimension=0, tiled=True)
    stack = lax.all_gather(stack, "rep", axis=0)
    moves = [
        (k, 0, attn_width, min(k * attn_width, attn_columns - attn_width))
        for k in range(net.reps)
    ]
    sum_attn = widen(stack, attn_columns, moves, 0, stack.shape[1])
    row = sum_attn[shard]
    sum_gain_one, sum_query_bias, sum_key_bias, sum_value_bias, sum_gain_two = [
        row[e - s : e] for s, e in zip(sizes, ends)
    ]
    a, b, c = query_width, query_width + kv_width, query_width + 2 * kv_width
    return (
        output,
        tokens_grad,
        sum_gain_one,
        sum_attn[:shard, :a],
        sum_query_bias,
        sum_attn[:shard, a:b],
        sum_key_bias,
        sum_attn[:shard, b:c],
        sum_value_bias,
        sum_attn[:shard, c:],
        sum_gain_two,
        sum_gate,
        sum_up,
        sum_down,
    )


def solution(mesh):
    both = ("rep", "seq")
    return jax.shard_map(
        on_device,
        mesh=mesh,
        in_specs=(
            P(both, None),
            P(both, None),
            P(both),
            P(both),
            P(both),
            P("seq"),
            P("seq", None),
            P("seq"),
            P("seq", None),
            P("seq"),
            P("seq", None),
            P("seq"),
            P("seq", None),
            P("seq"),
            P("seq", None),
            P("seq", None),
            P("seq", None),
        ),
        out_specs=(
            P(both, None),
            P(both, None),
            P("seq"),
            P("seq", None),
            P("seq"),
            P("seq", None),
            P("seq"),
            P("seq", None),
            P("seq"),
            P("seq", None),
            P("seq"),
            P("seq", None),
            P("seq", None),
            P("seq", None),
        ),
        check_vma=False,
    )
```

time: 1600 us -> 769 us (0.48)
  waiting for transfers between devices: 983 us -> 350 us
  matrix products: 327 us -> 71 us
  Pallas kernels: 0 us -> 110 us
  blocking collectives: 123 us -> 16.9 us
  starting transfers between devices: 1.4 us -> 60.4 us
    reduce_scatter x9 -> x3, waiting for transfers between devices: 549 us -> 49.9 us  [the longest x1 49.8 us: on_device(): stack = lax.psum_scatter(stack, 'rep', scatter_dimension=0, tiled=True)[0]]
    dot_general x119 -> x12, matrix products: 327 us -> 71 us  [contract(): lax.dot_general(left, right, (((left_dim,), (right_dim,)), ((), ())), pre...]
    ppermute x0 -> x47, waiting for transfers between devices: none -> 199 us  [the longest x4 84.8 us: flip_seq(): return lax.ppermute(value, 'seq', [(i, i ^ bit) for i in range(self.seqs)])]
    all_gather x5 -> x4, waiting for transfers between devices: 274 us -> 100 us  [the longest x1 29.6 us: on_device(): mine = lax.all_gather(mine, 'rep', axis=0, axis_index_groups=net.same_half)]
    psum x2 -> x0, waiting for transfers between devices: 157 us -> none  [the longest x1 111 us: on_device(): lax.psum(own_query.astype(jnp.bfloat16), 'rep').astype(jnp.float32)]
    pallas_call x0 -> x14, Pallas kernels: none -> 110 us  [the longest x3 36.3 us: weight_grad(): pl.pallas_call(body, name='weight_grad', out_shape=out_shape, grid_spec=p...]
    all_gather x6 -> x1, blocking collectives: 98.9 us -> 16.9 us  [gather_seq(): return lax.all_gather(value, 'seq', axis=0, tiled=True)]
    ppermute x0 -> x47, starting transfers between devices: none -> 60.2 us  [the longest x39 32.7 us: flip(): return lax.ppermute(value, 'rep', [(i, i ^ bit) for i in range(self.reps)])]
  transfers between devices with their start and end apart: 16 -> 54, of which waited for: 11 -> 19; matrix products, arithmetic and copies ran while one was open for 14% -> 24% of each run, Pallas kernels for 0% -> 13%
where the time goes in v1:
time: 769 us; the launch traced here: 760 us
  waiting for transfers between devices  350 us (46%)
  Pallas kernels  110 us (14%)
  local copies, waits for them, and re-layouts  76.7 us (10%)
  matrix products  71 us (9%)
  starting transfers between devices  60.4 us (8%)
  other arithmetic  59.6 us (8%)
  blocking collectives  16.9 us (2%)
  between operations  15.6 us (2%)
    ppermute x4, waiting for transfers between devices, flip_seq(): return lax.ppermute(value, 'seq', [(i, i ^ bit) for i in range(self.seqs)])  84.8 us
    ppermute x39, waiting for transfers between devices, flip(): return lax.ppermute(value, 'rep', [(i, i ^ bit) for i in range(self.reps)])  81.4 us
    dot_general x12, matrix products, contract(): lax.dot_general(left, right, (((left_dim,), (right_dim,)), ((), ())), pre...  71 us
    reduce_scatter x1, waiting for transfers between devices, on_device(): stack = lax.psum_scatter(stack, 'rep', scatter_dimension=0, tiled=True)[0]  49.8 us
    pallas_call x3, Pallas kernels, weight_grad(): pl.pallas_call(body, name='weight_grad', out_shape=out_shape, grid_spec=p...  36.3 us
    ppermute x39, starting transfers between devices, flip(): return lax.ppermute(value, 'rep', [(i, i ^ bit) for i in range(self.reps)])  32.7 us
    ppermute x4, waiting for transfers between devices, slide(): return lax.ppermute(value, 'seq', pairs)  32.5 us
    all_gather x1, waiting for transfers between devices, on_device(): mine = lax.all_gather(mine, 'rep', axis=0, axis_index_groups=net.same_half)  29.6 us
  transfers between devices with their start and end apart: 54, of which 19 were waited for; matrix products, arithmetic and copies ran while one was open for 24% of the time, Pallas kernels for 13%

profile of v1, /device:TPU:0, one launch (start us, length us, event | category | flops | bytes accessed | tf_op | source)
XLA Modules:
  0.0 760.3 jit_solution(17985835276229006522)
XLA Ops:
  11.9 16.9 %all_gather.24 = bf16[928,256]{1,0:T(8,128)(2,1)S(1)} all-gather(bf16[232,256]{1,0:T(8,128)(2,1)S(1)} %pad_maximum_fusion.15), channel_id=1, replica_groups=mesh['rep'=8,'seq'=4] {'seq'}, dimensions={0}, use_global_device_ids=true | all-gather | bytes 593920 | tf_op jit(solution)/shard_map/all_gather | solution.py:51
  66.3 20.4 %all-gather.8.cloned.1.call-done = bf16[1792,640]{1,0:T(8,128)(2,1)} async-done(((bf16[448,640]{1,0:T(8,128)(2,1)}), bf16[1792,640]{1,0:T(8,128)(2,1)}) %all-gather.8.cloned.1.call-update) | async-done | bytes 2293776 | tf_op jit(solution)/shard_map/all_gather | solution.py:51
  124.0 13.8 %collective-permute-start.24 = (bf16[1216,256]{1,0:T(8,128)(2,1)}, bf16[1216,256]{1,0:T(8,128)(2,1)}, u32[]{:S(2)}, u32[]{:S(2)}) collective-permute-start(bf16[1216,256]{1,0:T(8,128)(2,1)} %copy.126), channel_id=1, source_target_pairs={{0,1},{1,0},{2,3},{3,2},{4,5},{5,4},{6,7},{7,6},{8,9},{9,8},{10,11... | collective-permute-start | bytes 1867784 | tf_op jit(solution)/shard_map/ppermute | solution.py:44
  142.5 12.1 %attend_forward.1 = bf16[14,64,512]{2,1,0:T(8,128)(2,1)} custom-call(s32[2]{0:T(128)} %slice.264.runs_ref, bf16[14,64,512]{2,1,0:T(8,128)(2,1)} %multiply_convert_fusion.4.q_ref, bf16[2,1280,64]{2,1,0:T(8,128)(2,1)} %get-tuple-element.146.k_ref, bf16[2,64,1280]{2,1,0:T(8,128)(2,1)} %get-tuple-element.152.v_ref), custom_call_target="tpu_custom_call" | custom-call | flops 18790481920 | bytes 3670016 | tf_op jit(solution)/shard_map/attend_forward/pallas_call | solution.py:281
  163.4 17.0 %collective-permute-done.22.refs_3_ = bf16[672,640]{1,0:T(8,128)(2,1)} collective-permute-done((bf16[672,640]{1,0:T(8,128)(2,1)}, bf16[672,640]{1,0:T(8,128)(2,1)}, u32[]{:S(2)}, u32[]{:S(2)}) %collective-permute-start.22) | collective-permute-done | bytes 860192 | tf_op jit(solution)/shard_map/ppermute | solution.py:41
  193.7 6.0 assemble.7
  199.8 8.2 %fusion.24 = f32[1024,2432]{1,0:T(8,128)S(1)} fusion(bf16[896,2432]{1,0:T(8,128)(2,1)} %assemble.7, bf16[512,896]{0,1:T(8,128)(2,1)} %collective-permute-done.18, bf16[512,896]{0,1:T(8,128)(2,1)} %multiply_convert_fusion.3), kind=kOutput, calls=%fused_computation.92 | convolution fusion | flops 4466409472 | bytes 16154624 | tf_op jit(solution)/shard_map/dot_general | solution.py:390
  215.1 12.0 %multiply_convert_fusion.2 = (bf16[1024,2432]{1,0:T(8,128)(2,1)}, f32[1024,2432]{1,0:T(8,128)}) fusion(f32[1024,2432]{1,0:T(8,128)S(1)} %fusion.24, bf16[896,2432]{1,0:T(8,128)(2,1)S(1)} %bitcast.87, bf16[512,896]{0,1:T(8,128)(2,1)} %collective-permute-done.18, bf16[512,896]{0,1:T(8,128)(2,1)} %multiply_convert_fusion.3), kind=kOutput, calls=%fused_computation.2 | convolution fusion | flops 4481351680 | bytes 31096832 | tf_op jit(solution)/shard_map/dot_general | solution.py:390
  227.1 11.9 %weight_grad.3 = (bf16[2,128,2432]{2,1,0:T(8,128)(2,1)}, bf16[2,128,2432]{2,1,0:T(8,128)(2,1)}, bf16[2,128,2432]{2,1,0:T(8,128)(2,1)}, bf16[2,128,2432]{2,1,0:T(8,128)(2,1)}) custom-call(s32[2]{0:T(128)} %pad_add_fusion.place, bf16[896,1024]{1,0:T(8,128)(2,1)} %get-tuple-element.141.left_ref, bf16[1024,2432]{1,0:T(8,128)(2,1)} %get-tuple-element.171.right_ref), custom_call_target="tpu_custom_call" | custom-call | flops 4462739456 | bytes 11173888 | tf_op jit(solution)/shard_map/weight_grad/pallas_call | solution.py:226
  262.9 16.1 %multiply_convert_fusion = (bf16[1024,2432]{1,0:T(8,128)(2,1)}, bf16[1024,2432]{1,0:T(8,128)(2,1)}) fusion(f32[1024,2432]{1,0:T(8,128)} %copy-done.40, f32[1024,2432]{1,0:T(8,128)} %get-tuple-element.172, bf16[1024,896]{0,1:T(8,128)(2,1)} %get-tuple-element.41, bf16[2432,896]{1,0:T(8,128)(2,1)} %assemble.9), kind=kOutput, calls=%fused_computation | convolution fusion | flops 4495114240 | bytes 36077568 | tf_op jit(solution)/shard_map/dot_general | solution.py:390
  279.0 12.1 %weight_grad.5 = (bf16[2,896,640]{2,1,0:T(8,128)(2,1)}, bf16[2,896,640]{2,1,0:T(8,128)(2,1)}) custom-call(s32[2]{0:T(128)} %pad_add_fusion.place, bf16[896,1024]{1,0:T(8,128)(2,1)} %fusion.22.left_ref, bf16[1024,2432]{1,0:T(8,128)(2,1)} %get-tuple-element.47.right_ref), custom_call_target="tpu_custom_call" | custom-call | flops 4462739456 | bytes 11173888 | tf_op jit(solution)/shard_map/weight_grad/pallas_call | solution.py:226
  291.8 12.3 %weight_grad.4 = (bf16[2,896,640]{2,1,0:T(8,128)(2,1)}, bf16[2,896,640]{2,1,0:T(8,128)(2,1)}) custom-call(s32[2]{0:T(128)} %pad_add_fusion.place, bf16[896,1024]{1,0:T(8,128)(2,1)} %fusion.22.left_ref, bf16[1024,2432]{1,0:T(8,128)(2,1)} %get-tuple-element.46.right_ref), custom_call_target="tpu_custom_call" | custom-call | flops 4462739456 | bytes 11173888 | tf_op jit(solution)/shard_map/weight_grad/pallas_call | solution.py:226
  310.5 42.0 %collective-permute-done.36 = bf16[1,128,2432]{2,1,0:T(8,128)(2,1)S(1)} collective-permute-done((bf16[1,128,2432]{2,1,0:T(8,128)(2,1)S(1)}, bf16[1,128,2432]{2,1,0:T(8,128)(2,1)S(1)}, u32[]{:S(2)}, u32[]{:S(2)}) %collective-permute-start.36) | collective-permute-done | bytes 622624 | tf_op jit(solution)/shard_map/ppermute | solution.py:41
  354.8 10.0 %collective-permute-done.37 = bf16[1,128,2432]{2,1,0:T(8,128)(2,1)S(1)} collective-permute-done((bf16[1,128,2432]{2,1,0:T(8,128)(2,1)S(1)}, bf16[1,128,2432]{2,1,0:T(8,128)(2,1)S(1)}, u32[]{:S(2)}, u32[]{:S(2)}) %collective-permute-start.37) | collective-permute-done | bytes 622624 | tf_op jit(solution)/shard_map/ppermute | solution.py:41
  367.0 6.9 fusion.58
  379.3 7.1 fusion.57
  400.2 20.7 %attend_backward.1 = (f32[14,64,512]{2,1,0:T(8,128)}, f32[2,64,1280]{2,1,0:T(8,128)}, f32[2,64,1280]{2,1,0:T(8,128)}) custom-call(s32[2]{0:T(128)} %slice.264.runs_ref, bf16[14,64,512]{2,1,0:T(8,128)(2,1)} %multiply_convert_fusion.4.q_ref, bf16[14,64,512]{2,1,0:T(8,128)(2,1)} %bitcast.110, bf16[2,1280,64]{2,1,0:T(8,128)(2,1)} %get-tuple-element.146.k_ref, ...), custom_call_target="tpu_custom_call" | custom-call | flops 37580963840 | bytes 3670016 | tf_op jit(solution)/shard_map/attend_backward/pallas_call | solution.py:353
  438.4 25.0 %collective-permute-done.41 = bf16[256,256]{1,0:T(8,128)(2,1)S(1)} collective-permute-done((bf16[256,256]{1,0:T(8,128)(2,1)S(1)}, bf16[256,256]{1,0:T(8,128)(2,1)S(1)}, u32[]{:S(2)}, u32[]{:S(2)}) %collective-permute-start.41) | collective-permute-done | bytes 131104 | tf_op jit(solution)/shard_map/ppermute | solution.py:48
  478.5 49.8 %reduce-scatter.4.cloned.1.call-done = bf16[1,1024,256]{2,1,0:T(8,128)(2,1)} async-done(((bf16[8,1024,256]{2,1,0:T(8,128)(2,1)}), bf16[1,1024,256]{2,1,0:T(8,128)(2,1)}) %reduce-scatter.4.cloned.1.call-update) | async-done | bytes 524304 | tf_op jit(solution)/shard_map/reduce_scatter | solution.py:718
  537.4 22.8 %collective-permute-done.44 = bf16[1216,256]{1,0:T(8,128)(2,1)} collective-permute-done((bf16[1216,256]{1,0:T(8,128)(2,1)}, bf16[1216,256]{1,0:T(8,128)(2,1)}, u32[]{:S(2)}, u32[]{:S(2)}) %collective-permute-start.44) | collective-permute-done | bytes 622624 | tf_op jit(solution)/shard_map/ppermute | solution.py:44
  569.4 58.6 %collective-permute-done.45 = bf16[1216,256]{1,0:T(8,128)(2,1)} collective-permute-done((bf16[1216,256]{1,0:T(8,128)(2,1)}, bf16[1216,256]{1,0:T(8,128)(2,1)}, u32[]{:S(2)}, u32[]{:S(2)}) %collective-permute-start.45) | collective-permute-done | bytes 622624 | tf_op jit(solution)/shard_map/ppermute | solution.py:44
  649.6 29.6 %all-gather.14.cloned.1.call-done = bf16[4864,256]{1,0:T(8,128)(2,1)} async-done(((bf16[1216,256]{1,0:T(8,128)(2,1)}), bf16[4864,256]{1,0:T(8,128)(2,1)}) %all-gather.14.cloned.1.call-update) | async-done | bytes 2490384 | tf_op jit(solution)/shard_map/all_gather | solution.py:678
  683.5 20.8 %all-gather.10.cloned.1.call-done = bf16[2048,256]{1,0:T(8,128)(2,1)} async-done(((bf16[256,256]{1,0:T(8,128)(2,1)}), bf16[2048,256]{1,0:T(8,128)(2,1)}) %all-gather.10.cloned.1.call-update) | async-done | bytes 1048592 | tf_op jit(solution)/shard_map/all_gather | solution.py:720
  715.1 29.4 %all-gather.12.cloned.1.call-done = bf16[3584,640]{1,0:T(8,128)(2,1)} async-done(((bf16[448,640]{1,0:T(8,128)(2,1)}), bf16[3584,640]{1,0:T(8,128)(2,1)}) %all-gather.12.cloned.1.call-update) | async-done | bytes 4587536 | tf_op jit(solution)/shard_map/all_gather | solution.py:670
  (348 shorter events, 262.9 us)
Async XLA Ops:
  7.2 79.5 %all-gather.8.cloned.1.call-start = ((), (), s32[]{:S(2)}) async-start(), calls=%async_computation.3 | async-start | bytes 2867200 | tf_op jit(solution)/shard_map/all_gather | solution.py:51
  35.9 492.4 %reduce-scatter.4.cloned.1.call-start = ((), (), s32[]{:S(2)}) async-start(), calls=%async_computation.4 | async-start | bytes 4718592 | tf_op jit(solution)/shard_map/reduce_scatter | solution.py:718
  53.2 48.7 %collective-permute-start.32 = (bf16[512,896]{0,1:T(8,128)(2,1)S(1)}, bf16[512,896]{0,1:T(8,128)(2,1)}, u32[]{:S(2)}, u32[]{:S(2)}) collective-permute-start(bf16[512,896]{0,1:T(8,128)(2,1)S(1)} %copy.139), channel_id=1, source_target_pairs={{0,4},{4,0},{8,12},{12,8},{16,20},{20,16},{24,28},{28,24},{1,5},{5... | collective-permute-start | bytes 2752520 | tf_op jit(solution)/shard_map/ppermute | solution.py:41
  100.4 37.4 %collective-permute-start.17 = (bf16[672,640]{1,0:T(8,128)(2,1)}, bf16[672,640]{1,0:T(8,128)(2,1)}, u32[]{:S(2)}, u32[]{:S(2)}) collective-permute-start(bf16[672,640]{1,0:T(8,128)(2,1)} %bitcast.11.refs_0_), channel_id=1, source_target_pairs={{0,16},{4,20},{8,24},{12,28},{16,0},{20,4},{24,8},{28,12},{1,17},{... | collective-permute-start | bytes 2580488 | tf_op jit(solution)/shard_map/ppermute | solution.py:41
  101.9 35.9 %collective-permute-start.16 = (bf16[672,640]{1,0:T(8,128)(2,1)}, bf16[672,640]{1,0:T(8,128)(2,1)}, u32[]{:S(2)}, u32[]{:S(2)}) collective-permute-start(bf16[672,640]{1,0:T(8,128)(2,1)} %bitcast.10.refs_0_), channel_id=1, source_target_pairs={{0,8},{4,12},{8,0},{12,4},{16,24},{20,28},{24,16},{28,20},{1,9},{5... | collective-permute-start | bytes 2580488 | tf_op jit(solution)/shard_map/ppermute | solution.py:41
  114.3 49.1 %collective-permute-start.21 = (bf16[672,640]{1,0:T(8,128)(2,1)}, bf16[672,640]{1,0:T(8,128)(2,1)}, u32[]{:S(2)}, u32[]{:S(2)}) collective-permute-start(bf16[672,640]{1,0:T(8,128)(2,1)} %bitcast.11.refs_0_), channel_id=1, source_target_pairs={{0,8},{4,12},{8,0},{12,4},{16,24},{20,28},{24,16},{28,20},{1,9},{5... | collective-permute-start | bytes 2580488 | tf_op jit(solution)/shard_map/ppermute | solution.py:41
  115.8 47.6 %collective-permute-start.19 = (bf16[672,640]{1,0:T(8,128)(2,1)}, bf16[672,640]{1,0:T(8,128)(2,1)}, u32[]{:S(2)}, u32[]{:S(2)}) collective-permute-start(bf16[672,640]{1,0:T(8,128)(2,1)} %bitcast.10.refs_0_), channel_id=1, source_target_pairs={{0,16},{4,20},{8,24},{12,28},{16,0},{20,4},{24,8},{28,12},{1,17},{... | collective-permute-start | bytes 2580488 | tf_op jit(solution)/shard_map/ppermute | solution.py:41
  158.6 41.1 %collective-permute-start.18 = (bf16[512,896]{0,1:T(8,128)(2,1)}, bf16[512,896]{0,1:T(8,128)(2,1)}, u32[]{:S(2)}, u32[]{:S(2)}) collective-permute-start(bf16[512,896]{0,1:T(8,128)(2,1)} %multiply_convert_fusion.3), channel_id=1, source_target_pairs={{0,4},{4,0},{8,12},{12,8},{16,20},{20,16},{24,28},{28,24},{1,5},{5... | collective-permute-start | bytes 2752520 | tf_op jit(solution)/shard_map/ppermute | solution.py:41
  184.4 62.5 %collective-permute-start.28 = (bf16[2432,128]{0,1:T(8,128)(2,1)S(1)}, bf16[2432,128]{0,1:T(8,128)(2,1)}, u32[]{:S(2)}, u32[]{:S(2)}) collective-permute-start(bf16[2432,128]{0,1:T(8,128)(2,1)S(1)} %get-tuple-element.149), channel_id=1, source_target_pairs={{0,8},{4,12},{8,0},{12,4},{16,24},{20,28},{24,16},{28,20},{1,9},{5... | collective-permute-start | bytes 1867784 | tf_op jit(solution)/shard_map/ppermute | solution.py:41
  185.8 64.7 %collective-permute-start.26 = (bf16[2432,128]{0,1:T(8,128)(2,1)S(1)}, bf16[2432,128]{0,1:T(8,128)(2,1)}, u32[]{:S(2)}, u32[]{:S(2)}) collective-permute-start(bf16[2432,128]{0,1:T(8,128)(2,1)S(1)} %get-tuple-element.150), channel_id=1, source_target_pairs={{0,16},{4,20},{8,24},{12,28},{16,0},{20,4},{24,8},{28,12},{1,17},{... | collective-permute-start | bytes 1867784 | tf_op jit(solution)/shard_map/ppermute | solution.py:41
  208.0 44.6 %collective-permute-start.30 = (bf16[2432,128]{0,1:T(8,128)(2,1)}, bf16[2432,128]{0,1:T(8,128)(2,1)}, u32[]{:S(2)}, u32[]{:S(2)}) collective-permute-start(bf16[2432,128]{0,1:T(8,128)(2,1)} %collective-permute-done.29), channel_id=1, source_target_pairs={{0,8},{4,12},{8,0},{12,4},{16,24},{20,28},{24,16},{28,20},{1,9},{5... | collective-permute-start | bytes 1867784 | tf_op jit(solution)/shard_map/ppermute | solution.py:41
  214.8 40.0 %collective-permute-start.27 = (bf16[2432,128]{0,1:T(8,128)(2,1)}, bf16[2432,128]{0,1:T(8,128)(2,1)}, u32[]{:S(2)}, u32[]{:S(2)}) collective-permute-start(bf16[2432,128]{0,1:T(8,128)(2,1)} %collective-permute-done.25), channel_id=1, source_target_pairs={{0,16},{4,20},{8,24},{12,28},{16,0},{20,4},{24,8},{28,12},{1,17},{... | collective-permute-start | bytes 1867784 | tf_op jit(solution)/shard_map/ppermute | solution.py:41
  238.9 66.5 %collective-permute-start.33 = (bf16[2,128,2432]{2,1,0:T(8,128)(2,1)}, bf16[2,128,2432]{2,1,0:T(8,128)(2,1)}, u32[]{:S(2)}, u32[]{:S(2)}) collective-permute-start(bf16[2,128,2432]{2,1,0:T(8,128)(2,1)} %get-tuple-element.38), channel_id=1, source_target_pairs={{0,8},{4,12},{8,0},{12,4},{16,24},{20,28},{24,16},{28,20},{1,9},{5... | collective-permute-start | bytes 3735560 | tf_op jit(solution)/shard_map/ppermute | solution.py:41
  247.0 61.7 %collective-permute-start.34 = (bf16[2,128,2432]{2,1,0:T(8,128)(2,1)}, bf16[2,128,2432]{2,1,0:T(8,128)(2,1)}, u32[]{:S(2)}, u32[]{:S(2)}) collective-permute-start(bf16[2,128,2432]{2,1,0:T(8,128)(2,1)} %get-tuple-element.40), channel_id=1, source_target_pairs={{0,16},{4,20},{8,24},{12,28},{16,0},{20,4},{24,8},{28,12},{1,17},{... | collective-permute-start | bytes 3735560 | tf_op jit(solution)/shard_map/ppermute | solution.py:41
  291.1 96.0 %collective-permute-start.39 = (bf16[2,896,640]{2,1,0:T(8,128)(2,1)}, bf16[2,896,640]{2,1,0:T(8,128)(2,1)}, u32[]{:S(2)}, u32[]{:S(2)}) collective-permute-start(bf16[2,896,640]{2,1,0:T(8,128)(2,1)} %get-tuple-element.45), channel_id=1, source_target_pairs={{0,16},{4,20},{8,24},{12,28},{16,0},{20,4},{24,8},{28,12},{1,17},{... | collective-permute-start | bytes 6881288 | tf_op jit(solution)/shard_map/ppermute | solution.py:41
  304.1 88.2 %collective-permute-start.38 = (bf16[2,896,640]{2,1,0:T(8,128)(2,1)}, bf16[2,896,640]{2,1,0:T(8,128)(2,1)S(1)}, u32[]{:S(2)}, u32[]{:S(2)}) collective-permute-start(bf16[2,896,640]{2,1,0:T(8,128)(2,1)} %get-tuple-element.43), channel_id=1, source_target_pairs={{0,8},{4,12},{8,0},{12,4},{16,24},{20,28},{24,16},{28,20},{1,9},{5... | collective-permute-start | bytes 6881288 | tf_op jit(solution)/shard_map/ppermute | solution.py:41
  306.8 45.6 %collective-permute-start.36 = (bf16[1,128,2432]{2,1,0:T(8,128)(2,1)S(1)}, bf16[1,128,2432]{2,1,0:T(8,128)(2,1)S(1)}, u32[]{:S(2)}, u32[]{:S(2)}) collective-permute-start(bf16[1,128,2432]{2,1,0:T(8,128)(2,1)S(1)} %add_convert_fusion.11), channel_id=1, source_target_pairs={{0,16},{4,20},{8,24},{12,28},{16,0},{20,4},{24,8},{28,12},{1,17},{... | collective-permute-start | bytes 1867784 | tf_op jit(solution)/shard_map/ppermute | solution.py:41
  310.0 54.8 %collective-permute-start.37 = (bf16[1,128,2432]{2,1,0:T(8,128)(2,1)S(1)}, bf16[1,128,2432]{2,1,0:T(8,128)(2,1)S(1)}, u32[]{:S(2)}, u32[]{:S(2)}) collective-permute-start(bf16[1,128,2432]{2,1,0:T(8,128)(2,1)S(1)} %add_convert_fusion.9), channel_id=1, source_target_pairs={{0,8},{4,12},{8,0},{12,4},{16,24},{20,28},{24,16},{28,20},{1,9},{5... | collective-permute-start | bytes 1867784 | tf_op jit(solution)/shard_map/ppermute | solution.py:41
  478.4 162.6 %reduce-scatter.6.cloned.1.call-start = ((), (), s32[]{:S(2)}) async-start(), calls=%async_computation.5 | async-start | bytes 655360 | tf_op jit(solution)/shard_map/reduce_scatter | solution.py:719
  528.3 113.2 %reduce-scatter.8.cloned.1.call-start = ((), (), s32[]{:S(2)}) async-start(), calls=%async_computation.6 | async-start | bytes 2867200 | tf_op jit(solution)/shard_map/reduce_scatter | solution.py:669
  531.2 148.0 %all-gather.14.cloned.1.call-start = ((), (), s32[]{:S(2)}) async-start(), calls=%async_computation.9 | async-start | bytes 3112960 | tf_op jit(solution)/shard_map/all_gather | solution.py:678
  567.0 61.0 %collective-permute-start.45 = (bf16[1216,256]{1,0:T(8,128)(2,1)}, bf16[1216,256]{1,0:T(8,128)(2,1)}, u32[]{:S(2)}, u32[]{:S(2)}) collective-permute-start(bf16[1216,256]{1,0:T(8,128)(2,1)} %copy.151), channel_id=1, source_target_pairs={{0,2},{1,3},{2,0},{3,1},{4,6},{5,7},{6,4},{7,5},{8,10},{9,11},{10,... | collective-permute-start | bytes 1867784 | tf_op jit(solution)/shard_map/ppermute | solution.py:44
  640.9 63.4 %all-gather.10.cloned.1.call-start = ((), (), s32[]{:S(2)}) async-start(), calls=%async_computation.7 | async-start | bytes 1179648 | tf_op jit(solution)/shard_map/all_gather | solution.py:720
  641.5 103.0 %all-gather.12.cloned.1.call-start = ((), (), s32[]{:S(2)}) async-start(), calls=%async_computation.8 | async-start | bytes 5160960 | tf_op jit(solution)/shard_map/all_gather | solution.py:670
  (80 other events, 1216.1 us)
Sparse Core Ops, SparseCore 0:
  36.1 50.5 all-gather.7
  478.5 49.6 reduce-scatter.3
  530.6 26.9 reduce-scatter.5
  560.3 68.6 reduce-scatter.7
  641.0 38.1 all-gather.13
  681.0 23.3 all-gather.9
  706.3 38.2 all-gather.11

commit v2 on v1

--- a/solution.py
+++ b/solution.py
@@ -61,27 +61,42 @@
 
 
 class Fold:
-    def __init__(self, net, parts, order):
+    def __init__(self, net, parts, order, scale=2):
         self.net = net
+        self.scale = scale
         self.keep, self.send = parts
         self.bits = list(order)
 
-    def step(self):
-        got = self.net.flip(self.send, 2 * self.bits.pop(0))
+    def launch(self):
+        self.got = self.net.flip(self.send, self.scale * self.bits.pop(0))
+
+    def collect(self):
         half = self.keep.shape[0] // 2
+        total = lambda own, got: (own.astype(F32) + got.astype(F32)).astype(BF16)
         if half == 0:
-            self.keep = (self.keep.astype(F32) + got.astype(F32)).astype(BF16)
+            self.keep = total(self.keep, self.got)
             return
-        self.send = (self.keep[half:].astype(F32) + got[half:].astype(F32)).astype(BF16)
-        self.keep = (self.keep[:half].astype(F32) + got[:half].astype(F32)).astype(BF16)
-
-    def state(self):
-        return (self.keep, self.send) if self.bits else (self.keep,)
-
-    def rest(self):
+        self.send = total(self.keep[half:], self.got[half:])
+        self.keep = total(self.keep[:half], self.got[:half])
+
+    def until_last(self):
         while self.bits:
-            self.step()
-        return self.keep[0]
+            self.collect()
+            self.launch()
+
+
+def got_of(folds):
+    return [f.got for f in folds]
+
+
+def launch_all(folds):
+    for fold in folds:
+        fold.launch()
+
+
+def collect_all(folds):
+    for fold in folds:
+        fold.collect()
 
 
 def after(value, *others):
@@ -105,7 +120,7 @@
     return piece
 
 
-def assemble(net, regions, columns, index, rows, steps, place_of, own=None):
+def assemble(net, regions, columns, index, rows, steps, place_of, own=None, dtype=BF16):
     flat = [p for region in regions for p in region[3]]
     skip = 0 if own is None else 1
 
@@ -116,9 +131,10 @@
             at = 0
             for start, span, parts, pieces in regions:
                 for m, piece in enumerate(pieces):
-                    offset = start + cut_offset(index(place) ^ m, span, parts)
+                    base = start(place) if callable(start) else start
+                    offset = base + cut_offset(index(place) ^ m, span, parts)
                     col = pl.multiple_of(offset, LANES)
-                    out[:, pl.ds(col, piece.shape[1])] = refs[at][...]
+                    out[:, pl.ds(col, piece.shape[1])] = refs[at][...].astype(dtype)
                     at += 1
 
         if own is None:
@@ -142,7 +158,7 @@
     return pl.pallas_call(
         body,
         name="assemble",
-        out_shape=jax.ShapeDtypeStruct((rows * steps, columns), flat[0].dtype),
+        out_shape=jax.ShapeDtypeStruct((rows * steps, columns), dtype),
         grid_spec=pltpu.PrefetchScalarGridSpec(
             num_scalar_prefetch=1,
             grid=(steps,),
@@ -155,67 +171,8 @@
     )(net.place, *flat)
 
 
-def widen(stack, columns, moves, first, rows):
-    count, _, width = stack.shape
-    block = rows // 4
-    skip = first // block
-
-    def body(stack_ref, out_ref):
-        for k, source, span, target in moves:
-            out_ref[:, target : target + span] = stack_ref[k, :, source : source + span].astype(
-                F32
-            )
-
-    return pl.pallas_call(
-        body,
-        name="widen",
-        out_shape=jax.ShapeDtypeStruct((rows, columns), F32),
-        grid=(4,),
-        in_specs=[pl.BlockSpec((count, block, width), lambda i: (0, i + skip, 0))],
-        out_specs=pl.BlockSpec((block, columns), lambda i: (i, 0)),
-        cost_estimate=pl.CostEstimate(
-            flops=0, transcendentals=0, bytes_accessed=6 * rows * columns
-        ),
-    )(stack)
-
-
-def weight_grad(net, left_t, right, cuts, split_left):
-    total, tokens = left_t.shape
-    columns = right.shape[1]
-    widths = [cut_width(span, net.pairs) for _, span, _ in cuts]
+def pieces_call(net, body, name, left, right, shapes):
     half = net.pairs // 2
-    shapes = [(w, columns) if split_left else (total, w) for w in widths]
-
-    def body(place, left_ref, right_ref, *outs):
-        step = pl.program_id(0)
-        slabs = []
-        for (start, span, order), width in zip(cuts, widths):
-            piece = (place[0] // 2) ^ piece_of_rank(step, order)
-            at = pl.multiple_of(start + cut_offset(piece, span, net.pairs), LANES)
-            if split_left:
-                slabs.append(left_ref[pl.ds(at, width), :])
-            else:
-                slabs.append(right_ref[:, pl.ds(at, width)])
-        axis = 0 if split_left else 1
-        slab = slabs[0] if len(slabs) == 1 else jnp.concatenate(slabs, axis=axis)
-        pair = (slab, right_ref[...]) if split_left else (left_ref[...], slab)
-        val = jnp.dot(*pair, preferred_element_type=F32).astype(BF16)
-
-        def put(which):
-            at = 0
-            for k, width in enumerate(widths):
-                span = slice(at, at + width)
-                outs[2 * k + which][0] = val[span, :] if split_left else val[:, span]
-                at += width
-
-        @pl.when(step < half)
-        def _():
-            put(0)
-
-        @pl.when(step >= half)
-        def _():
-            put(1)
-
     out_shape, out_specs = [], []
     for shape in shapes:
         out_shape += [jax.ShapeDtypeStruct((half,) + shape, BF16)] * 2
@@ -223,26 +180,158 @@
             pl.BlockSpec((1,) + shape, lambda i, p: (jnp.minimum(i, half - 1), 0, 0)),
             pl.BlockSpec((1,) + shape, lambda i, p: (jnp.maximum(i - half, 0), 0, 0)),
         ]
+
+    def whole(place, left_ref, right_ref, *outs):
+        step = pl.program_id(0)
+        values = body(step, place[0] // 2, left_ref, right_ref)
+
+        @pl.when(step < half)
+        def _():
+            for k, value in enumerate(values):
+                outs[2 * k][0] = value
+
+        @pl.when(step >= half)
+        def _():
+            for k, value in enumerate(values):
+                outs[2 * k + 1][0] = value
+
     outs = pl.pallas_call(
-        body,
-        name="weight_grad",
+        whole,
+        name=name,
         out_shape=out_shape,
         grid_spec=pltpu.PrefetchScalarGridSpec(
             num_scalar_prefetch=1,
             grid=(net.pairs,),
             in_specs=[
-                pl.BlockSpec((total, tokens), lambda i, p: (0, 0)),
-                pl.BlockSpec((tokens, columns), lambda i, p: (0, 0)),
+                pl.BlockSpec(left.shape, lambda i, p: (0, 0)),
+                pl.BlockSpec(right.shape, lambda i, p: (0, 0)),
             ],
             out_specs=out_specs,
         ),
+        cost_estimate=pl.CostEstimate(
+            flops=2 * left.shape[0] * left.shape[1] * right.shape[1],
+            transcendentals=0,
+            bytes_accessed=2 * (left.size + right.size + left.shape[0] * right.shape[1]),
+        ),
+    )(net.place, left, right)
+    return [tuple(outs[2 * k : 2 * k + 2]) for k in range(len(shapes))]
+
+
+def unit_grad(net, left_t, right):
+    total, tokens = left_t.shape
+    columns = right.shape[1]
+    width = cut_width(columns, net.pairs)
+    start = lambda i: cut_offset(i, columns, net.pairs)
+
+    def body(left_ref, right_ref, out_ref):
+        at = pl.multiple_of(start(pl.program_id(0)), LANES)
+        out_ref[0] = jnp.dot(
+            left_ref[...], right_ref[:, pl.ds(at, width)], preferred_element_type=F32
+        ).astype(BF16)
+
+    return pl.pallas_call(
+        body,
+        name="unit_grad",
+        out_shape=jax.ShapeDtypeStruct((net.pairs, total, width), BF16),
+        grid=(net.pairs,),
+        in_specs=[
+            pl.BlockSpec((total, tokens), lambda i: (0, 0)),
+            pl.BlockSpec((tokens, columns), lambda i: (0, 0)),
+        ],
+        out_specs=pl.BlockSpec((1, total, width), lambda i: (i, 0, 0)),
         cost_estimate=pl.CostEstimate(
             flops=2 * total * tokens * columns,
             transcendentals=0,
-            bytes_accessed=2 * (total * tokens + tokens * columns + total * columns),
-        ),
-    )(net.place, left_t, right)
-    return [tuple(outs[2 * k : 2 * k + 2]) for k in range(len(cuts))]
+            bytes_accessed=2 * (left_t.size + right.size + total * columns),
+        ),
+    )(left_t, right)
+
+
+def down_grad(net, left_t, right, colours):
+    widths = [cut_width(span, net.pairs) for _, span, _ in colours]
+    columns = right.shape[1]
+
+    def body(step, pair, left_ref, right_ref):
+        slabs = []
+        for (start, span, order), width in zip(colours, widths):
+            piece = pair ^ piece_of_rank(step, order)
+            at = pl.multiple_of(start + cut_offset(piece, span, net.pairs), LANES)
+            slabs.append(left_ref[pl.ds(at, width), :])
+        val = jnp.dot(
+            jnp.concatenate(slabs, axis=0), right_ref[...], preferred_element_type=F32
+        ).T.astype(BF16)
+        values, at = [], 0
+        for width in widths:
+            values.append(val[:, at : at + width])
+            at += width
+        return values
+
+    return pieces_call(net, body, "down_grad", left_t, right, [(columns, w) for w in widths])
+
+
+def attn_grad(net, first_t, first_right, second_t, second_right, extra, orders):
+    reps, seqs = net.reps, net.seqs
+    rows = first_t.shape[0] // seqs
+    pad = extra.shape[1]
+    part = (rows + pad) // len(orders)
+    split = first_right.shape[1]
+    columns = split + second_right.shape[1]
+    width = cut_width(columns, reps)
+    half = reps // 2
+
+    def body(place, a_ref, b_ref, c_ref, d_ref, e_ref, *refs):
+        outs, full = refs[:-1], refs[-1]
+        step = pl.program_id(0)
+
+        @pl.when(step == 0)
+        def _():
+            first = jnp.dot(a_ref[...], b_ref[...], preferred_element_type=F32).astype(BF16)
+            second = jnp.dot(c_ref[...], d_ref[...], preferred_element_type=F32).astype(BF16)
+            for s in range(seqs):
+                full[s, :rows, :split] = first[s * rows : (s + 1) * rows]
+                full[s, :rows, split:] = second[s * rows : (s + 1) * rows]
+                full[s, rows:, :] = e_ref[s]
+
+        for k, order in enumerate(orders):
+            piece = place[0] ^ piece_of_rank(step, order)
+            at = pl.multiple_of(cut_offset(piece, columns, reps), LANES)
+
+            @pl.when(step < half)
+            def _():
+                outs[2 * k][0] = full[:, k * part : (k + 1) * part, pl.ds(at, width)]
+
+            @pl.when(step >= half)
+            def _():
+                outs[2 * k + 1][0] = full[:, k * part : (k + 1) * part, pl.ds(at, width)]
+
+    shape = (seqs, part, width)
+    out_shape, out_specs = [], []
+    for _ in orders:
+        out_shape += [jax.ShapeDtypeStruct((half,) + shape, BF16)] * 2
+        out_specs += [
+            pl.BlockSpec((1,) + shape, lambda i, p: (jnp.minimum(i, half - 1), 0, 0, 0)),
+            pl.BlockSpec((1,) + shape, lambda i, p: (jnp.maximum(i - half, 0), 0, 0, 0)),
+        ]
+    args = (first_t, first_right, second_t, second_right)
+    outs = pl.pallas_call(
+        body,
+        name="attn_grad",
+        out_shape=out_shape,
+        grid_spec=pltpu.PrefetchScalarGridSpec(
+            num_scalar_prefetch=1,
+            grid=(reps,),
+            in_specs=[pl.BlockSpec(v.shape, lambda i, p: (0, 0)) for v in args]
+            + [pl.BlockSpec(extra.shape, lambda i, p: (0, 0, 0))],
+            out_specs=out_specs,
+            scratch_shapes=[pltpu.VMEM((seqs, rows + pad, columns), BF16)],
+        ),
+        cost_estimate=pl.CostEstimate(
+            flops=2 * first_t.size * columns,
+            transcendentals=0,
+            bytes_accessed=2 * (seqs * (rows + pad) * columns + 4 * first_t.size),
+        ),
+    )(net.place, *args, extra)
+    return [tuple(outs[2 * k : 2 * k + 2]) for k in range(len(orders))]
 
 
 def attend_forward(queries_t, keys, values_t, runs):
@@ -451,9 +540,18 @@
     ends = [sum(sizes[: i + 1]) for i in range(len(sizes))]
     shard = attn_shard.shape[0]
     attn_width = cut_width(attn_columns, net.reps)
+    units = gate_weight.shape[1] // 2
+    unit_width = cut_width(units, net.pairs)
+
+    def cut_units(weight):
+        start = net.half * units + cut_offset(net.pair, units, net.pairs)
+        return lax.dynamic_slice_in_dim(weight, start, unit_width, 1)
+
+    unit_pieces = jnp.concatenate([cut_units(gate_weight), cut_units(up_weight)], axis=0)
     attn_piece = lax.dynamic_slice_in_dim(
         attn_shard, cut_offset(net.rep, attn_columns, net.reps), attn_width, 1
     )
+    attn_piece = after(attn_piece, unit_pieces)
     extra = pl.cdiv(vectors.shape[0], attn_width * 8) * 8
     vector_rows = jnp.pad(vectors, (0, extra * attn_width - vectors.shape[0])).reshape(
         extra, attn_width
@@ -491,41 +589,25 @@
     proj_full = attn_full[:, : query_width + 2 * kv_width]
     out_full = attn_full[:, query_width + 2 * kv_width :]
 
-    units = gate_weight.shape[1] // 2
-    unit_width = cut_width(units, net.pairs)
-
-    def gather_units(weight):
-        start = net.half * units + cut_offset(net.pair, units, net.pairs)
-        return lax.dynamic_slice_in_dim(weight, start, unit_width, 1)
-
-    both_seq = net.gather_seq(
-        jnp.concatenate([gather_units(gate_weight), gather_units(up_weight)], axis=0)
-    ).reshape(seqs, 2, shard, unit_width)
+    both_seq = net.gather_seq(unit_pieces).reshape(seqs, 2, shard, unit_width)
     both_seq = jnp.concatenate([both_seq, both_seq], axis=0)
     both_seq = lax.dynamic_slice_in_dim(both_seq, net.seq + 1, seqs - 1, 0)
     gate_seq = both_seq[:, 0].reshape((seqs - 1) * shard, unit_width)
     up_seq = both_seq[:, 1].reshape((seqs - 1) * shard, unit_width)
+
+    shard_units = down_weight.shape[0]
     tiles = width // LANES
     split = pl.cdiv(tiles, 2) * LANES
     colours = [(0, split, order_a), (split, width - split, order_b)]
-    down_piece = jnp.concatenate(
-        [
-            lax.dynamic_slice_in_dim(
-                down_weight,
-                start + cut_offset(net.pair, span, net.pairs),
-                cut_width(span, net.pairs),
-                1,
-            )
-            for start, span, _ in colours
-        ],
-        axis=1,
-    )
-    down_piece = after(down_piece, gate_seq, up_seq)
-    held = jnp.where(own_half, down_piece, net.flip_seq(down_piece, seqs // 2))
-    other = net.flip_seq(held, 1)
-    down_seq = jnp.concatenate(
-        [jnp.where(even, held, other), jnp.where(even, other, held)], axis=0
-    )
+    down_cuts = [
+        lax.dynamic_slice_in_dim(
+            down_weight,
+            start + cut_offset(net.pair, span, net.pairs),
+            cut_width(span, net.pairs),
+            1,
+        )
+        for start, span, _ in colours
+    ]
 
     cotangent_both = jnp.concatenate([cotangent, net.flip(cotangent, 1)], axis=0)
 
@@ -559,6 +641,8 @@
         step += 1
     kv_t = jnp.concatenate(halo + [kv_own], axis=1).reshape(2 * KVH, HD, -1)
     kv_t = after(kv_t, gate_parts, up_parts)
+    down_cuts = after(down_cuts, kv_t)
+    down_got = [net.flip_seq(v, seqs // 2) for v in down_cuts]
     for bit_a, bit_b in zip(bits_a[1:], bits_b[1:]):
         net.grow(gate_parts, bit_a)
         net.grow(up_parts, bit_b)
@@ -566,20 +650,15 @@
     up_pieces = [up_parts[m] for m in range(net.pairs)]
     kv = jnp.transpose(kv_t, (0, 2, 1))
     attended_t = attend_forward(queries_t, kv[:KVH], kv_t[KVH:], runs)
-    attended_t = attended_t.reshape(query_width, rows)
+    attended_t = after(attended_t.reshape(query_width, rows), down_got)
+    held = [jnp.where(own_half, u, v) for u, v in zip(down_cuts, down_got)]
+    other = [net.flip_seq(v, 1) for v in held]
     mixed = tokens_wide + contract(attended_t, out_full, 0, 0)
 
     unit_two, scale_two = rms_unit(mixed, 1)
     normed_two = (unit_two * gain_two).astype(BF16)
     normed_both = jnp.concatenate([normed_two, net.flip(normed_two, 1)], axis=0)
     pair_index = lambda place: place[0] // 2
-    down_seq = after(down_seq, gate_pieces, up_pieces)
-    down_pieces, at = [], 0
-    for start, span, order in colours:
-        piece_width = cut_width(span, net.pairs)
-        piece = down_seq[:, at : at + piece_width]
-        down_pieces.append((start, span, net.pairs, net.spread(piece, order)))
-        at += piece_width
     next_shard = lambda i, p: (p[1] + i) % seqs
 
     def assemble_units(pieces, weight):
@@ -590,53 +669,92 @@
     gate_half = assemble_units(gate_pieces, gate_weight)
     up_half = assemble_units(up_pieces, up_weight)
     gate_pre = contract(normed_both, gate_half, 1, 0)
-    up_pre = contract(normed_both, up_half, 1, 0)
+    down_seq = [
+        jnp.concatenate([jnp.where(even, u, v), jnp.where(even, v, u)], axis=0)
+        for u, v in zip(held, other)
+    ]
+    down_parts = [{0: v} for v in down_seq]
+    for held, order in zip(down_parts, (order_a, order_b)):
+        net.grow(held, order[0])
+    up_pre = contract(after(normed_both, other, gate_pre), up_half, 1, 0)
     sigmoid_gate = jax.nn.sigmoid(gate_pre)
     silu_gate = gate_pre * sigmoid_gate
-    hidden = (silu_gate * up_pre).astype(BF16)
-    grad_down = weight_grad(net, cotangent_both.T, hidden, colours, True)
+    hidden = after((silu_gate * up_pre).astype(BF16), down_parts)
+    for held, order in zip(down_parts, (order_a, order_b)):
+        for bit in order[1:]:
+            net.grow(held, bit)
+    down_pieces = [
+        (start, span, net.pairs, [held[m] for m in range(net.pairs)])
+        for held, (start, span, _) in zip(down_parts, colours)
+    ]
+    grad_down = down_grad(net, cotangent_both.T, hidden, colours)
     fold_down = [Fold(net, g, order) for g, (_, _, order) in zip(grad_down, colours)]
+    launch_all(fold_down)
     down_half = assemble(
         net, down_pieces, width, pair_index, units // 4, 4, lambda i, p: i
     )
-    output_both = contract(hidden, down_half, 1, 0)
-    output = (mixed + output_both[:rows] + net.flip(output_both[rows:], 1)).astype(BF16)
     d_hidden = contract(after(cotangent_both, grad_down), down_half, 1, 1)
     d_gate = (d_hidden * up_pre * sigmoid_gate * (1.0 + gate_pre * (1.0 - sigmoid_gate))).astype(
         BF16
     )
     d_up = (d_hidden * silu_gate).astype(BF16)
     normed_both_t = normed_both.T
+
+    def sum_pairs(grad):
+        return lax.psum_scatter(
+            grad, "rep", scatter_dimension=0, tiled=True, axis_index_groups=net.same_half
+        )[0]
+
+    d_gate, d_up = after((d_gate, d_up), got_of(fold_down))
     for fold in fold_down:
-        fold.step()
-    grad_gate = weight_grad(net, normed_both_t, d_gate, [(0, units, order_a)], False)
-    grad_up = weight_grad(net, normed_both_t, d_up, [(0, units, order_b)], False)
-    fold_units = [Fold(net, grad_gate[0], order_a), Fold(net, grad_up[0], order_b)]
-    d_gate, d_up = after((d_gate, d_up), grad_gate, grad_up, *[f.state() for f in fold_down])
+        fold.until_last()
+    grad_gate = unit_grad(net, normed_both_t, d_gate)
+    gate_sum = sum_pairs(grad_gate)
+    d_gate, d_up = after((d_gate, d_up), grad_gate, got_of(fold_down))
+    collect_all(fold_down)
+    first = [f.keep[0, :shard_units] for f in fold_down]
+    second = [f.keep[0, shard_units:] for f in fold_down]
+    mine = [jnp.where(even, u, v) for u, v in zip(first, second)]
+    got = [net.flip_seq(jnp.where(even, v, u), 1) for u, v in zip(first, second)]
+    grad_up = unit_grad(net, normed_both_t, d_up)
+    up_sum = sum_pairs(grad_up)
+    d_gate, d_up = after((d_gate, d_up), grad_up, got)
+    total = lambda own, other: (own.astype(F32) + other.astype(F32)).astype(BF16)
+    mine = [total(u, v) for u, v in zip(mine, got)]
+
+    def start_seq(folds):
+        collect_all(folds)
+        both = [f.keep[0].reshape(seqs, -1, f.keep.shape[-1]) for f in folds]
+        both = jnp.concatenate(both, axis=1)
+        far = net.seq >= seqs // 2
+        upper, lower = both[seqs // 2 :], both[: seqs // 2]
+        return (
+            jnp.where(far, upper, lower),
+            net.flip_seq(jnp.where(far, lower, upper), seqs // 2),
+        )
+
+    def next_seq(own, got):
+        sums = total(own, got)
+        return (
+            jnp.where(even, sums[0], sums[1]),
+            net.flip_seq(jnp.where(even, sums[1], sums[0]), 1),
+        )
+
+    def settle_units(piece, order):
+        pieces = net.spread(piece, order)
+        return [v for m in range(net.pairs) for v in (pieces[m], net.flip(pieces[m], 1))]
+
     d_normed_both = contract(d_gate, gate_half, 1, 1) + contract(d_up, up_half, 1, 1)
     d_normed_two = d_normed_both[:rows] + net.flip(d_normed_both[rows:], 1)
     grad_gain_two = jnp.sum(d_normed_two * unit_two, axis=0)
     d_mixed = cotangent.astype(F32) + norm_back(d_normed_two * gain_two, unit_two, scale_two, 1)
 
-    for fold in fold_down:
-        fold.rest()
-    d_mixed = after(d_mixed, *[f.keep for f in fold_down])
-    for fold in fold_units:
-        fold.step()
-    piece = jnp.concatenate([f.keep[0] for f in fold_down], axis=0).T
-    span = piece.shape[0] // 2
-    first, second = piece[:span], piece[span:]
-    mine = jnp.where(even, first, second)
-    mine = mine.astype(F32) + net.flip_seq(jnp.where(even, second, first), 1).astype(F32)
-    mine = (mine + net.flip_seq(mine.astype(BF16), seqs // 2).astype(F32)).astype(BF16)
-    mine = jnp.where(own_half, mine, net.flip(mine, 1))
-
     d_branch = d_mixed.astype(BF16)
     d_attended_t = contract(out_full, d_branch, 1, 1).astype(BF16)
     d_query_t, d_key_t, d_value_t = attend_backward(
         queries_t, d_attended_t.reshape(H, HD, rows), kv[:KVH], kv_t[:KVH], kv[KVH:], runs
     )
-    d_key_t, d_value_t = after((d_key_t, d_value_t), *[f.state() for f in fold_units])
+    d_key_t, d_value_t = after((d_key_t, d_value_t), gate_sum)
     d_kv = jnp.concatenate(
         [d_key_t.reshape(kv_width, -1), d_value_t.reshape(kv_width, -1)], axis=0
     )
@@ -644,12 +762,24 @@
     d_kv_own = d_kv[:, lead:]
     need = lead
     step = 1
+    backs = []
     while need > 0:
         take = min(need, rows)
-        back = net.slide(d_kv[:, need - take : need].astype(BF16), -step).astype(F32)
-        d_kv_own = d_kv_own + jnp.pad(back, ((0, 0), (rows - take, 0)))
+        backs.append(d_kv[:, need - take : need].astype(BF16))
         need -= take
-        step += 1
+    backs = lax.optimization_barrier(backs)
+    backs = [net.slide(v, -step - 1) for step, v in enumerate(backs)]
+    d_kv_own = after(d_kv_own, backs)
+    for back in backs:
+        take = back.shape[1]
+        d_kv_own = d_kv_own + jnp.pad(back.astype(F32), ((0, 0), (rows - take, 0)))
+    sum_seq = lambda v: lax.psum_scatter(v, "seq", scatter_dimension=0, tiled=True)
+    gate_sum, up_sum = sum_seq(gate_sum), sum_seq(up_sum)
+    mine = after(mine, d_kv_own)
+    mine = [total(v, net.flip_seq(v, seqs // 2)) for v in mine]
+    mine = [jnp.where(own_half, v, net.flip(v, 1)) for v in mine]
+    output_both = contract(after(hidden, d_kv_own), down_half, 1, 0)
+    output = (mixed + output_both[:rows] + net.flip(output_both[rows:], 1)).astype(BF16)
     d_query_pre_t = rotate(d_query_t * factor, cosine, -sine).reshape(query_width, rows)
     d_key_pre_t = rotate(d_kv_own[:kv_width].reshape(KVH, HD, rows), cosine, -sine)
     d_proj_t = jnp.concatenate(
@@ -663,30 +793,32 @@
         BF16
     )
 
-    both = jnp.concatenate(
-        [f.rest().reshape(seqs, shard, unit_width) for f in fold_units], axis=1
-    ).reshape(-1, unit_width)
-    both = lax.psum_scatter(both, "seq", scatter_dimension=0, tiled=True)
-    both = lax.all_gather(both, "rep", axis=0)
-    moves = [
-        (2 * k + h, 0, unit_width, h * units + min(k * unit_width, units - unit_width))
-        for k in range(net.pairs)
-        for h in range(2)
-    ]
-    sum_gate = widen(both, 2 * units, moves, 0, shard)
-    sum_up = widen(both, 2 * units, moves, shard, shard)
-    mine = lax.all_gather(mine, "rep", axis=0, axis_index_groups=net.same_half)
-    moves, at = [], 0
-    for start, span, _ in colours:
-        w = cut_width(span, net.pairs)
-        moves += [(k, at, w, start + min(k * w, span - w)) for k in range(net.pairs)]
-        at += w
-    sum_down = widen(mine, width, moves, 0, mine.shape[1])
-
-    grad_qkv = contract(normed_one, d_proj, 0, 0)
-    grad_out = contract(attended_t, d_branch, 1, 0)
-    grad_attn = jnp.concatenate([grad_qkv, grad_out], axis=1).astype(BF16)
-    grad_attn = grad_attn.reshape(seqs, shard, attn_columns)
+    gate_sums = settle_units(gate_sum, order_a)
+    up_sums = settle_units(up_sum, order_b)
+    down_sums = [net.spread(v, order) for v, (_, _, order) in zip(mine, colours)]
+
+    def join_units(sums):
+        regions = [
+            (lambda place, h=h: ((place[0] + h) % 2) * units, units, net.pairs, sums[h::2])
+            for h in range(2)
+        ]
+        return assemble(
+            net, regions, 2 * units, pair_index, shard // 4, 4, lambda i, p: i, dtype=F32
+        )
+
+    sum_gate = join_units(gate_sums)
+    sum_up = join_units(up_sums)
+    sum_down = assemble(
+        net,
+        [(start, span, net.pairs, v) for v, (start, span, _) in zip(down_sums, colours)],
+        width,
+        pair_index,
+        shard_units // 4,
+        4,
+        lambda i, p: i,
+        dtype=F32,
+    )
+
     pieces_of = lambda v: v.reshape(seqs, -1)
     small = jnp.concatenate(
         [
@@ -698,31 +830,32 @@
         ],
         axis=1,
     ).astype(BF16)
-    pad = 32
+    pad = pl.cdiv(shard + 1, 64) * 64 - shard
     small = jnp.pad(small, ((0, 0), (0, attn_columns - small.shape[1])))[:, None]
     small = jnp.pad(small, ((0, 0), (0, pad - 1), (0, 0)))
-    grad_attn = jnp.concatenate([grad_attn, small], axis=1).reshape(-1, attn_columns)
-    if attn_columns % (net.reps * LANES) == 0:
-        stack = jnp.transpose(
-            grad_attn.reshape(-1, net.reps, attn_width), (1, 0, 2)
+    attn_orders = [(1,) + tuple(2 * b for b in order) for order in net.orders]
+    folds = [
+        Fold(net, parts, order, 1)
+        for parts, order in zip(
+            attn_grad(net, normed_one.T, d_proj, attended_t, d_branch, small, attn_orders),
+            attn_orders,
         )
-    else:
-        stack = jnp.stack(
-            [
-                grad_attn[:, o : o + attn_width]
-                for o in (
-                    min(k * attn_width, attn_columns - attn_width) for k in range(net.reps)
-                )
-            ]
-        )
-    stack = lax.psum_scatter(stack, "rep", scatter_dimension=0, tiled=True)[0]
-    stack = lax.psum_scatter(stack, "seq", scatter_dimension=0, tiled=True)
-    stack = lax.all_gather(stack, "rep", axis=0)
-    moves = [
-        (k, 0, attn_width, min(k * attn_width, attn_columns - attn_width))
-        for k in range(net.reps)
     ]
-    sum_attn = widen(stack, attn_columns, moves, 0, stack.shape[1])
+    launch_all(folds)
+    for fold in folds:
+        fold.until_last()
+    attn_own, attn_got = next_seq(*start_seq(folds))
+    attn_sums = settle_units(total(attn_own, attn_got), order_b)
+    sum_attn = assemble(
+        net,
+        [(0, attn_columns, net.reps, attn_sums)],
+        attn_columns,
+        lambda place: place[0],
+        (shard + pad) // 4,
+        4,
+        lambda i, p: i,
+        dtype=F32,
+    )
     row = sum_attn[shard]
     sum_gain_one, sum_query_bias, sum_key_bias, sum_value_bias, sum_gain_two = [
         row[e - s : e] for s, e in zip(sizes, ends)

time: 769 us -> 560 us (0.73)
  waiting for transfers between devices: 350 us -> 147 us
  local copies, waits for them, and re-layouts: 76.7 us -> 51.4 us
  Pallas kernels: 110 us -> 119 us
    all_gather x3 -> x0, waiting for transfers between devices: 79.8 us -> none  [the longest x1 29.6 us: on_device(): mine = lax.all_gather(mine, 'rep', axis=0, axis_index_groups=net.same_half)]
    reduce_scatter x3 -> x2, waiting for transfers between devices: 49.9 us -> 0.01 us  [on_device(): lax.psum_scatter(v, 'seq', scatter_dimension=0, tiled=True)]
    ppermute x4 -> x10, waiting for transfers between devices: 84.8 us -> 50.7 us  [flip_seq(): return lax.ppermute(value, 'seq', [(i, i ^ bit) for i in range(self.seqs)])]
    ppermute x11 -> x0, local copies, waits for them, and re-layouts: 22.1 us -> none  [the longest x7 14.3 us: flip(): return lax.ppermute(value, 'rep', [(i, i ^ bit) for i in range(self.reps)])]
    all_gather x1, waiting for transfers between devices: 20.4 us -> 0.01 us  [gather_seq(): return lax.all_gather(value, 'seq', axis=0, tiled=True)]
    pallas_call x5 -> x9, Pallas kernels: 24.6 us -> 44 us  [assemble(): pl.pallas_call(body, name='assemble', out_shape=jax.ShapeDtypeStruct((row...]
    ppermute x4, waiting for transfers between devices: 32.5 us -> 15.3 us  [slide(): return lax.ppermute(value, 'seq', pairs)]
    ppermute x39 -> x69, starting transfers between devices: 32.7 us -> 46.2 us  [flip(): return lax.ppermute(value, 'rep', [(i, i ^ bit) for i in range(self.reps)])]
  transfers between devices with their start and end apart: 54 -> 88, of which waited for: 19 -> 28; matrix products, arithmetic and copies ran while one was open for 24% -> 32% of each run, Pallas kernels for 13% -> 19%
where the time goes in v2:
time: 560 us; the launch traced here: 552 us
  waiting for transfers between devices  147 us (26%)
  Pallas kernels  119 us (21%)
  matrix products  72.3 us (13%)
  starting transfers between devices  64.7 us (12%)
  other arithmetic  62 us (11%)
  local copies, waits for them, and re-layouts  51.4 us (9%)
  blocking collectives  19.6 us (4%)
  between operations  15.3 us (3%)
    ppermute x69, waiting for transfers between devices, flip(): return lax.ppermute(value, 'rep', [(i, i ^ bit) for i in range(self.reps)])  80.7 us
    dot_general x10, matrix products, contract(): lax.dot_general(left, right, (((left_dim,), (right_dim,)), ((), ())), pre...  72.3 us
    ppermute x10, waiting for transfers between devices, flip_seq(): return lax.ppermute(value, 'seq', [(i, i ^ bit) for i in range(self.seqs)])  50.7 us
    ppermute x69, starting transfers between devices, flip(): return lax.ppermute(value, 'rep', [(i, i ^ bit) for i in range(self.reps)])  46.2 us
    pallas_call x9, Pallas kernels, assemble(): pl.pallas_call(body, name='assemble', out_shape=jax.ShapeDtypeStruct((row...  44 us
    pallas_call x2, Pallas kernels, unit_grad(): pl.pallas_call(body, name='unit_grad', out_shape=jax.ShapeDtypeStruct((ne...  21.3 us
    pallas_call x1, Pallas kernels, attend_backward(): pl.pallas_call(body, name='attend_backward', out_shape=(jax.ShapeDtypeStr...  20.8 us
    all_gather x1, blocking collectives, gather_seq(): return lax.all_gather(value, 'seq', axis=0, tiled=True)  19.6 us
  transfers between devices with their start and end apart: 88, of which 28 were waited for; matrix products, arithmetic and copies ran while one was open for 32% of the time, Pallas kernels for 19%

profile of v2, /device:TPU:0, one launch (start us, length us, event | category | flops | bytes accessed | tf_op | source)
XLA Modules:
  0.0 551.6 jit_solution(7299861814853670397)
XLA Ops:
  10.2 19.6 %all_gather.6 = bf16[928,256]{1,0:T(8,128)(2,1)S(1)} all-gather(bf16[232,256]{1,0:T(8,128)(2,1)S(1)} %pad_maximum_fusion.13), channel_id=1, replica_groups=mesh['rep'=8,'seq'=4] {'seq'}, dimensions={0}, use_global_device_ids=true | all-gather | bytes 593920 | tf_op jit(solution)/shard_map/all_gather | solution.py:51
  88.5 11.9 %collective-permute-done.16.refs_1_ = bf16[672,640]{1,0:T(8,128)(2,1)} collective-permute-done((bf16[672,640]{1,0:T(8,128)(2,1)}, bf16[672,640]{1,0:T(8,128)(2,1)}, u32[]{:S(2)}, u32[]{:S(2)}) %collective-permute-start.16) | collective-permute-done | bytes 860192 | tf_op jit(solution)/shard_map/ppermute | solution.py:41
  109.9 12.1 %attend_forward.1 = bf16[14,64,512]{2,1,0:T(8,128)(2,1)} custom-call(s32[2]{0:T(128)} %slice.302.runs_ref, bf16[14,64,512]{2,1,0:T(8,128)(2,1)} %multiply_convert_fusion.4.q_ref, bf16[2,1280,64]{2,1,0:T(8,128)(2,1)} %get-tuple-element.114.k_ref, bf16[2,64,1280]{2,1,0:T(8,128)(2,1)} %get-tuple-element.119.v_ref), custom_call_target="tpu_custom_call" | custom-call | flops 18790481920 | bytes 3670016 | tf_op jit(solution)/shard_map/attend_forward/pallas_call | solution.py:370
  125.6 6.0 %collective-permute-done.19 = bf16[1216,128]{1,0:T(8,128)(2,1)S(1)} collective-permute-done((bf16[1216,128]{1,0:T(8,128)(2,1)S(1)}, bf16[1216,128]{1,0:T(8,128)(2,1)S(1)}, u32[]{:S(2)}, u32[]{:S(2)}) %collective-permute-start.19) | collective-permute-done | bytes 311328 | tf_op jit(solution)/shard_map/ppermute | solution.py:44
  141.1 8.2 %collective-permute-done.24 = bf16[1216,128]{1,0:T(8,128)(2,1)S(1)} collective-permute-done((bf16[1216,128]{1,0:T(8,128)(2,1)S(1)}, bf16[1216,128]{1,0:T(8,128)(2,1)S(1)}, u32[]{:S(2)}, u32[]{:S(2)}) %collective-permute-start.24) | collective-permute-done | bytes 311328 | tf_op jit(solution)/shard_map/ppermute | solution.py:44
  151.6 5.9 %assemble.12 = bf16[896,2432]{1,0:T(8,128)(2,1)} custom-call(s32[2]{0:T(128)} %pad_add_fusion.place, bf16[672,640]{1,0:T(8,128)(2,1)} %bitcast.11.refs_0_, bf16[672,640]{1,0:T(8,128)(2,1)} %collective-permute-done.25.refs_1_, bf16[672,640]{1,0:T(8,128)(2,1)} %collective-permute-done.17.refs_2_, bf16[672,640]{1,0:T(8,128)(2,1)} %collective-permute-done.26.refs_3_, ...), custom_call_target="tpu_custom_call" | custom-call | bytes 8716288 | tf_op jit(solution)/shard_map/assemble/pallas_call | solution.py:158
  160.4 5.9 %assemble.11 = bf16[896,2432]{1,0:T(8,128)(2,1)} custom-call(s32[2]{0:T(128)} %pad_add_fusion.place, bf16[672,640]{1,0:T(8,128)(2,1)} %bitcast.10.refs_0_, bf16[672,640]{1,0:T(8,128)(2,1)} %collective-permute-done.16.refs_1_, bf16[672,640]{1,0:T(8,128)(2,1)} %collective-permute-done.21.refs_2_, bf16[672,640]{1,0:T(8,128)(2,1)} %collective-permute-done.22.refs_3_, ...), custom_call_target="tpu_custom_call" | custom-call | bytes 8716288 | tf_op jit(solution)/shard_map/assemble/pallas_call | solution.py:158
  169.2 7.3 %fusion.41 = f32[1024,2432]{1,0:T(8,128)S(1)} fusion(bf16[896,2432]{1,0:T(8,128)(2,1)S(1)} %copy-done.6, bf16[512,896]{1,0:T(8,128)(2,1)} %collective-permute-done.20, bf16[512,896]{1,0:T(8,128)(2,1)S(1)} %multiply_convert_fusion.3), kind=kOutput, calls=%fused_computation.150 | convolution fusion | flops 4466409472 | bytes 16154624 | tf_op jit(solution)/shard_map/dot_general | solution.py:479
  181.6 9.4 %multiply_convert_fusion.2 = (bf16[1024,2432]{1,0:T(8,128)(2,1)}, f32[1024,2432]{1,0:T(8,128)}) fusion(f32[1024,2432]{1,0:T(8,128)S(1)} %fusion.41, bf16[1024,896]{1,0:T(8,128)(2,1)S(1)} %get-tuple-element.52, bf16[896,2432]{1,0:T(8,128)(2,1)S(1)} %bitcast.84), kind=kOutput, calls=%fused_computation.2 | convolution fusion | flops 4477681664 | bytes 31096832 | tf_op jit(solution)/shard_map/dot_general | solution.py:479
  194.9 12.2 %down_grad.1 = (bf16[2,2432,128]{2,1,0:T(8,128)(2,1)}, bf16[2,2432,128]{2,1,0:T(8,128)(2,1)}, bf16[2,2432,128]{2,1,0:T(8,128)(2,1)}, bf16[2,2432,128]{2,1,0:T(8,128)(2,1)}) custom-call(s32[2]{0:T(128)} %pad_add_fusion.place, bf16[896,1024]{1,0:T(8,128)(2,1)} %get-tuple-element.109.left_ref, bf16[1024,2432]{1,0:T(8,128)(2,1)} %get-tuple-element.72.right_ref), custom_call_target="tpu_custom_call" | custom-call | flops 4462739456 | bytes 11173888 | tf_op jit(solution)/shard_map/down_grad/pallas_call | solution.py:198
  209.8 6.0 %assemble.13 = bf16[2432,896]{1,0:T(8,128)(2,1)} custom-call(s32[2]{0:T(128)} %pad_add_fusion.place, bf16[2432,128]{1,0:T(8,128)(2,1)} %copy-done.12, bf16[2432,128]{1,0:T(8,128)(2,1)} %collective-permute-done.27.refs_1_, bf16[2432,128]{1,0:T(8,128)(2,1)} %collective-permute-done.30.refs_2_, bf16[2432,128]{1,0:T(8,128)(2,1)} %collective-permute-done.31.refs_3_, ...), custom_call_target="tpu_custom_call" | custom-call | bytes 8716288 | tf_op jit(solution)/shard_map/assemble/pallas_call | solution.py:158
  215.8 16.2 %multiply_convert_fusion = (bf16[1024,2432]{1,0:T(8,128)(2,1)}, bf16[1024,2432]{1,0:T(8,128)(2,1)}) fusion(f32[1024,2432]{1,0:T(8,128)} %copy-done.76, f32[1024,2432]{1,0:T(8,128)} %get-tuple-element.143, bf16[1024,896]{0,1:T(8,128)(2,1)} %get-tuple-element.58, bf16[2432,896]{1,0:T(8,128)(2,1)} %assemble.13), kind=kOutput, calls=%fused_computation | convolution fusion | flops 4495114240 | bytes 36077568 | tf_op jit(solution)/shard_map/dot_general | solution.py:479
  235.8 10.4 %unit_grad.2 = bf16[4,896,640]{2,1,0:T(8,128)(2,1)} custom-call(bf16[896,1024]{1,0:T(8,128)(2,1)} %copy.67.left_ref, bf16[1024,2432]{1,0:T(8,128)(2,1)} %get-tuple-element.63.right_ref), custom_call_target="tpu_custom_call" | custom-call | flops 4462739456 | bytes 11173888 | tf_op jit(solution)/shard_map/unit_grad/pallas_call | solution.py:232
  252.1 21.4 %collective-permute-done.36 = bf16[1,2432,128]{2,1,0:T(8,128)(2,1)S(1)} collective-permute-done((bf16[1,2432,128]{2,1,0:T(8,128)(2,1)S(1)}, bf16[1,2432,128]{2,1,0:T(8,128)(2,1)S(1)}, u32[]{:S(2)}, u32[]{:S(2)}) %collective-permute-start.36) | collective-permute-done | bytes 622624 | tf_op jit(solution)/shard_map/ppermute | solution.py:41
  280.3 10.9 %unit_grad.3 = bf16[4,896,640]{2,1,0:T(8,128)(2,1)} custom-call(bf16[896,1024]{1,0:T(8,128)(2,1)} %copy.67.left_ref, bf16[1024,2432]{1,0:T(8,128)(2,1)} %get-tuple-element.64.right_ref), custom_call_target="tpu_custom_call" | custom-call | flops 4462739456 | bytes 11173888 | tf_op jit(solution)/shard_map/unit_grad/pallas_call | solution.py:232
  291.3 9.6 %fusion.53 = f32[1024,896]{1,0:T(8,128)S(1)} fusion(bf16[1024,2432]{1,0:T(8,128)(2,1)} %get-tuple-element.64.right_ref, bf16[896,2432]{1,0:T(8,128)(2,1)} %assemble.12), kind=kOutput, calls=%fused_computation.162 | convolution fusion | flops 4462739456 | bytes 13008896 | tf_op jit(solution)/shard_map/dot_general | solution.py:479
  300.8 8.9 %convolution_add_fusion.1 = f32[1024,896]{1,0:T(8,128)S(1)} fusion(f32[1024,896]{1,0:T(8,128)S(1)} %fusion.53, bf16[1024,2432]{1,0:T(8,128)(2,1)} %get-tuple-element.63.right_ref, bf16[896,2432]{1,0:T(8,128)(2,1)} %assemble.11), kind=kOutput, calls=%fused_computation.38 | convolution fusion | flops 4463656960 | bytes 16678912 | tf_op jit(solution)/shard_map/dot_general | solution.py:479
  326.2 20.8 %attend_backward.1 = (f32[14,64,512]{2,1,0:T(8,128)}, f32[2,64,1280]{2,1,0:T(8,128)}, f32[2,64,1280]{2,1,0:T(8,128)}) custom-call(s32[2]{0:T(128)} %slice.302.runs_ref, bf16[14,64,512]{2,1,0:T(8,128)(2,1)} %multiply_convert_fusion.4.q_ref, bf16[14,64,512]{2,1,0:T(8,128)(2,1)} %bitcast.114, bf16[2,1280,64]{2,1,0:T(8,128)(2,1)} %get-tuple-element.114.k_ref, ...), custom_call_target="tpu_custom_call" | custom-call | flops 37580963840 | bytes 3670016 | tf_op jit(solution)/shard_map/attend_backward/pallas_call | solution.py:442
  359.6 15.3 %collective-permute-done.42 = bf16[256,256]{0,1:T(8,128)(2,1)} collective-permute-done((bf16[256,256]{0,1:T(8,128)(2,1)}, bf16[256,256]{0,1:T(8,128)(2,1)}, u32[]{:S(2)}, u32[]{:S(2)}) %collective-permute-start.42) | collective-permute-done | bytes 131104 | tf_op jit(solution)/shard_map/ppermute | solution.py:48
  391.0 9.2 %attn_grad.1 = (bf16[4,4,128,256]{3,2,1,0:T(8,128)(2,1)}, bf16[4,4,128,256]{3,2,1,0:T(8,128)(2,1)}, bf16[4,4,128,256]{3,2,1,0:T(8,128)(2,1)}, bf16[4,4,128,256]{3,2,1,0:T(8,128)(2,1)}) custom-call(s32[2]{0:T(128)} %pad_add_fusion.place, bf16[896,512]{1,0:T(8,128)(2,1)} %copy.75.a_ref, bf16[512,1152]{1,0:T(8,128)(2,1)} %get-tuple-element.116.b_ref, ...), custom_call_target="tpu_custom_call" | custom-call | flops 1879048192 | bytes 7864320 | tf_op jit(solution)/shard_map/attn_grad/pallas_call | solution.py:316
  400.8 8.7 %fusion.54 = f32[1024,896]{1,0:T(8,128)S(1)} fusion(bf16[1024,2432]{1,0:T(8,128)(2,1)} %get-tuple-element.72.right_ref, bf16[2432,896]{1,0:T(8,128)(2,1)} %assemble.13), kind=kOutput, calls=%fused_computation.163 | convolution fusion | flops 4462739456 | bytes 13008896 | tf_op jit(solution)/shard_map/dot_general | solution.py:479
  413.8 7.5 %collective-permute-done.73 = bf16[1216,128]{1,0:T(8,128)(2,1)S(1)} collective-permute-done((bf16[1216,128]{1,0:T(8,128)(2,1)S(1)}, bf16[1216,128]{1,0:T(8,128)(2,1)S(1)}, u32[]{:S(2)}, u32[]{:S(2)}) %collective-permute-start.73) | collective-permute-done | bytes 311328 | tf_op jit(solution)/shard_map/ppermute | solution.py:44
  430.0 7.9 %collective-permute-done.45 = bf16[2,4,128,256]{3,2,1,0:T(8,128)(2,1)} collective-permute-done((bf16[2,4,128,256]{3,2,1,0:T(8,128)(2,1)}, bf16[2,4,128,256]{3,2,1,0:T(8,128)(2,1)}, u32[]{:S(2)}, u32[]{:S(2)}) %collective-permute-start.45) | collective-permute-done | bytes 524320 | tf_op jit(solution)/shard_map/ppermute | solution.py:41
  453.9 18.4 %collective-permute-done.50 = bf16[2,256,256]{2,1,0:T(8,128)(2,1)S(1)} collective-permute-done((bf16[2,256,256]{2,1,0:T(8,128)(2,1)S(1)}, bf16[2,256,256]{2,1,0:T(8,128)(2,1)S(1)}, u32[]{:S(2)}, u32[]{:S(2)}) %collective-permute-start.50) | collective-permute-done | bytes 262176 | tf_op jit(solution)/shard_map/ppermute | solution.py:44
  (463 shorter events, 266.9 us)
Async XLA Ops:
  7.3 67.3 %all-gather.2.cloned.1.call-start = ((), (), s32[]{:S(2)}) async-start(), calls=%async_computation.4 | async-start | bytes 2867200 | tf_op jit(solution)/shard_map/all_gather | solution.py:51
  9.7 340.3 %reduce-scatter.13.cloned.1.call-start = ((), (), s32[]{:S(2)}) async-start(), calls=%async_computation.7 | async-start | bytes 5734400
  52.6 29.0 %collective-permute-start.29 = (bf16[512,896]{0,1:T(8,128)(2,1)}, bf16[512,896]{0,1:T(8,128)(2,1)}, u32[]{:S(2)}, u32[]{:S(2)}) collective-permute-start(bf16[512,896]{0,1:T(8,128)(2,1)} %copy.66), channel_id=1, source_target_pairs={{0,4},{4,0},{8,12},{12,8},{16,20},{20,16},{24,28},{28,24},{1,5},{5... | collective-permute-start | bytes 2752520 | tf_op jit(solution)/shard_map/ppermute | solution.py:41
  86.5 71.1 %collective-permute-start.21 = (bf16[672,640]{1,0:T(8,128)(2,1)}, bf16[672,640]{1,0:T(8,128)(2,1)}, u32[]{:S(2)}, u32[]{:S(2)}) collective-permute-start(bf16[672,640]{1,0:T(8,128)(2,1)} %bitcast.10.refs_0_), channel_id=1, source_target_pairs={{0,16},{4,20},{8,24},{12,28},{16,0},{20,4},{24,8},{28,12},{1,17},{... | collective-permute-start | bytes 2580488 | tf_op jit(solution)/shard_map/ppermute | solution.py:41
  88.0 62.5 %collective-permute-start.25 = (bf16[672,640]{1,0:T(8,128)(2,1)}, bf16[672,640]{1,0:T(8,128)(2,1)}, u32[]{:S(2)}, u32[]{:S(2)}) collective-permute-start(bf16[672,640]{1,0:T(8,128)(2,1)} %bitcast.11.refs_0_), channel_id=1, source_target_pairs={{0,8},{4,12},{8,0},{12,4},{16,24},{20,28},{24,16},{28,20},{1,9},{5... | collective-permute-start | bytes 2580488 | tf_op jit(solution)/shard_map/ppermute | solution.py:41
  104.6 26.9 %collective-permute-start.19 = (bf16[1216,128]{1,0:T(8,128)(2,1)S(1)}, bf16[1216,128]{1,0:T(8,128)(2,1)S(1)}, u32[]{:S(2)}, u32[]{:S(2)}) collective-permute-start(bf16[1216,128]{1,0:T(8,128)(2,1)S(1)} %get-tuple-element.50), channel_id=1, source_target_pairs={{0,2},{1,3},{2,0},{3,1},{4,6},{5,7},{6,4},{7,5},{8,10},{9,11},{10,... | collective-permute-start | bytes 933896 | tf_op jit(solution)/shard_map/ppermute | solution.py:44
  122.1 36.9 %collective-permute-start.22 = (bf16[672,640]{1,0:T(8,128)(2,1)}, bf16[672,640]{1,0:T(8,128)(2,1)}, u32[]{:S(2)}, u32[]{:S(2)}) collective-permute-start(bf16[672,640]{1,0:T(8,128)(2,1)} %collective-permute-done.16.refs_1_), channel_id=1, source_target_pairs={{0,16},{4,20},{8,24},{12,28},{16,0},{20,4},{24,8},{28,12},{1,17},{... | collective-permute-start | bytes 2580488 | tf_op jit(solution)/shard_map/ppermute | solution.py:41
  125.0 26.1 %collective-permute-start.26 = (bf16[672,640]{1,0:T(8,128)(2,1)}, bf16[672,640]{1,0:T(8,128)(2,1)}, u32[]{:S(2)}, u32[]{:S(2)}) collective-permute-start(bf16[672,640]{1,0:T(8,128)(2,1)} %collective-permute-done.17.refs_2_), channel_id=1, source_target_pairs={{0,8},{4,12},{8,0},{12,4},{16,24},{20,28},{24,16},{28,20},{1,9},{5... | collective-permute-start | bytes 2580488 | tf_op jit(solution)/shard_map/ppermute | solution.py:41
  150.4 57.1 %collective-permute-start.32 = (bf16[2432,128]{1,0:T(8,128)(2,1)}, bf16[2432,128]{1,0:T(8,128)(2,1)}, u32[]{:S(2)}, u32[]{:S(2)}) collective-permute-start(bf16[2432,128]{1,0:T(8,128)(2,1)} %pad_maximum_fusion.7.refs_4_), channel_id=1, source_target_pairs={{0,8},{4,12},{8,0},{12,4},{16,24},{20,28},{24,16},{28,20},{1,9},{5... | collective-permute-start | bytes 1867784 | tf_op jit(solution)/shard_map/ppermute | solution.py:41
  151.0 25.4 %collective-permute-start.28 = (bf16[2432,128]{1,0:T(8,128)(2,1)}, bf16[2432,128]{1,0:T(8,128)(2,1)}, u32[]{:S(2)}, u32[]{:S(2)}) collective-permute-start(bf16[2432,128]{1,0:T(8,128)(2,1)} %pad_maximum_fusion.7.refs_4_), channel_id=1, source_target_pairs={{0,16},{4,20},{8,24},{12,28},{16,0},{20,4},{24,8},{28,12},{1,17},{... | collective-permute-start | bytes 1867784 | tf_op jit(solution)/shard_map/ppermute | solution.py:41
  157.5 51.4 %collective-permute-start.30 = (bf16[2432,128]{1,0:T(8,128)(2,1)S(1)}, bf16[2432,128]{1,0:T(8,128)(2,1)}, u32[]{:S(2)}, u32[]{:S(2)}) collective-permute-start(bf16[2432,128]{1,0:T(8,128)(2,1)S(1)} %pad_maximum_fusion.6.refs_0_), channel_id=1, source_target_pairs={{0,16},{4,20},{8,24},{12,28},{16,0},{20,4},{24,8},{28,12},{1,17},{... | collective-permute-start | bytes 1867784 | tf_op jit(solution)/shard_map/ppermute | solution.py:41
  176.5 32.5 %collective-permute-start.33 = (bf16[2432,128]{1,0:T(8,128)(2,1)}, bf16[2432,128]{1,0:T(8,128)(2,1)S(1)}, u32[]{:S(2)}, u32[]{:S(2)}) collective-permute-start(bf16[2432,128]{1,0:T(8,128)(2,1)} %collective-permute-done.28.refs_6_), channel_id=1, source_target_pairs={{0,8},{4,12},{8,0},{12,4},{16,24},{20,28},{24,16},{28,20},{1,9},{5... | collective-permute-start | bytes 1867784 | tf_op jit(solution)/shard_map/ppermute | solution.py:41
  181.0 28.0 %collective-permute-start.31 = (bf16[2432,128]{1,0:T(8,128)(2,1)}, bf16[2432,128]{1,0:T(8,128)(2,1)}, u32[]{:S(2)}, u32[]{:S(2)}) collective-permute-start(bf16[2432,128]{1,0:T(8,128)(2,1)} %collective-permute-done.27.refs_1_), channel_id=1, source_target_pairs={{0,16},{4,20},{8,24},{12,28},{16,0},{20,4},{24,8},{28,12},{1,17},{... | collective-permute-start | bytes 1867784 | tf_op jit(solution)/shard_map/ppermute | solution.py:41
  207.0 28.5 %collective-permute-start.34 = (bf16[2,2432,128]{2,1,0:T(8,128)(2,1)}, bf16[2,2432,128]{2,1,0:T(8,128)(2,1)}, u32[]{:S(2)}, u32[]{:S(2)}) collective-permute-start(bf16[2,2432,128]{2,1,0:T(8,128)(2,1)} %get-tuple-element.55), channel_id=1, source_target_pairs={{0,8},{4,12},{8,0},{12,4},{16,24},{20,28},{24,16},{28,20},{1,9},{5... | collective-permute-start | bytes 3735560 | tf_op jit(solution)/shard_map/ppermute | solution.py:41
  207.6 28.2 %collective-permute-start.35 = (bf16[2,2432,128]{2,1,0:T(8,128)(2,1)}, bf16[2,2432,128]{2,1,0:T(8,128)(2,1)}, u32[]{:S(2)}, u32[]{:S(2)}) collective-permute-start(bf16[2,2432,128]{2,1,0:T(8,128)(2,1)} %get-tuple-element.57), channel_id=1, source_target_pairs={{0,16},{4,20},{8,24},{12,28},{16,0},{20,4},{24,8},{28,12},{1,17},{... | collective-permute-start | bytes 3735560 | tf_op jit(solution)/shard_map/ppermute | solution.py:41
  246.2 183.8 %reduce-scatter.15.cloned.1.call-start = ((), (), s32[]{:S(2)}) async-start(), calls=%async_computation.8 | async-start | bytes 5734400
  247.9 25.6 %collective-permute-start.36 = (bf16[1,2432,128]{2,1,0:T(8,128)(2,1)S(1)}, bf16[1,2432,128]{2,1,0:T(8,128)(2,1)S(1)}, u32[]{:S(2)}, u32[]{:S(2)}) collective-permute-start(bf16[1,2432,128]{2,1,0:T(8,128)(2,1)S(1)} %add_convert_fusion.5), channel_id=1, source_target_pairs={{0,16},{4,20},{8,24},{12,28},{16,0},{20,4},{24,8},{28,12},{1,17},{... | collective-permute-start | bytes 1867784 | tf_op jit(solution)/shard_map/ppermute | solution.py:41
  250.6 27.6 %collective-permute-start.37 = (bf16[1,2432,128]{2,1,0:T(8,128)(2,1)S(1)}, bf16[1,2432,128]{2,1,0:T(8,128)(2,1)S(1)}, u32[]{:S(2)}, u32[]{:S(2)}) collective-permute-start(bf16[1,2432,128]{2,1,0:T(8,128)(2,1)S(1)} %add_convert_fusion.4), channel_id=1, source_target_pairs={{0,8},{4,12},{8,0},{12,4},{16,24},{20,28},{24,16},{28,20},{1,9},{5... | collective-permute-start | bytes 1867784 | tf_op jit(solution)/shard_map/ppermute | solution.py:41
  291.2 193.8 %reduce-scatter.9.cloned.1.call-start = ((), (), s32[]{:S(2)}) async-start(), calls=%async_computation.5 | async-start | bytes 1433600 | tf_op jit(solution)/shard_map/reduce_scatter | solution.py:776
  359.4 144.3 %reduce-scatter.11.cloned.1.call-start = ((), (), s32[]{:S(2)}) async-start(), calls=%async_computation.6 | async-start | bytes 1433600 | tf_op jit(solution)/shard_map/reduce_scatter | solution.py:776
  384.4 37.0 %collective-permute-start.73 = (bf16[1216,128]{1,0:T(8,128)(2,1)S(1)}, bf16[1216,128]{1,0:T(8,128)(2,1)S(1)}, u32[]{:S(2)}, u32[]{:S(2)}) collective-permute-start(bf16[1216,128]{1,0:T(8,128)(2,1)S(1)} %fusion.19), channel_id=1, source_target_pairs={{0,2},{1,3},{2,0},{3,1},{4,6},{5,7},{6,4},{7,5},{8,10},{9,11},{10,... | collective-permute-start | bytes 933896 | tf_op jit(solution)/shard_map/ppermute | solution.py:44
  400.2 25.0 %collective-permute-start.47 = (bf16[4,4,128,256]{3,2,1,0:T(8,128)(2,1)}, bf16[4,4,128,256]{3,2,1,0:T(8,128)(2,1)S(1)}, u32[]{:S(2)}, u32[]{:S(2)}) collective-permute-start(bf16[4,4,128,256]{3,2,1,0:T(8,128)(2,1)} %get-tuple-element.77), channel_id=1, source_target_pairs={{0,4},{4,0},{8,12},{12,8},{16,20},{20,16},{24,28},{28,24},{1,5},{5... | collective-permute-start | bytes 3145736 | tf_op jit(solution)/shard_map/ppermute | solution.py:41
  413.8 77.8 %collective-permute-start.43 = (f32[512,896]{1,0:T(8,128)}, f32[512,896]{1,0:T(8,128)}, u32[]{:S(2)}, u32[]{:S(2)}) collective-permute-start(f32[512,896]{1,0:T(8,128)} %slice.429), channel_id=1, source_target_pairs={{0,4},{4,0},{8,12},{12,8},{16,20},{20,16},{24,28},{28,24},{1,5},{5... | collective-permute-start | bytes 5505032 | tf_op jit(solution)/shard_map/ppermute | solution.py:41
  443.2 30.8 %collective-permute-start.75 = (bf16[1216,128]{1,0:T(8,128)(2,1)S(1)}, bf16[1216,128]{1,0:T(8,128)(2,1)}, u32[]{:S(2)}, u32[]{:S(2)}) collective-permute-start(bf16[1216,128]{1,0:T(8,128)(2,1)S(1)} %broadcast_select_fusion.5.refs_0_), channel_id=1, source_target_pairs={{0,8},{4,12},{8,0},{12,4},{16,24},{20,28},{24,16},{28,20},{1,9},{5... | collective-permute-start | bytes 933896 | tf_op jit(solution)/shard_map/ppermute | solution.py:41
  (144 other events, 1536.3 us)
Sparse Core Ops, SparseCore 0:
  10.2 53.8 all-gather.1
  246.4 62.3 reduce-scatter.12
  311.8 55.8 reduce-scatter.14
  369.9 43.2 reduce-scatter.8
  430.2 38.1 reduce-scatter.10

commit v3 on v2

--- a/solution.py
+++ b/solution.py
@@ -710,17 +710,16 @@
         fold.until_last()
     grad_gate = unit_grad(net, normed_both_t, d_gate)
     gate_sum = sum_pairs(grad_gate)
-    d_gate, d_up = after((d_gate, d_up), grad_gate, got_of(fold_down))
+    d_gate, d_up = after((d_gate, d_up), grad_gate)
+    grad_up = unit_grad(net, normed_both_t, d_up)
+    up_sum = sum_pairs(grad_up)
+    d_gate, d_up = after((d_gate, d_up), grad_up, got_of(fold_down))
     collect_all(fold_down)
     first = [f.keep[0, :shard_units] for f in fold_down]
     second = [f.keep[0, shard_units:] for f in fold_down]
     mine = [jnp.where(even, u, v) for u, v in zip(first, second)]
     got = [net.flip_seq(jnp.where(even, v, u), 1) for u, v in zip(first, second)]
-    grad_up = unit_grad(net, normed_both_t, d_up)
-    up_sum = sum_pairs(grad_up)
-    d_gate, d_up = after((d_gate, d_up), grad_up, got)
     total = lambda own, other: (own.astype(F32) + other.astype(F32)).astype(BF16)
-    mine = [total(u, v) for u, v in zip(mine, got)]
 
     def start_seq(folds):
         collect_all(folds)
@@ -745,6 +744,9 @@
         return [v for m in range(net.pairs) for v in (pieces[m], net.flip(pieces[m], 1))]
 
     d_normed_both = contract(d_gate, gate_half, 1, 1) + contract(d_up, up_half, 1, 1)
+    d_normed_both = after(d_normed_both, got)
+    mine = [total(u, v) for u, v in zip(mine, got)]
+    got = [net.flip_seq(v, seqs // 2) for v in mine]
     d_normed_two = d_normed_both[:rows] + net.flip(d_normed_both[rows:], 1)
     grad_gain_two = jnp.sum(d_normed_two * unit_two, axis=0)
     d_mixed = cotangent.astype(F32) + norm_back(d_normed_two * gain_two, unit_two, scale_two, 1)
@@ -754,7 +756,9 @@
     d_query_t, d_key_t, d_value_t = attend_backward(
         queries_t, d_attended_t.reshape(H, HD, rows), kv[:KVH], kv_t[:KVH], kv[KVH:], runs
     )
-    d_key_t, d_value_t = after((d_key_t, d_value_t), gate_sum)
+    d_key_t, d_value_t = after((d_key_t, d_value_t), gate_sum, got)
+    mine = [total(u, v) for u, v in zip(mine, got)]
+    mine = [jnp.where(own_half, v, net.flip(v, 1)) for v in mine]
     d_kv = jnp.concatenate(
         [d_key_t.reshape(kv_width, -1), d_value_t.reshape(kv_width, -1)], axis=0
     )
@@ -775,11 +779,6 @@
         d_kv_own = d_kv_own + jnp.pad(back.astype(F32), ((0, 0), (rows - take, 0)))
     sum_seq = lambda v: lax.psum_scatter(v, "seq", scatter_dimension=0, tiled=True)
     gate_sum, up_sum = sum_seq(gate_sum), sum_seq(up_sum)
-    mine = after(mine, d_kv_own)
-    mine = [total(v, net.flip_seq(v, seqs // 2)) for v in mine]
-    mine = [jnp.where(own_half, v, net.flip(v, 1)) for v in mine]
-    output_both = contract(after(hidden, d_kv_own), down_half, 1, 0)
-    output = (mixed + output_both[:rows] + net.flip(output_both[rows:], 1)).astype(BF16)
     d_query_pre_t = rotate(d_query_t * factor, cosine, -sine).reshape(query_width, rows)
     d_key_pre_t = rotate(d_kv_own[:kv_width].reshape(KVH, HD, rows), cosine, -sine)
     d_proj_t = jnp.concatenate(
@@ -795,8 +794,6 @@
 
     gate_sums = settle_units(gate_sum, order_a)
     up_sums = settle_units(up_sum, order_b)
-    down_sums = [net.spread(v, order) for v, (_, _, order) in zip(mine, colours)]
-
     def join_units(sums):
         regions = [
             (lambda place, h=h: ((place[0] + h) % 2) * units, units, net.pairs, sums[h::2])
@@ -805,19 +802,6 @@
         return assemble(
             net, regions, 2 * units, pair_index, shard // 4, 4, lambda i, p: i, dtype=F32
         )
-
-    sum_gate = join_units(gate_sums)
-    sum_up = join_units(up_sums)
-    sum_down = assemble(
-        net,
-        [(start, span, net.pairs, v) for v, (start, span, _) in zip(down_sums, colours)],
-        width,
-        pair_index,
-        shard_units // 4,
-        4,
-        lambda i, p: i,
-        dtype=F32,
-    )
 
     pieces_of = lambda v: v.reshape(seqs, -1)
     small = jnp.concatenate(
@@ -842,10 +826,15 @@
         )
     ]
     launch_all(folds)
+    attn_got = got_of(folds)
+    mine = after(mine, attn_got)
     for fold in folds:
         fold.until_last()
+    output_both = contract(after(hidden, attn_got), down_half, 1, 0)
+    output = (mixed + output_both[:rows] + net.flip(output_both[rows:], 1)).astype(BF16)
     attn_own, attn_got = next_seq(*start_seq(folds))
     attn_sums = settle_units(total(attn_own, attn_got), order_b)
+    attn_sums = after(attn_sums, gate_sums, up_sums)
     sum_attn = assemble(
         net,
         [(0, attn_columns, net.reps, attn_sums)],
@@ -856,6 +845,21 @@
         lambda i, p: i,
         dtype=F32,
     )
+    down_sums = [net.spread(v, order) for v, (_, _, order) in zip(mine, colours)]
+
+    down_sums = after(down_sums, gate_sums, up_sums)
+    sum_down = assemble(
+        net,
+        [(start, span, net.pairs, v) for v, (start, span, _) in zip(down_sums, colours)],
+        width,
+        pair_index,
+        shard_units // 4,
+        4,
+        lambda i, p: i,
+        dtype=F32,
+    )
+    sum_gate = join_units(gate_sums)
+    sum_up = join_units(up_sums)
     row = sum_attn[shard]
     sum_gain_one, sum_query_bias, sum_key_bias, sum_value_bias, sum_gain_two = [
         row[e - s : e] for s, e in zip(sizes, ends)

time: 560 us -> 530 us (0.946)
  waiting for transfers between devices: 147 us -> 124 us
  other arithmetic: 62 us -> 56.2 us
  starting transfers between devices: 64.7 us -> 70.4 us
    ppermute x10, waiting for transfers between devices: 50.7 us -> 35.2 us  [flip_seq(): return lax.ppermute(value, 'seq', [(i, i ^ bit) for i in range(self.seqs)])]
    ppermute x69, waiting for transfers between devices: 80.7 us -> 69.1 us  [flip(): return lax.ppermute(value, 'rep', [(i, i ^ bit) for i in range(self.reps)])]
    ppermute x69, starting transfers between devices: 46.2 us -> 52.2 us  [flip(): return lax.ppermute(value, 'rep', [(i, i ^ bit) for i in range(self.reps)])]
  transfers between devices with their start and end apart: 88 -> 88, of which waited for: 28 -> 27; matrix products, arithmetic and copies ran while one was open for 32% -> 31% of each run, Pallas kernels for 19% -> 18%
where the time goes in v3:
time: 530 us; the launch traced here: 522 us
  waiting for transfers between devices  124 us (23%)
  Pallas kernels  119 us (22%)
  starting transfers between devices  70.4 us (13%)
  matrix products  69.4 us (13%)
  other arithmetic  56.2 us (11%)
  local copies, waits for them, and re-layouts  48.3 us (9%)
  blocking collectives  19.6 us (4%)
  between operations  15.5 us (3%)
    dot_general x10, matrix products, contract(): lax.dot_general(left, right, (((left_dim,), (right_dim,)), ((), ())), pre...  69.4 us
    ppermute x69, waiting for transfers between devices, flip(): return lax.ppermute(value, 'rep', [(i, i ^ bit) for i in range(self.reps)])  69.1 us
    ppermute x69, starting transfers between devices, flip(): return lax.ppermute(value, 'rep', [(i, i ^ bit) for i in range(self.reps)])  52.2 us
    pallas_call x9, Pallas kernels, assemble(): pl.pallas_call(body, name='assemble', out_shape=jax.ShapeDtypeStruct((row...  43.7 us
    ppermute x10, waiting for transfers between devices, flip_seq(): return lax.ppermute(value, 'seq', [(i, i ^ bit) for i in range(self.seqs)])  35.2 us
    pallas_call x2, Pallas kernels, unit_grad(): pl.pallas_call(body, name='unit_grad', out_shape=jax.ShapeDtypeStruct((ne...  20.8 us
    pallas_call x1, Pallas kernels, attend_backward(): pl.pallas_call(body, name='attend_backward', out_shape=(jax.ShapeDtypeStr...  20.7 us
    all_gather x1, blocking collectives, gather_seq(): return lax.all_gather(value, 'seq', axis=0, tiled=True)  19.6 us
  transfers between devices with their start and end apart: 88, of which 27 were waited for; matrix products, arithmetic and copies ran while one was open for 31% of the time, Pallas kernels for 18%

profile of v3, /device:TPU:0, one launch (start us, length us, event | category | flops | bytes accessed | tf_op | source)
XLA Modules:
  0.0 521.9 jit_solution(2591749523868279428)
XLA Ops:
  10.2 19.6 %all_gather.6 = bf16[928,256]{1,0:T(8,128)(2,1)S(1)} all-gather(bf16[232,256]{1,0:T(8,128)(2,1)S(1)} %pad_maximum_fusion.13), channel_id=1, replica_groups=mesh['rep'=8,'seq'=4] {'seq'}, dimensions={0}, use_global_device_ids=true | all-gather | bytes 593920 | tf_op jit(solution)/shard_map/all_gather | solution.py:51
  89.1 12.2 %collective-permute-done.16.refs_1_ = bf16[672,640]{1,0:T(8,128)(2,1)} collective-permute-done((bf16[672,640]{1,0:T(8,128)(2,1)}, bf16[672,640]{1,0:T(8,128)(2,1)}, u32[]{:S(2)}, u32[]{:S(2)}) %collective-permute-start.16) | collective-permute-done | bytes 860192 | tf_op jit(solution)/shard_map/ppermute | solution.py:41
  109.0 12.2 %attend_forward.1 = bf16[14,64,512]{2,1,0:T(8,128)(2,1)} custom-call(s32[2]{0:T(128)} %slice.302.runs_ref, bf16[14,64,512]{2,1,0:T(8,128)(2,1)} %multiply_convert_fusion.4.q_ref, bf16[2,1280,64]{2,1,0:T(8,128)(2,1)} %get-tuple-element.148.k_ref, bf16[2,64,1280]{2,1,0:T(8,128)(2,1)} %get-tuple-element.154.v_ref), custom_call_target="tpu_custom_call" | custom-call | flops 18790481920 | bytes 3670016 | tf_op jit(solution)/shard_map/attend_forward/pallas_call | solution.py:370
  125.9 6.0 %collective-permute-done.19 = bf16[1216,128]{1,0:T(8,128)(2,1)S(1)} collective-permute-done((bf16[1216,128]{1,0:T(8,128)(2,1)S(1)}, bf16[1216,128]{1,0:T(8,128)(2,1)S(1)}, u32[]{:S(2)}, u32[]{:S(2)}) %collective-permute-start.19) | collective-permute-done | bytes 311328 | tf_op jit(solution)/shard_map/ppermute | solution.py:44
  141.5 8.2 %collective-permute-done.24 = bf16[1216,128]{1,0:T(8,128)(2,1)S(1)} collective-permute-done((bf16[1216,128]{1,0:T(8,128)(2,1)S(1)}, bf16[1216,128]{1,0:T(8,128)(2,1)S(1)}, u32[]{:S(2)}, u32[]{:S(2)}) %collective-permute-start.24) | collective-permute-done | bytes 311328 | tf_op jit(solution)/shard_map/ppermute | solution.py:44
  152.0 5.9 %assemble.12 = bf16[896,2432]{1,0:T(8,128)(2,1)} custom-call(s32[2]{0:T(128)} %pad_add_fusion.place, bf16[672,640]{1,0:T(8,128)(2,1)} %bitcast.11.refs_0_, bf16[672,640]{1,0:T(8,128)(2,1)} %collective-permute-done.25.refs_1_, bf16[672,640]{1,0:T(8,128)(2,1)} %collective-permute-done.17.refs_2_, bf16[672,640]{1,0:T(8,128)(2,1)} %collective-permute-done.26.refs_3_, ...), custom_call_target="tpu_custom_call" | custom-call | bytes 8716288 | tf_op jit(solution)/shard_map/assemble/pallas_call | solution.py:158
  160.8 5.9 %assemble.11 = bf16[896,2432]{1,0:T(8,128)(2,1)} custom-call(s32[2]{0:T(128)} %pad_add_fusion.place, bf16[672,640]{1,0:T(8,128)(2,1)} %bitcast.10.refs_0_, bf16[672,640]{1,0:T(8,128)(2,1)} %collective-permute-done.16.refs_1_, bf16[672,640]{1,0:T(8,128)(2,1)} %collective-permute-done.21.refs_2_, bf16[672,640]{1,0:T(8,128)(2,1)} %collective-permute-done.22.refs_3_, ...), custom_call_target="tpu_custom_call" | custom-call | bytes 8716288 | tf_op jit(solution)/shard_map/assemble/pallas_call | solution.py:158
  169.5 7.3 %fusion.41 = f32[1024,2432]{1,0:T(8,128)S(1)} fusion(bf16[896,2432]{1,0:T(8,128)(2,1)S(1)} %copy-done.2, bf16[512,896]{1,0:T(8,128)(2,1)} %collective-permute-done.20, bf16[512,896]{1,0:T(8,128)(2,1)S(1)} %multiply_convert_fusion.3), kind=kOutput, calls=%fused_computation.150 | convolution fusion | flops 4466409472 | bytes 16154624 | tf_op jit(solution)/shard_map/dot_general | solution.py:479
  182.0 9.4 %multiply_convert_fusion.2 = (bf16[1024,2432]{1,0:T(8,128)(2,1)}, f32[1024,2432]{1,0:T(8,128)}) fusion(f32[1024,2432]{1,0:T(8,128)S(1)} %fusion.41, bf16[1024,896]{1,0:T(8,128)(2,1)S(1)} %get-tuple-element.69, bf16[896,2432]{1,0:T(8,128)(2,1)S(1)} %bitcast.84), kind=kOutput, calls=%fused_computation.2 | convolution fusion | flops 4477681664 | bytes 31096832 | tf_op jit(solution)/shard_map/dot_general | solution.py:479
  195.2 12.1 %down_grad.1 = (bf16[2,2432,128]{2,1,0:T(8,128)(2,1)}, bf16[2,2432,128]{2,1,0:T(8,128)(2,1)}, bf16[2,2432,128]{2,1,0:T(8,128)(2,1)}, bf16[2,2432,128]{2,1,0:T(8,128)(2,1)}) custom-call(s32[2]{0:T(128)} %pad_add_fusion.place, bf16[896,1024]{1,0:T(8,128)(2,1)} %get-tuple-element.143.left_ref, bf16[1024,2432]{1,0:T(8,128)(2,1)} %get-tuple-element.93.right_ref), custom_call_target="tpu_custom_call" | custom-call | flops 4462739456 | bytes 11173888 | tf_op jit(solution)/shard_map/down_grad/pallas_call | solution.py:198
  210.2 6.0 %assemble.13 = bf16[2432,896]{1,0:T(8,128)(2,1)} custom-call(s32[2]{0:T(128)} %pad_add_fusion.place, bf16[2432,128]{1,0:T(8,128)(2,1)} %copy-done.10, bf16[2432,128]{1,0:T(8,128)(2,1)} %collective-permute-done.27.refs_1_, bf16[2432,128]{1,0:T(8,128)(2,1)} %collective-permute-done.30.refs_2_, bf16[2432,128]{1,0:T(8,128)(2,1)} %collective-permute-done.31.refs_3_, ...), custom_call_target="tpu_custom_call" | custom-call | bytes 8716288 | tf_op jit(solution)/shard_map/assemble/pallas_call | solution.py:158
  216.1 16.2 %multiply_convert_fusion = (bf16[1024,2432]{1,0:T(8,128)(2,1)}, bf16[1024,2432]{1,0:T(8,128)(2,1)}) fusion(f32[1024,2432]{1,0:T(8,128)} %copy-done.79, f32[1024,2432]{1,0:T(8,128)} %get-tuple-element.178, bf16[1024,896]{0,1:T(8,128)(2,1)} %get-tuple-element.75, bf16[2432,896]{1,0:T(8,128)(2,1)} %assemble.13), kind=kOutput, calls=%fused_computation | convolution fusion | flops 4495114240 | bytes 36077568 | tf_op jit(solution)/shard_map/dot_general | solution.py:479
  236.1 10.4 %unit_grad.2 = bf16[4,896,640]{2,1,0:T(8,128)(2,1)} custom-call(bf16[896,1024]{1,0:T(8,128)(2,1)} %copy.67.left_ref, bf16[1024,2432]{1,0:T(8,128)(2,1)} %get-tuple-element.80.right_ref), custom_call_target="tpu_custom_call" | custom-call | flops 4462739456 | bytes 11173888 | tf_op jit(solution)/shard_map/unit_grad/pallas_call | solution.py:232
  253.9 10.4 %unit_grad.3 = bf16[4,896,640]{2,1,0:T(8,128)(2,1)} custom-call(bf16[896,1024]{1,0:T(8,128)(2,1)} %copy.67.left_ref, bf16[1024,2432]{1,0:T(8,128)(2,1)} %get-tuple-element.81.right_ref), custom_call_target="tpu_custom_call" | custom-call | flops 4462739456 | bytes 11173888 | tf_op jit(solution)/shard_map/unit_grad/pallas_call | solution.py:232
  264.4 11.3 %collective-permute-done.36 = bf16[1,2432,128]{2,1,0:T(8,128)(2,1)} collective-permute-done((bf16[1,2432,128]{2,1,0:T(8,128)(2,1)}, bf16[1,2432,128]{2,1,0:T(8,128)(2,1)}, u32[]{:S(2)}, u32[]{:S(2)}) %collective-permute-start.36) | collective-permute-done | bytes 622624 | tf_op jit(solution)/shard_map/ppermute | solution.py:41
  283.2 9.5 %fusion.53 = f32[1024,896]{1,0:T(8,128)S(1)} fusion(bf16[1024,2432]{1,0:T(8,128)(2,1)} %get-tuple-element.81.right_ref, bf16[896,2432]{1,0:T(8,128)(2,1)} %assemble.12), kind=kOutput, calls=%fused_computation.162 | convolution fusion | flops 4462739456 | bytes 13008896 | tf_op jit(solution)/shard_map/dot_general | solution.py:479
  292.7 5.5 %convolution_add_fusion.1 = f32[1024,896]{1,0:T(8,128)S(1)} fusion(f32[1024,896]{1,0:T(8,128)S(1)} %fusion.53, bf16[1024,2432]{1,0:T(8,128)(2,1)S(1)} %bitcast.118, bf16[896,2432]{1,0:T(8,128)(2,1)S(1)} %bitcast.86), kind=kOutput, calls=%fused_computation.38 | convolution fusion | flops 4463656960 | bytes 16678912 | tf_op jit(solution)/shard_map/dot_general | solution.py:479
  307.8 20.7 %attend_backward.1 = (f32[14,64,512]{2,1,0:T(8,128)}, f32[2,64,1280]{2,1,0:T(8,128)}, f32[2,64,1280]{2,1,0:T(8,128)}) custom-call(s32[2]{0:T(128)} %slice.302.runs_ref, bf16[14,64,512]{2,1,0:T(8,128)(2,1)} %multiply_convert_fusion.4.q_ref, bf16[14,64,512]{2,1,0:T(8,128)(2,1)} %bitcast.116, bf16[2,1280,64]{2,1,0:T(8,128)(2,1)} %get-tuple-element.148.k_ref, ...), custom_call_target="tpu_custom_call" | custom-call | flops 37580963840 | bytes 3670016 | tf_op jit(solution)/shard_map/attend_backward/pallas_call | solution.py:442
  341.1 19.1 %collective-permute-done.44 = bf16[256,256]{0,1:T(8,128)(2,1)} collective-permute-done((bf16[256,256]{0,1:T(8,128)(2,1)}, bf16[256,256]{0,1:T(8,128)(2,1)}, u32[]{:S(2)}, u32[]{:S(2)}) %collective-permute-start.44) | collective-permute-done | bytes 131104 | tf_op jit(solution)/shard_map/ppermute | solution.py:48
  377.6 9.3 %attn_grad.1 = (bf16[4,4,128,256]{3,2,1,0:T(8,128)(2,1)}, bf16[4,4,128,256]{3,2,1,0:T(8,128)(2,1)}, bf16[4,4,128,256]{3,2,1,0:T(8,128)(2,1)}, bf16[4,4,128,256]{3,2,1,0:T(8,128)(2,1)}) custom-call(s32[2]{0:T(128)} %pad_add_fusion.place, bf16[896,512]{1,0:T(8,128)(2,1)} %copy.75.a_ref, bf16[512,1152]{1,0:T(8,128)(2,1)} %get-tuple-element.150.b_ref, ...), custom_call_target="tpu_custom_call" | custom-call | flops 1879048192 | bytes 7864320 | tf_op jit(solution)/shard_map/attn_grad/pallas_call | solution.py:316
  401.0 7.6 %collective-permute-done.48 = bf16[2,4,128,256]{3,2,1,0:T(8,128)(2,1)S(1)} collective-permute-done((bf16[2,4,128,256]{3,2,1,0:T(8,128)(2,1)}, bf16[2,4,128,256]{3,2,1,0:T(8,128)(2,1)S(1)}, u32[]{:S(2)}, u32[]{:S(2)}) %collective-permute-start.48) | collective-permute-done | bytes 524320 | tf_op jit(solution)/shard_map/ppermute | solution.py:41
  414.6 8.7 %fusion.54 = f32[1024,896]{1,0:T(8,128)S(1)} fusion(bf16[1024,2432]{1,0:T(8,128)(2,1)} %get-tuple-element.93.right_ref, bf16[2432,896]{1,0:T(8,128)(2,1)} %assemble.13), kind=kOutput, calls=%fused_computation.163 | convolution fusion | flops 4462739456 | bytes 13008896 | tf_op jit(solution)/shard_map/dot_general | solution.py:479
  432.2 8.9 %collective-permute-done.52 = bf16[2,256,256]{2,1,0:T(8,128)(2,1)S(1)} collective-permute-done((bf16[2,256,256]{2,1,0:T(8,128)(2,1)}, bf16[2,256,256]{2,1,0:T(8,128)(2,1)S(1)}, u32[]{:S(2)}, u32[]{:S(2)}) %collective-permute-start.52) | collective-permute-done | bytes 262176 | tf_op jit(solution)/shard_map/ppermute | solution.py:44
  454.1 5.6 %collective-permute-done.71.refs_2_ = bf16[224,640]{1,0:T(8,128)(2,1)S(1)} collective-permute-done((bf16[224,640]{1,0:T(8,128)(2,1)}, bf16[224,640]{1,0:T(8,128)(2,1)S(1)}, u32[]{:S(2)}, u32[]{:S(2)}) %collective-permute-start.71) | collective-permute-done | bytes 286752 | tf_op jit(solution)/shard_map/ppermute | solution.py:41
  (478 shorter events, 258.4 us)
Async XLA Ops:
  7.3 68.2 %all-gather.2.cloned.1.call-start = ((), (), s32[]{:S(2)}) async-start(), calls=%async_computation.4 | async-start | bytes 2867200 | tf_op jit(solution)/shard_map/all_gather | solution.py:51
  9.7 321.8 %reduce-scatter.13.cloned.1.call-start = ((), (), s32[]{:S(2)}) async-start(), calls=%async_computation.7 | async-start | bytes 5734400
  52.5 30.0 %collective-permute-start.29 = (bf16[512,896]{0,1:T(8,128)(2,1)S(1)}, bf16[512,896]{0,1:T(8,128)(2,1)}, u32[]{:S(2)}, u32[]{:S(2)}) collective-permute-start(bf16[512,896]{0,1:T(8,128)(2,1)S(1)} %copy.66), channel_id=1, source_target_pairs={{0,4},{4,0},{8,12},{12,8},{16,20},{20,16},{24,28},{28,24},{1,5},{5... | collective-permute-start | bytes 2752520 | tf_op jit(solution)/shard_map/ppermute | solution.py:41
  87.1 70.8 %collective-permute-start.21 = (bf16[672,640]{1,0:T(8,128)(2,1)}, bf16[672,640]{1,0:T(8,128)(2,1)}, u32[]{:S(2)}, u32[]{:S(2)}) collective-permute-start(bf16[672,640]{1,0:T(8,128)(2,1)} %bitcast.10.refs_0_), channel_id=1, source_target_pairs={{0,16},{4,20},{8,24},{12,28},{16,0},{20,4},{24,8},{28,12},{1,17},{... | collective-permute-start | bytes 2580488 | tf_op jit(solution)/shard_map/ppermute | solution.py:41
  88.6 62.3 %collective-permute-start.25 = (bf16[672,640]{1,0:T(8,128)(2,1)}, bf16[672,640]{1,0:T(8,128)(2,1)}, u32[]{:S(2)}, u32[]{:S(2)}) collective-permute-start(bf16[672,640]{1,0:T(8,128)(2,1)} %bitcast.11.refs_0_), channel_id=1, source_target_pairs={{0,8},{4,12},{8,0},{12,4},{16,24},{20,28},{24,16},{28,20},{1,9},{5... | collective-permute-start | bytes 2580488 | tf_op jit(solution)/shard_map/ppermute | solution.py:41
  105.0 27.0 %collective-permute-start.19 = (bf16[1216,128]{1,0:T(8,128)(2,1)S(1)}, bf16[1216,128]{1,0:T(8,128)(2,1)S(1)}, u32[]{:S(2)}, u32[]{:S(2)}) collective-permute-start(bf16[1216,128]{1,0:T(8,128)(2,1)S(1)} %get-tuple-element.67), channel_id=1, source_target_pairs={{0,2},{1,3},{2,0},{3,1},{4,6},{5,7},{6,4},{7,5},{8,10},{9,11},{10,... | collective-permute-start | bytes 933896 | tf_op jit(solution)/shard_map/ppermute | solution.py:44
  121.3 38.1 %collective-permute-start.22 = (bf16[672,640]{1,0:T(8,128)(2,1)}, bf16[672,640]{1,0:T(8,128)(2,1)}, u32[]{:S(2)}, u32[]{:S(2)}) collective-permute-start(bf16[672,640]{1,0:T(8,128)(2,1)} %collective-permute-done.16.refs_1_), channel_id=1, source_target_pairs={{0,16},{4,20},{8,24},{12,28},{16,0},{20,4},{24,8},{28,12},{1,17},{... | collective-permute-start | bytes 2580488 | tf_op jit(solution)/shard_map/ppermute | solution.py:41
  125.3 26.1 %collective-permute-start.26 = (bf16[672,640]{1,0:T(8,128)(2,1)}, bf16[672,640]{1,0:T(8,128)(2,1)}, u32[]{:S(2)}, u32[]{:S(2)}) collective-permute-start(bf16[672,640]{1,0:T(8,128)(2,1)} %collective-permute-done.17.refs_2_), channel_id=1, source_target_pairs={{0,8},{4,12},{8,0},{12,4},{16,24},{20,28},{24,16},{28,20},{1,9},{5... | collective-permute-start | bytes 2580488 | tf_op jit(solution)/shard_map/ppermute | solution.py:41
  150.8 57.1 %collective-permute-start.32 = (bf16[2432,128]{1,0:T(8,128)(2,1)}, bf16[2432,128]{1,0:T(8,128)(2,1)}, u32[]{:S(2)}, u32[]{:S(2)}) collective-permute-start(bf16[2432,128]{1,0:T(8,128)(2,1)} %pad_maximum_fusion.7.refs_4_), channel_id=1, source_target_pairs={{0,8},{4,12},{8,0},{12,4},{16,24},{20,28},{24,16},{28,20},{1,9},{5... | collective-permute-start | bytes 1867784 | tf_op jit(solution)/shard_map/ppermute | solution.py:41
  157.9 51.4 %collective-permute-start.30 = (bf16[2432,128]{1,0:T(8,128)(2,1)S(1)}, bf16[2432,128]{1,0:T(8,128)(2,1)}, u32[]{:S(2)}, u32[]{:S(2)}) collective-permute-start(bf16[2432,128]{1,0:T(8,128)(2,1)S(1)} %pad_maximum_fusion.6.refs_0_), channel_id=1, source_target_pairs={{0,16},{4,20},{8,24},{12,28},{16,0},{20,4},{24,8},{28,12},{1,17},{... | collective-permute-start | bytes 1867784 | tf_op jit(solution)/shard_map/ppermute | solution.py:41
  176.9 32.5 %collective-permute-start.33 = (bf16[2432,128]{1,0:T(8,128)(2,1)}, bf16[2432,128]{1,0:T(8,128)(2,1)S(1)}, u32[]{:S(2)}, u32[]{:S(2)}) collective-permute-start(bf16[2432,128]{1,0:T(8,128)(2,1)} %collective-permute-done.28.refs_6_), channel_id=1, source_target_pairs={{0,8},{4,12},{8,0},{12,4},{16,24},{20,28},{24,16},{28,20},{1,9},{5... | collective-permute-start | bytes 1867784 | tf_op jit(solution)/shard_map/ppermute | solution.py:41
  181.4 28.0 %collective-permute-start.31 = (bf16[2432,128]{1,0:T(8,128)(2,1)}, bf16[2432,128]{1,0:T(8,128)(2,1)}, u32[]{:S(2)}, u32[]{:S(2)}) collective-permute-start(bf16[2432,128]{1,0:T(8,128)(2,1)} %collective-permute-done.27.refs_1_), channel_id=1, source_target_pairs={{0,16},{4,20},{8,24},{12,28},{16,0},{20,4},{24,8},{28,12},{1,17},{... | collective-permute-start | bytes 1867784 | tf_op jit(solution)/shard_map/ppermute | solution.py:41
  207.4 28.5 %collective-permute-start.34 = (bf16[2,2432,128]{2,1,0:T(8,128)(2,1)}, bf16[2,2432,128]{2,1,0:T(8,128)(2,1)}, u32[]{:S(2)}, u32[]{:S(2)}) collective-permute-start(bf16[2,2432,128]{2,1,0:T(8,128)(2,1)} %get-tuple-element.72), channel_id=1, source_target_pairs={{0,8},{4,12},{8,0},{12,4},{16,24},{20,28},{24,16},{28,20},{1,9},{5... | collective-permute-start | bytes 3735560 | tf_op jit(solution)/shard_map/ppermute | solution.py:41
  207.9 28.2 %collective-permute-start.35 = (bf16[2,2432,128]{2,1,0:T(8,128)(2,1)}, bf16[2,2432,128]{2,1,0:T(8,128)(2,1)}, u32[]{:S(2)}, u32[]{:S(2)}) collective-permute-start(bf16[2,2432,128]{2,1,0:T(8,128)(2,1)} %get-tuple-element.74), channel_id=1, source_target_pairs={{0,16},{4,20},{8,24},{12,28},{16,0},{20,4},{24,8},{28,12},{1,17},{... | collective-permute-start | bytes 3735560 | tf_op jit(solution)/shard_map/ppermute | solution.py:41
  246.6 154.4 %reduce-scatter.15.cloned.1.call-start = ((), (), s32[]{:S(2)}) async-start(), calls=%async_computation.8 | async-start | bytes 5734400
  249.0 26.7 %collective-permute-start.36 = (bf16[1,2432,128]{2,1,0:T(8,128)(2,1)}, bf16[1,2432,128]{2,1,0:T(8,128)(2,1)}, u32[]{:S(2)}, u32[]{:S(2)}) collective-permute-start(bf16[1,2432,128]{2,1,0:T(8,128)(2,1)} %add_convert_fusion.5), channel_id=1, source_target_pairs={{0,16},{4,20},{8,24},{12,28},{16,0},{20,4},{24,8},{28,12},{1,17},{... | collective-permute-start | bytes 1867784 | tf_op jit(solution)/shard_map/ppermute | solution.py:41
  252.6 28.9 %collective-permute-start.37 = (bf16[1,2432,128]{2,1,0:T(8,128)(2,1)}, bf16[1,2432,128]{2,1,0:T(8,128)(2,1)}, u32[]{:S(2)}, u32[]{:S(2)}) collective-permute-start(bf16[1,2432,128]{2,1,0:T(8,128)(2,1)} %add_convert_fusion.4), channel_id=1, source_target_pairs={{0,8},{4,12},{8,0},{12,4},{16,24},{20,28},{24,16},{28,20},{1,9},{5... | collective-permute-start | bytes 1867784 | tf_op jit(solution)/shard_map/ppermute | solution.py:41
  264.3 167.6 %reduce-scatter.9.cloned.1.call-start = ((), (), s32[]{:S(2)}) async-start(), calls=%async_computation.5 | async-start | bytes 1433600 | tf_op jit(solution)/shard_map/reduce_scatter | solution.py:780
  298.6 32.9 %collective-permute-start.41 = (bf16[1216,128]{1,0:T(8,128)(2,1)S(1)}, bf16[1216,128]{1,0:T(8,128)(2,1)}, u32[]{:S(2)}, u32[]{:S(2)}) collective-permute-start(bf16[1216,128]{1,0:T(8,128)(2,1)S(1)} %fusion.19), channel_id=1, source_target_pairs={{0,2},{1,3},{2,0},{3,1},{4,6},{5,7},{6,4},{7,5},{8,10},{9,11},{10,... | collective-permute-start | bytes 933896 | tf_op jit(solution)/shard_map/ppermute | solution.py:44
  298.8 32.7 %collective-permute-start.42 = (bf16[1216,128]{1,0:T(8,128)(2,1)S(1)}, bf16[1216,128]{1,0:T(8,128)(2,1)}, u32[]{:S(2)}, u32[]{:S(2)}) collective-permute-start(bf16[1216,128]{1,0:T(8,128)(2,1)S(1)} %fusion.18), channel_id=1, source_target_pairs={{0,2},{1,3},{2,0},{3,1},{4,6},{5,7},{6,4},{7,5},{8,10},{9,11},{10,... | collective-permute-start | bytes 933896 | tf_op jit(solution)/shard_map/ppermute | solution.py:44
  334.6 25.7 %collective-permute-start.43 = (bf16[256,512]{0,1:T(8,128)(2,1)}, bf16[256,512]{0,1:T(8,128)(2,1)}, u32[]{:S(2)}, u32[]{:S(2)}) collective-permute-start(bf16[256,512]{0,1:T(8,128)(2,1)} %slice.426), channel_id=1, source_target_pairs={{1,0},{2,1},{3,2},{5,4},{6,5},{7,6},{9,8},{10,9},{11,10},{13,12},{... | collective-permute-start | bytes 786440 | tf_op jit(solution)/shard_map/ppermute | solution.py:48
  341.0 103.9 %reduce-scatter.11.cloned.1.call-start = ((), (), s32[]{:S(2)}) async-start(), calls=%async_computation.6 | async-start | bytes 1433600 | tf_op jit(solution)/shard_map/reduce_scatter | solution.py:780
  390.5 37.4 %collective-permute-start.76 = (bf16[1216,128]{1,0:T(8,128)(2,1)}, bf16[1216,128]{1,0:T(8,128)(2,1)}, u32[]{:S(2)}, u32[]{:S(2)}) collective-permute-start(bf16[1216,128]{1,0:T(8,128)(2,1)} %add_convert_fusion.12), channel_id=1, source_target_pairs={{0,4},{4,0},{8,12},{12,8},{16,20},{20,16},{24,28},{28,24},{1,5},{5... | collective-permute-start | bytes 933896 | tf_op jit(solution)/shard_map/ppermute | solution.py:41
  424.8 53.7 %collective-permute-start.47 = (f32[512,896]{1,0:T(8,128)}, f32[512,896]{1,0:T(8,128)}, u32[]{:S(2)}, u32[]{:S(2)}) collective-permute-start(f32[512,896]{1,0:T(8,128)} %slice.436), channel_id=1, source_target_pairs={{0,4},{4,0},{8,12},{12,8},{16,20},{20,16},{24,28},{28,24},{1,5},{5... | collective-permute-start | bytes 5505032 | tf_op jit(solution)/shard_map/ppermute | solution.py:41
  (151 other events, 1542.4 us)
Sparse Core Ops, SparseCore 0:
  10.2 53.8 all-gather.1
  246.7 63.9 reduce-scatter.12
  313.8 55.8 reduce-scatter.14
  371.8 28.8 reduce-scatter.8
  402.9 27.3 reduce-scatter.10

commit v4 on v3

--- a/solution.py
+++ b/solution.py
@@ -834,7 +834,7 @@
     output = (mixed + output_both[:rows] + net.flip(output_both[rows:], 1)).astype(BF16)
     attn_own, attn_got = next_seq(*start_seq(folds))
     attn_sums = settle_units(total(attn_own, attn_got), order_b)
-    attn_sums = after(attn_sums, gate_sums, up_sums)
+    attn_sums = after(attn_sums, gate_sums[::2], up_sums[::2])
     sum_attn = assemble(
         net,
         [(0, attn_columns, net.reps, attn_sums)],
@@ -847,7 +847,7 @@
     )
     down_sums = [net.spread(v, order) for v, (_, _, order) in zip(mine, colours)]
 
-    down_sums = after(down_sums, gate_sums, up_sums)
+    down_sums = after(down_sums, gate_sums[::2], up_sums[::2])
     sum_down = assemble(
         net,
         [(start, span, net.pairs, v) for v, (start, span, _) in zip(down_sums, colours)],

time: 530 us -> 523 us (0.987)
    ppermute x10, waiting for transfers between devices: 35.2 us -> 27.2 us  [flip_seq(): return lax.ppermute(value, 'seq', [(i, i ^ bit) for i in range(self.seqs)])]
  transfers between devices with their start and end apart: 88 -> 88, of which waited for: 27 -> 26; matrix products, arithmetic and copies ran while one was open for 31% -> 31% of each run, Pallas kernels for 18% -> 20%
where the time goes in v4:
time: 523 us; the launch traced here: 515 us
  waiting for transfers between devices  123 us (24%)
  Pallas kernels  119 us (23%)
  matrix products  69.4 us (13%)
  starting transfers between devices  68.3 us (13%)
  other arithmetic  52 us (10%)
  local copies, waits for them, and re-layouts  47.4 us (9%)
  blocking collectives  19.6 us (4%)
  between operations  15.5 us (3%)
    ppermute x69, waiting for transfers between devices, flip(): return lax.ppermute(value, 'rep', [(i, i ^ bit) for i in range(self.reps)])  74.1 us
    dot_general x10, matrix products, contract(): lax.dot_general(left, right, (((left_dim,), (right_dim,)), ((), ())), pre...  69.4 us
    ppermute x69, starting transfers between devices, flip(): return lax.ppermute(value, 'rep', [(i, i ^ bit) for i in range(self.reps)])  50.1 us
    pallas_call x9, Pallas kernels, assemble(): pl.pallas_call(body, name='assemble', out_shape=jax.ShapeDtypeStruct((row...  43.8 us
    ppermute x10, waiting for transfers between devices, flip_seq(): return lax.ppermute(value, 'seq', [(i, i ^ bit) for i in range(self.seqs)])  27.2 us
    ppermute x4, waiting for transfers between devices, slide(): return lax.ppermute(value, 'seq', pairs)  21.9 us
    pallas_call x2, Pallas kernels, unit_grad(): pl.pallas_call(body, name='unit_grad', out_shape=jax.ShapeDtypeStruct((ne...  20.8 us
    pallas_call x1, Pallas kernels, attend_backward(): pl.pallas_call(body, name='attend_backward', out_shape=(jax.ShapeDtypeStr...  20.7 us
  transfers between devices with their start and end apart: 88, of which 26 were waited for; matrix products, arithmetic and copies ran while one was open for 31% of the time, Pallas kernels for 20%

profile of v4, /device:TPU:0, one launch (start us, length us, event | category | flops | bytes accessed | tf_op | source)
XLA Modules:
  0.0 514.6 jit_solution(872588416887581220)
XLA Ops:
  10.2 19.6 %all_gather.6 = bf16[928,256]{1,0:T(8,128)(2,1)S(1)} all-gather(bf16[232,256]{1,0:T(8,128)(2,1)S(1)} %pad_maximum_fusion.13), channel_id=1, replica_groups=mesh['rep'=8,'seq'=4] {'seq'}, dimensions={0}, use_global_device_ids=true | all-gather | bytes 593920 | tf_op jit(solution)/shard_map/all_gather | solution.py:51
  70.2 5.3 %collective-permute-start.15 = (bf16[256,512]{1,0:T(8,128)(2,1)}, bf16[256,512]{1,0:T(8,128)(2,1)}, u32[]{:S(2)}, u32[]{:S(2)}) collective-permute-start(bf16[256,512]{1,0:T(8,128)(2,1)} %pad_maximum_fusion.9), channel_id=1, source_target_pairs={{0,1},{1,2},{2,3},{4,5},{5,6},{6,7},{8,9},{9,10},{10,11},{12,13},{... | collective-permute-start | bytes 786440 | tf_op jit(solution)/shard_map/ppermute | solution.py:48
  89.1 12.2 %collective-permute-done.16.refs_1_ = bf16[672,640]{1,0:T(8,128)(2,1)} collective-permute-done((bf16[672,640]{1,0:T(8,128)(2,1)}, bf16[672,640]{1,0:T(8,128)(2,1)}, u32[]{:S(2)}, u32[]{:S(2)}) %collective-permute-start.16) | collective-permute-done | bytes 860192 | tf_op jit(solution)/shard_map/ppermute | solution.py:41
  109.0 12.2 %attend_forward.1 = bf16[14,64,512]{2,1,0:T(8,128)(2,1)} custom-call(s32[2]{0:T(128)} %slice.302.runs_ref, bf16[14,64,512]{2,1,0:T(8,128)(2,1)} %multiply_convert_fusion.4.q_ref, bf16[2,1280,64]{2,1,0:T(8,128)(2,1)} %get-tuple-element.148.k_ref, bf16[2,64,1280]{2,1,0:T(8,128)(2,1)} %get-tuple-element.154.v_ref), custom_call_target="tpu_custom_call" | custom-call | flops 18790481920 | bytes 3670016 | tf_op jit(solution)/shard_map/attend_forward/pallas_call | solution.py:370
  125.9 6.0 %collective-permute-done.19 = bf16[1216,128]{1,0:T(8,128)(2,1)S(1)} collective-permute-done((bf16[1216,128]{1,0:T(8,128)(2,1)S(1)}, bf16[1216,128]{1,0:T(8,128)(2,1)S(1)}, u32[]{:S(2)}, u32[]{:S(2)}) %collective-permute-start.19) | collective-permute-done | bytes 311328 | tf_op jit(solution)/shard_map/ppermute | solution.py:44
  141.5 8.2 %collective-permute-done.24 = bf16[1216,128]{1,0:T(8,128)(2,1)S(1)} collective-permute-done((bf16[1216,128]{1,0:T(8,128)(2,1)S(1)}, bf16[1216,128]{1,0:T(8,128)(2,1)S(1)}, u32[]{:S(2)}, u32[]{:S(2)}) %collective-permute-start.24) | collective-permute-done | bytes 311328 | tf_op jit(solution)/shard_map/ppermute | solution.py:44
  152.0 5.9 %assemble.12 = bf16[896,2432]{1,0:T(8,128)(2,1)} custom-call(s32[2]{0:T(128)} %pad_add_fusion.place, bf16[672,640]{1,0:T(8,128)(2,1)} %bitcast.11.refs_0_, bf16[672,640]{1,0:T(8,128)(2,1)} %collective-permute-done.25.refs_1_, bf16[672,640]{1,0:T(8,128)(2,1)} %collective-permute-done.17.refs_2_, bf16[672,640]{1,0:T(8,128)(2,1)} %collective-permute-done.26.refs_3_, ...), custom_call_target="tpu_custom_call" | custom-call | bytes 8716288 | tf_op jit(solution)/shard_map/assemble/pallas_call | solution.py:158
  160.8 5.9 %assemble.11 = bf16[896,2432]{1,0:T(8,128)(2,1)} custom-call(s32[2]{0:T(128)} %pad_add_fusion.place, bf16[672,640]{1,0:T(8,128)(2,1)} %bitcast.10.refs_0_, bf16[672,640]{1,0:T(8,128)(2,1)} %collective-permute-done.16.refs_1_, bf16[672,640]{1,0:T(8,128)(2,1)} %collective-permute-done.21.refs_2_, bf16[672,640]{1,0:T(8,128)(2,1)} %collective-permute-done.22.refs_3_, ...), custom_call_target="tpu_custom_call" | custom-call | bytes 8716288 | tf_op jit(solution)/shard_map/assemble/pallas_call | solution.py:158
  169.5 7.3 %fusion.41 = f32[1024,2432]{1,0:T(8,128)S(1)} fusion(bf16[896,2432]{1,0:T(8,128)(2,1)S(1)} %copy-done.2, bf16[512,896]{1,0:T(8,128)(2,1)} %collective-permute-done.20, bf16[512,896]{1,0:T(8,128)(2,1)S(1)} %multiply_convert_fusion.3), kind=kOutput, calls=%fused_computation.150 | convolution fusion | flops 4466409472 | bytes 16154624 | tf_op jit(solution)/shard_map/dot_general | solution.py:479
  182.0 9.4 %multiply_convert_fusion.2 = (bf16[1024,2432]{1,0:T(8,128)(2,1)}, f32[1024,2432]{1,0:T(8,128)}) fusion(f32[1024,2432]{1,0:T(8,128)S(1)} %fusion.41, bf16[1024,896]{1,0:T(8,128)(2,1)S(1)} %get-tuple-element.69, bf16[896,2432]{1,0:T(8,128)(2,1)S(1)} %bitcast.84), kind=kOutput, calls=%fused_computation.2 | convolution fusion | flops 4477681664 | bytes 31096832 | tf_op jit(solution)/shard_map/dot_general | solution.py:479
  195.2 12.2 %down_grad.1 = (bf16[2,2432,128]{2,1,0:T(8,128)(2,1)}, bf16[2,2432,128]{2,1,0:T(8,128)(2,1)}, bf16[2,2432,128]{2,1,0:T(8,128)(2,1)}, bf16[2,2432,128]{2,1,0:T(8,128)(2,1)}) custom-call(s32[2]{0:T(128)} %pad_add_fusion.place, bf16[896,1024]{1,0:T(8,128)(2,1)} %get-tuple-element.143.left_ref, bf16[1024,2432]{1,0:T(8,128)(2,1)} %get-tuple-element.93.right_ref), custom_call_target="tpu_custom_call" | custom-call | flops 4462739456 | bytes 11173888 | tf_op jit(solution)/shard_map/down_grad/pallas_call | solution.py:198
  210.3 6.0 %assemble.13 = bf16[2432,896]{1,0:T(8,128)(2,1)} custom-call(s32[2]{0:T(128)} %pad_add_fusion.place, bf16[2432,128]{1,0:T(8,128)(2,1)} %copy-done.11, bf16[2432,128]{1,0:T(8,128)(2,1)} %collective-permute-done.27.refs_1_, bf16[2432,128]{1,0:T(8,128)(2,1)} %collective-permute-done.30.refs_2_, bf16[2432,128]{1,0:T(8,128)(2,1)} %collective-permute-done.31.refs_3_, ...), custom_call_target="tpu_custom_call" | custom-call | bytes 8716288 | tf_op jit(solution)/shard_map/assemble/pallas_call | solution.py:158
  216.2 16.2 %multiply_convert_fusion = (bf16[1024,2432]{1,0:T(8,128)(2,1)}, bf16[1024,2432]{1,0:T(8,128)(2,1)}) fusion(f32[1024,2432]{1,0:T(8,128)} %copy-done.72, f32[1024,2432]{1,0:T(8,128)} %get-tuple-element.178, bf16[1024,896]{0,1:T(8,128)(2,1)} %get-tuple-element.75, bf16[2432,896]{1,0:T(8,128)(2,1)} %assemble.13), kind=kOutput, calls=%fused_computation | convolution fusion | flops 4495114240 | bytes 36077568 | tf_op jit(solution)/shard_map/dot_general | solution.py:479
  236.2 10.4 %unit_grad.2 = bf16[4,896,640]{2,1,0:T(8,128)(2,1)} custom-call(bf16[896,1024]{1,0:T(8,128)(2,1)} %copy.67.left_ref, bf16[1024,2432]{1,0:T(8,128)(2,1)} %get-tuple-element.80.right_ref), custom_call_target="tpu_custom_call" | custom-call | flops 4462739456 | bytes 11173888 | tf_op jit(solution)/shard_map/unit_grad/pallas_call | solution.py:232
  254.0 10.4 %unit_grad.3 = bf16[4,896,640]{2,1,0:T(8,128)(2,1)} custom-call(bf16[896,1024]{1,0:T(8,128)(2,1)} %copy.67.left_ref, bf16[1024,2432]{1,0:T(8,128)(2,1)} %get-tuple-element.81.right_ref), custom_call_target="tpu_custom_call" | custom-call | flops 4462739456 | bytes 11173888 | tf_op jit(solution)/shard_map/unit_grad/pallas_call | solution.py:232
  264.5 11.3 %collective-permute-done.36 = bf16[1,2432,128]{2,1,0:T(8,128)(2,1)} collective-permute-done((bf16[1,2432,128]{2,1,0:T(8,128)(2,1)}, bf16[1,2432,128]{2,1,0:T(8,128)(2,1)}, u32[]{:S(2)}, u32[]{:S(2)}) %collective-permute-start.36) | collective-permute-done | bytes 622624 | tf_op jit(solution)/shard_map/ppermute | solution.py:41
  283.3 9.5 %fusion.53 = f32[1024,896]{1,0:T(8,128)S(1)} fusion(bf16[1024,2432]{1,0:T(8,128)(2,1)} %get-tuple-element.81.right_ref, bf16[896,2432]{1,0:T(8,128)(2,1)} %assemble.12), kind=kOutput, calls=%fused_computation.162 | convolution fusion | flops 4462739456 | bytes 13008896 | tf_op jit(solution)/shard_map/dot_general | solution.py:479
  292.8 5.5 %convolution_add_fusion.1 = f32[1024,896]{1,0:T(8,128)S(1)} fusion(f32[1024,896]{1,0:T(8,128)S(1)} %fusion.53, bf16[1024,2432]{1,0:T(8,128)(2,1)S(1)} %bitcast.118, bf16[896,2432]{1,0:T(8,128)(2,1)S(1)} %bitcast.86), kind=kOutput, calls=%fused_computation.38 | convolution fusion | flops 4463656960 | bytes 16678912 | tf_op jit(solution)/shard_map/dot_general | solution.py:479
  307.8 20.7 %attend_backward.1 = (f32[14,64,512]{2,1,0:T(8,128)}, f32[2,64,1280]{2,1,0:T(8,128)}, f32[2,64,1280]{2,1,0:T(8,128)}) custom-call(s32[2]{0:T(128)} %slice.302.runs_ref, bf16[14,64,512]{2,1,0:T(8,128)(2,1)} %multiply_convert_fusion.4.q_ref, bf16[14,64,512]{2,1,0:T(8,128)(2,1)} %bitcast.116, bf16[2,1280,64]{2,1,0:T(8,128)(2,1)} %get-tuple-element.148.k_ref, ...), custom_call_target="tpu_custom_call" | custom-call | flops 37580963840 | bytes 3670016 | tf_op jit(solution)/shard_map/attend_backward/pallas_call | solution.py:442
  341.2 21.9 %collective-permute-done.44 = bf16[256,256]{0,1:T(8,128)(2,1)} collective-permute-done((bf16[256,256]{0,1:T(8,128)(2,1)}, bf16[256,256]{0,1:T(8,128)(2,1)}, u32[]{:S(2)}, u32[]{:S(2)}) %collective-permute-start.44) | collective-permute-done | bytes 131104 | tf_op jit(solution)/shard_map/ppermute | solution.py:48
  380.5 9.3 %attn_grad.1 = (bf16[4,4,128,256]{3,2,1,0:T(8,128)(2,1)}, bf16[4,4,128,256]{3,2,1,0:T(8,128)(2,1)}, bf16[4,4,128,256]{3,2,1,0:T(8,128)(2,1)}, bf16[4,4,128,256]{3,2,1,0:T(8,128)(2,1)}) custom-call(s32[2]{0:T(128)} %pad_add_fusion.place, bf16[896,512]{1,0:T(8,128)(2,1)} %copy.75.a_ref, bf16[512,1152]{1,0:T(8,128)(2,1)} %get-tuple-element.150.b_ref, ...), custom_call_target="tpu_custom_call" | custom-call | flops 1879048192 | bytes 7864320 | tf_op jit(solution)/shard_map/attn_grad/pallas_call | solution.py:316
  399.7 11.0 %collective-permute-done.48 = bf16[2,4,128,256]{3,2,1,0:T(8,128)(2,1)} collective-permute-done((bf16[2,4,128,256]{3,2,1,0:T(8,128)(2,1)}, bf16[2,4,128,256]{3,2,1,0:T(8,128)(2,1)}, u32[]{:S(2)}, u32[]{:S(2)}) %collective-permute-start.48) | collective-permute-done | bytes 524320 | tf_op jit(solution)/shard_map/ppermute | solution.py:41
  423.6 8.7 %fusion.54 = f32[1024,896]{1,0:T(8,128)S(1)} fusion(bf16[1024,2432]{1,0:T(8,128)(2,1)} %get-tuple-element.93.right_ref, bf16[2432,896]{1,0:T(8,128)(2,1)} %assemble.13), kind=kOutput, calls=%fused_computation.163 | convolution fusion | flops 4462739456 | bytes 13008896 | tf_op jit(solution)/shard_map/dot_general | solution.py:479
  443.9 6.6 %collective-permute-done.82.refs_7_ = bf16[1216,128]{1,0:T(8,128)(2,1)S(1)} collective-permute-done((bf16[1216,128]{1,0:T(8,128)(2,1)}, bf16[1216,128]{1,0:T(8,128)(2,1)S(1)}, u32[]{:S(2)}, u32[]{:S(2)}) %collective-permute-start.82) | collective-permute-done | bytes 311328 | tf_op jit(solution)/shard_map/ppermute | solution.py:41
  (464 shorter events, 247.4 us)
Async XLA Ops:
  7.3 68.2 %all-gather.2.cloned.1.call-start = ((), (), s32[]{:S(2)}) async-start(), calls=%async_computation.4 | async-start | bytes 2867200 | tf_op jit(solution)/shard_map/all_gather | solution.py:51
  9.7 321.8 %reduce-scatter.13.cloned.1.call-start = ((), (), s32[]{:S(2)}) async-start(), calls=%async_computation.7 | async-start | bytes 5734400
  52.6 29.9 %collective-permute-start.29 = (bf16[512,896]{0,1:T(8,128)(2,1)S(1)}, bf16[512,896]{0,1:T(8,128)(2,1)}, u32[]{:S(2)}, u32[]{:S(2)}) collective-permute-start(bf16[512,896]{0,1:T(8,128)(2,1)S(1)} %copy.66), channel_id=1, source_target_pairs={{0,4},{4,0},{8,12},{12,8},{16,20},{20,16},{24,28},{28,24},{1,5},{5... | collective-permute-start | bytes 2752520 | tf_op jit(solution)/shard_map/ppermute | solution.py:41
  87.0 70.8 %collective-permute-start.21 = (bf16[672,640]{1,0:T(8,128)(2,1)}, bf16[672,640]{1,0:T(8,128)(2,1)}, u32[]{:S(2)}, u32[]{:S(2)}) collective-permute-start(bf16[672,640]{1,0:T(8,128)(2,1)} %bitcast.10.refs_0_), channel_id=1, source_target_pairs={{0,16},{4,20},{8,24},{12,28},{16,0},{20,4},{24,8},{28,12},{1,17},{... | collective-permute-start | bytes 2580488 | tf_op jit(solution)/shard_map/ppermute | solution.py:41
  88.5 62.3 %collective-permute-start.25 = (bf16[672,640]{1,0:T(8,128)(2,1)}, bf16[672,640]{1,0:T(8,128)(2,1)}, u32[]{:S(2)}, u32[]{:S(2)}) collective-permute-start(bf16[672,640]{1,0:T(8,128)(2,1)} %bitcast.11.refs_0_), channel_id=1, source_target_pairs={{0,8},{4,12},{8,0},{12,4},{16,24},{20,28},{24,16},{28,20},{1,9},{5... | collective-permute-start | bytes 2580488 | tf_op jit(solution)/shard_map/ppermute | solution.py:41
  104.9 27.0 %collective-permute-start.19 = (bf16[1216,128]{1,0:T(8,128)(2,1)S(1)}, bf16[1216,128]{1,0:T(8,128)(2,1)S(1)}, u32[]{:S(2)}, u32[]{:S(2)}) collective-permute-start(bf16[1216,128]{1,0:T(8,128)(2,1)S(1)} %get-tuple-element.67), channel_id=1, source_target_pairs={{0,2},{1,3},{2,0},{3,1},{4,6},{5,7},{6,4},{7,5},{8,10},{9,11},{10,... | collective-permute-start | bytes 933896 | tf_op jit(solution)/shard_map/ppermute | solution.py:44
  121.2 38.1 %collective-permute-start.22 = (bf16[672,640]{1,0:T(8,128)(2,1)}, bf16[672,640]{1,0:T(8,128)(2,1)}, u32[]{:S(2)}, u32[]{:S(2)}) collective-permute-start(bf16[672,640]{1,0:T(8,128)(2,1)} %collective-permute-done.16.refs_1_), channel_id=1, source_target_pairs={{0,16},{4,20},{8,24},{12,28},{16,0},{20,4},{24,8},{28,12},{1,17},{... | collective-permute-start | bytes 2580488 | tf_op jit(solution)/shard_map/ppermute | solution.py:41
  125.3 26.1 %collective-permute-start.26 = (bf16[672,640]{1,0:T(8,128)(2,1)}, bf16[672,640]{1,0:T(8,128)(2,1)}, u32[]{:S(2)}, u32[]{:S(2)}) collective-permute-start(bf16[672,640]{1,0:T(8,128)(2,1)} %collective-permute-done.17.refs_2_), channel_id=1, source_target_pairs={{0,8},{4,12},{8,0},{12,4},{16,24},{20,28},{24,16},{28,20},{1,9},{5... | collective-permute-start | bytes 2580488 | tf_op jit(solution)/shard_map/ppermute | solution.py:41
  150.8 57.2 %collective-permute-start.32 = (bf16[2432,128]{1,0:T(8,128)(2,1)}, bf16[2432,128]{1,0:T(8,128)(2,1)}, u32[]{:S(2)}, u32[]{:S(2)}) collective-permute-start(bf16[2432,128]{1,0:T(8,128)(2,1)} %pad_maximum_fusion.7.refs_4_), channel_id=1, source_target_pairs={{0,8},{4,12},{8,0},{12,4},{16,24},{20,28},{24,16},{28,20},{1,9},{5... | collective-permute-start | bytes 1867784 | tf_op jit(solution)/shard_map/ppermute | solution.py:41
  157.9 51.5 %collective-permute-start.30 = (bf16[2432,128]{1,0:T(8,128)(2,1)S(1)}, bf16[2432,128]{1,0:T(8,128)(2,1)}, u32[]{:S(2)}, u32[]{:S(2)}) collective-permute-start(bf16[2432,128]{1,0:T(8,128)(2,1)S(1)} %pad_maximum_fusion.6.refs_0_), channel_id=1, source_target_pairs={{0,16},{4,20},{8,24},{12,28},{16,0},{20,4},{24,8},{28,12},{1,17},{... | collective-permute-start | bytes 1867784 | tf_op jit(solution)/shard_map/ppermute | solution.py:41
  176.8 32.6 %collective-permute-start.33 = (bf16[2432,128]{1,0:T(8,128)(2,1)}, bf16[2432,128]{1,0:T(8,128)(2,1)S(1)}, u32[]{:S(2)}, u32[]{:S(2)}) collective-permute-start(bf16[2432,128]{1,0:T(8,128)(2,1)} %collective-permute-done.28.refs_6_), channel_id=1, source_target_pairs={{0,8},{4,12},{8,0},{12,4},{16,24},{20,28},{24,16},{28,20},{1,9},{5... | collective-permute-start | bytes 1867784 | tf_op jit(solution)/shard_map/ppermute | solution.py:41
  181.4 28.1 %collective-permute-start.31 = (bf16[2432,128]{1,0:T(8,128)(2,1)}, bf16[2432,128]{1,0:T(8,128)(2,1)}, u32[]{:S(2)}, u32[]{:S(2)}) collective-permute-start(bf16[2432,128]{1,0:T(8,128)(2,1)} %collective-permute-done.27.refs_1_), channel_id=1, source_target_pairs={{0,16},{4,20},{8,24},{12,28},{16,0},{20,4},{24,8},{28,12},{1,17},{... | collective-permute-start | bytes 1867784 | tf_op jit(solution)/shard_map/ppermute | solution.py:41
  207.4 28.5 %collective-permute-start.34 = (bf16[2,2432,128]{2,1,0:T(8,128)(2,1)}, bf16[2,2432,128]{2,1,0:T(8,128)(2,1)}, u32[]{:S(2)}, u32[]{:S(2)}) collective-permute-start(bf16[2,2432,128]{2,1,0:T(8,128)(2,1)} %get-tuple-element.72), channel_id=1, source_target_pairs={{0,8},{4,12},{8,0},{12,4},{16,24},{20,28},{24,16},{28,20},{1,9},{5... | collective-permute-start | bytes 3735560 | tf_op jit(solution)/shard_map/ppermute | solution.py:41
  208.0 28.2 %collective-permute-start.35 = (bf16[2,2432,128]{2,1,0:T(8,128)(2,1)}, bf16[2,2432,128]{2,1,0:T(8,128)(2,1)}, u32[]{:S(2)}, u32[]{:S(2)}) collective-permute-start(bf16[2,2432,128]{2,1,0:T(8,128)(2,1)} %get-tuple-element.74), channel_id=1, source_target_pairs={{0,16},{4,20},{8,24},{12,28},{16,0},{20,4},{24,8},{28,12},{1,17},{... | collective-permute-start | bytes 3735560 | tf_op jit(solution)/shard_map/ppermute | solution.py:41
  246.7 153.0 %reduce-scatter.15.cloned.1.call-start = ((), (), s32[]{:S(2)}) async-start(), calls=%async_computation.8 | async-start | bytes 5734400
  249.0 26.7 %collective-permute-start.36 = (bf16[1,2432,128]{2,1,0:T(8,128)(2,1)}, bf16[1,2432,128]{2,1,0:T(8,128)(2,1)}, u32[]{:S(2)}, u32[]{:S(2)}) collective-permute-start(bf16[1,2432,128]{2,1,0:T(8,128)(2,1)} %add_convert_fusion.5), channel_id=1, source_target_pairs={{0,16},{4,20},{8,24},{12,28},{16,0},{20,4},{24,8},{28,12},{1,17},{... | collective-permute-start | bytes 1867784 | tf_op jit(solution)/shard_map/ppermute | solution.py:41
  252.7 28.9 %collective-permute-start.37 = (bf16[1,2432,128]{2,1,0:T(8,128)(2,1)}, bf16[1,2432,128]{2,1,0:T(8,128)(2,1)}, u32[]{:S(2)}, u32[]{:S(2)}) collective-permute-start(bf16[1,2432,128]{2,1,0:T(8,128)(2,1)} %add_convert_fusion.4), channel_id=1, source_target_pairs={{0,8},{4,12},{8,0},{12,4},{16,24},{20,28},{24,16},{28,20},{1,9},{5... | collective-permute-start | bytes 1867784 | tf_op jit(solution)/shard_map/ppermute | solution.py:41
  264.4 177.3 %reduce-scatter.9.cloned.1.call-start = ((), (), s32[]{:S(2)}) async-start(), calls=%async_computation.5 | async-start | bytes 1433600 | tf_op jit(solution)/shard_map/reduce_scatter | solution.py:780
  298.7 32.8 %collective-permute-start.41 = (bf16[1216,128]{1,0:T(8,128)(2,1)S(1)}, bf16[1216,128]{1,0:T(8,128)(2,1)}, u32[]{:S(2)}, u32[]{:S(2)}) collective-permute-start(bf16[1216,128]{1,0:T(8,128)(2,1)S(1)} %fusion.19), channel_id=1, source_target_pairs={{0,2},{1,3},{2,0},{3,1},{4,6},{5,7},{6,4},{7,5},{8,10},{9,11},{10,... | collective-permute-start | bytes 933896 | tf_op jit(solution)/shard_map/ppermute | solution.py:44
  298.9 32.6 %collective-permute-start.42 = (bf16[1216,128]{1,0:T(8,128)(2,1)S(1)}, bf16[1216,128]{1,0:T(8,128)(2,1)}, u32[]{:S(2)}, u32[]{:S(2)}) collective-permute-start(bf16[1216,128]{1,0:T(8,128)(2,1)S(1)} %fusion.18), channel_id=1, source_target_pairs={{0,2},{1,3},{2,0},{3,1},{4,6},{5,7},{6,4},{7,5},{8,10},{9,11},{10,... | collective-permute-start | bytes 933896 | tf_op jit(solution)/shard_map/ppermute | solution.py:44
  334.6 28.5 %collective-permute-start.43 = (bf16[256,512]{0,1:T(8,128)(2,1)}, bf16[256,512]{0,1:T(8,128)(2,1)}, u32[]{:S(2)}, u32[]{:S(2)}) collective-permute-start(bf16[256,512]{0,1:T(8,128)(2,1)} %slice.426), channel_id=1, source_target_pairs={{1,0},{2,1},{3,2},{5,4},{6,5},{7,6},{9,8},{10,9},{11,10},{13,12},{... | collective-permute-start | bytes 786440 | tf_op jit(solution)/shard_map/ppermute | solution.py:48
  336.3 26.8 %collective-permute-start.44 = (bf16[256,256]{0,1:T(8,128)(2,1)}, bf16[256,256]{0,1:T(8,128)(2,1)}, u32[]{:S(2)}, u32[]{:S(2)}) collective-permute-start(bf16[256,256]{0,1:T(8,128)(2,1)} %slice.427), channel_id=1, source_target_pairs={{2,0},{3,1},{6,4},{7,5},{10,8},{11,9},{14,12},{15,13},{18,16},{19,... | collective-permute-start | bytes 393224 | tf_op jit(solution)/shard_map/ppermute | solution.py:48
  341.1 101.3 %reduce-scatter.11.cloned.1.call-start = ((), (), s32[]{:S(2)}) async-start(), calls=%async_computation.6 | async-start | bytes 1433600 | tf_op jit(solution)/shard_map/reduce_scatter | solution.py:780
  433.9 59.9 %collective-permute-start.47 = (f32[512,896]{1,0:T(8,128)}, f32[512,896]{1,0:T(8,128)}, u32[]{:S(2)}, u32[]{:S(2)}) collective-permute-start(f32[512,896]{1,0:T(8,128)} %slice.436), channel_id=1, source_target_pairs={{0,4},{4,0},{8,12},{12,8},{16,20},{20,16},{24,28},{28,24},{1,5},{5... | collective-permute-start | bytes 5505032 | tf_op jit(solution)/shard_map/ppermute | solution.py:41
  (144 other events, 1531.9 us)
Sparse Core Ops, SparseCore 0:
  10.2 53.8 all-gather.1
  246.8 63.9 reduce-scatter.12
  313.9 55.8 reduce-scatter.14
  371.9 28.8 reduce-scatter.8
  403.0 32.3 reduce-scatter.10
